TPU v7x, 32 devices: a whole 2x2x4 slice. The times are simulated.
32 devices in a mesh: wide: 8 (over z, y), narrow: 4 (over x, core).
Axes of the slice: x: 2, y: 2, z: 4, core: 2. Of those that a mesh axis runs over, the one named last changes fastest.
Arguments:
- passage_ids: int32 [64, 384], P(('wide', 'narrow')), may hold values from 0 to 17999
- query_ids: int32 [8, 32], P('wide'), may hold values from 0 to 17999
- passage_query: int32 [64], replicated, may hold values from -1 to 7, as said below
- kept_mask: int32 [64], replicated, may hold values 0 or 1
- neg_count: int32 [8], P('wide'), may hold values from 1 to 7, as said below
- step_count: int32 [1], replicated, may hold values from 2 to 20
- embed_table: float32 [18384, 768], P(None, ('wide', 'narrow')), may hold values from -6 to 6
- attend_in: float32 [2, 768, 2304], P(None, ('wide', 'narrow')), may hold values from -0.3125 to 0.3125
- attend_out: float32 [2, 768, 768], P(None, ('wide', 'narrow')), may hold values from -0.625 to 0.625
- expand_weight: float32 [2, 768, 3072], P(None, ('wide', 'narrow')), may hold values from -0.21875 to 0.21875
- shrink_weight: float32 [2, 3072, 768], P(None, ('wide', 'narrow')), may hold values from -0.109375 to 0.109375
- norm_gains: float32 [2, 3, 768], P(None, None, ('wide', 'narrow')), may hold values from 0.5 to 1.5
- bias_terms: float32 [2, 8448], P(None, ('wide', 'narrow')), may hold values from -0.6 to 0.6
- embed_first: float32 [18384, 768], P(None, ('wide', 'narrow')), may hold values from -3.7598107e-05 to 3.7598107e-05
- embed_second: float32 [18384, 768], P(None, ('wide', 'narrow')), may hold values from 1.59032e-12 to 2.544512e-11
- attend_in_first: float32 [2, 768, 2304], P(None, ('wide', 'narrow')), may hold values from -0.0001252017 to 0.0001252017
- attend_in_second: float32 [2, 768, 2304], P(None, ('wide', 'narrow')), may hold values from 1.7670223e-11 to 2.8272357e-10
- attend_out_first: float32 [2, 768, 768], P(None, ('wide', 'narrow')), may hold values from -0.0001252017 to 0.0001252017
- attend_out_second: float32 [2, 768, 768], P(None, ('wide', 'narrow')), may hold values from 1.7670223e-11 to 2.8272357e-10
- expand_first: float32 [2, 768, 3072], P(None, ('wide', 'narrow')), may hold values from -0.0001252017 to 0.0001252017
- expand_second: float32 [2, 768, 3072], P(None, ('wide', 'narrow')), may hold values from 1.7670223e-11 to 2.8272357e-10
- shrink_first: float32 [2, 3072, 768], P(None, ('wide', 'narrow')), may hold values from -0.0001252017 to 0.0001252017
- shrink_second: float32 [2, 3072, 768], P(None, ('wide', 'narrow')), may hold values from 1.7670223e-11 to 2.8272357e-10
- gains_first: float32 [2, 3, 768], P(None, None, ('wide', 'narrow')), may hold values from -0.0003759811 to 0.0003759811
- gains_second: float32 [2, 3, 768], P(None, None, ('wide', 'narrow')), may hold values from 1.59032e-10 to 2.544512e-09
- bias_first: float32 [2, 8448], P(None, ('wide', 'narrow')), may hold values from -0.0003759811 to 0.0003759811
- bias_second: float32 [2, 8448], P(None, ('wide', 'narrow')), may hold values from 1.59032e-10 to 2.544512e-09
Outputs:
- loss: float32 [], replicated
- grad_norm: float32 [], replicated
- embed_table_new: float32 [18384, 768], P(None, ('wide', 'narrow'))
- embed_first_new: float32 [18384, 768], P(None, ('wide', 'narrow'))
- embed_second_new: float32 [18384, 768], P(None, ('wide', 'narrow'))
- attend_in_new: float32 [2, 768, 2304], P(None, ('wide', 'narrow'))
- attend_in_first_new: float32 [2, 768, 2304], P(None, ('wide', 'narrow'))
- attend_in_second_new: float32 [2, 768, 2304], P(None, ('wide', 'narrow'))
- attend_out_new: float32 [2, 768, 768], P(None, ('wide', 'narrow'))
- attend_out_first_new: float32 [2, 768, 768], P(None, ('wide', 'narrow'))
- attend_out_second_new: float32 [2, 768, 768], P(None, ('wide', 'narrow'))
- expand_new: float32 [2, 768, 3072], P(None, ('wide', 'narrow'))
- expand_first_new: float32 [2, 768, 3072], P(None, ('wide', 'narrow'))
- expand_second_new: float32 [2, 768, 3072], P(None, ('wide', 'narrow'))
- shrink_new: float32 [2, 3072, 768], P(None, ('wide', 'narrow'))
- shrink_first_new: float32 [2, 3072, 768], P(None, ('wide', 'narrow'))
- shrink_second_new: float32 [2, 3072, 768], P(None, ('wide', 'narrow'))
- norm_gains_new: float32 [2, 3, 768], P(None, None, ('wide', 'narrow'))
- gains_first_new: float32 [2, 3, 768], P(None, None, ('wide', 'narrow'))
- gains_second_new: float32 [2, 3, 768], P(None, None, ('wide', 'narrow'))
- bias_terms_new: float32 [2, 8448], P(None, ('wide', 'narrow'))
- bias_first_new: float32 [2, 8448], P(None, ('wide', 'narrow'))
- bias_second_new: float32 [2, 8448], P(None, ('wide', 'narrow'))
Inputs may be any that keep to these rules, and one draw needn't show every extreme that they name: `passage_query`: slots from 0 hold the passages of query 0, then of query 1 and so on, each query 2 to 8 consecutive slots (the first is its positive), one query exactly 8, 40 slots in all; the remaining slots hold -1. `neg_count`: one less than the number of slots of that query in passage_query.
All inputs are finite; a program needn't handle non-finite values.
Results may differ from a plain program's by a relative error of at most 0.022.
The roundings to bfloat16 on the way count: a program that leaves them out, or rounds other values in their place, can miss the bound.
Values may be sent and summed in bfloat16 or wider, within the bound.
A program may use at most 448 MiB of HBM per device.

v0:
```python
import functools

import jax
import jax.numpy as jnp
from jax import lax
from jax.experimental import pallas as pl
from jax.experimental.pallas import tpu as pltpu
from jax.sharding import PartitionSpec as P

D = 768
H = 12
HD = 64
FF = 3072
V = 18000
LP = 384
LQ = 32
LANE = 128
VALID_PER_QUERY = 5

MARGIN = 1.0
CLIP = 1.0
BETA_ONE = 0.9
BETA_TWO = 0.999
LEARN_RATES = (1.0, 0.02, 0.08, 0.02, 0.02, 1.0, 0.1)
WEIGHT_DECAY = 0.01
ADAM_EPS = 1e-08
NORM_EPS = 1e-05
AXES = ("wide", "narrow")
F32 = jnp.float32
BF16 = jnp.bfloat16
O_Q, O_V, O_O, O_1, O_IN, O_OUT, O_2, O_EMB = (
    0, D, 2 * D, 3 * D, 4 * D, 4 * D + FF, 5 * D + FF, 6 * D + FF
)


def dot(left, right, dims):
    return lax.dot_general(left, right, (dims, ((), ())), preferred_element_type=F32)


def norm_rows(values, gain, shift):
    center = values - jnp.mean(values, axis=-1, keepdims=True)
    spread = jnp.mean(center * center, axis=-1, keepdims=True)
    scale = lax.rsqrt(spread + NORM_EPS)
    hat = center * scale
    return hat * gain + shift, hat, scale


def norm_rows_back(grad, gain, hat, scale):
    scaled = grad * gain
    mean_one = jnp.mean(scaled, axis=-1, keepdims=True)
    mean_two = jnp.mean(scaled * hat, axis=-1, keepdims=True)
    return scale * (scaled - mean_one - hat * mean_two)


def gelu_both(upper):
    cdf = 0.5 * (1.0 + lax.erf(upper * 0.7071067811865476))
    pdf = jnp.exp(-0.5 * upper * upper) * 0.3989422804014327
    return upper * cdf, cdf + upper * pdf


def adam_update(weight, grad, first, second, step, rate):
    first_new = BETA_ONE * first + (1.0 - BETA_ONE) * grad
    second_new = BETA_TWO * second + (1.0 - BETA_TWO) * grad * grad
    first_hat = first_new / (1.0 - BETA_ONE**step)
    second_hat = second_new / (1.0 - BETA_TWO**step)
    weight_new = weight - rate * (
        first_hat / (jnp.sqrt(second_hat) + ADAM_EPS) + WEIGHT_DECAY * weight
    )
    return (weight_new, first_new, second_new)


MESH = pl.DeviceIdType.MESH
HASH = 512


class Send:
    def __init__(self, src, dst, take, put, many_src, many_dst, sources, targets):
        self.src, self.dst, self.take, self.put = src, dst, take, put
        self.many_src, self.many_dst = many_src, many_dst
        self.sources, self.targets = sources, targets


def inside(index, span):
    return jnp.logical_and(index >= span[0], index < span[1])


def comm_body(sends, n_in, n_out, nd, narrow, *refs):
    ins, outs = refs[:n_in], refs[n_in : n_in + n_out]
    send_sem, recv_sem, own_sem = refs[n_in + n_out :]
    me = lax.axis_index("wide") * narrow + lax.axis_index("narrow")
    barrier = pltpu.get_barrier_semaphore()

    def greet(k, carry):
        t = lax.rem(me + k, nd)
        pl.semaphore_signal(
            barrier, inc=1, device_id=(t // narrow, lax.rem(t, narrow)), device_id_type=MESH
        )
        return carry

    lax.fori_loop(1, nd, greet, 0)
    pl.semaphore_wait(barrier, nd - 1)

    def push(k, carry):
        t = lax.rem(me + k, nd)
        for i, s in enumerate(sends):

            @pl.when(jnp.logical_and(inside(me, s.sources), inside(t, s.targets)))
            def _():
                pltpu.make_async_remote_copy(
                    src_ref=s.take(ins[s.src], me, t),
                    dst_ref=s.put(outs[s.dst], me, t),
                    send_sem=send_sem.at[i],
                    recv_sem=recv_sem.at[i],
                    device_id=(t // narrow, lax.rem(t, narrow)),
                    device_id_type=MESH,
                ).start()

        return carry

    lax.fori_loop(1, nd, push, 0)
    for i, s in enumerate(sends):
        both = jnp.logical_and(inside(me, s.sources), inside(me, s.targets))

        @pl.when(both)
        def _():
            own = pltpu.make_async_copy(
                s.take(ins[s.src], me, me), s.put(outs[s.dst], me, me), own_sem.at[i]
            )
            own.start()
            own.wait()

    for i, s in enumerate(sends):
        n_t = s.targets[1] - s.targets[0]
        n_s = s.sources[1] - s.sources[0]
        is_s, is_t = inside(me, s.sources), inside(me, s.targets)
        for own in (0, 1):
            mine = is_t if own else jnp.logical_not(is_t)
            if n_t - own > 0:

                @pl.when(jnp.logical_and(is_s, mine))
                def _():
                    view = s.many_src(ins[s.src], n_t - own) if s.many_src(ins[s.src], 1) is not None else outs[s.dst].at[pl.ds(0, n_t - own)]
                    pltpu.make_async_copy(view, view, send_sem.at[i]).wait()

            mine = is_s if own else jnp.logical_not(is_s)
            if n_s - own > 0:

                @pl.when(jnp.logical_and(is_t, mine))
                def _():
                    view = s.many_dst(outs[s.dst], n_s - own)
                    pltpu.make_async_copy(view, view, recv_sem.at[i]).wait()


def comm(collective, arrays, out_shapes, sends, nd, narrow):
    vmem = pl.BlockSpec(memory_space=pltpu.VMEM)
    n = len(sends)
    return pl.pallas_call(
        functools.partial(comm_body, sends, len(arrays), len(out_shapes), nd, narrow),
        out_shape=[jax.ShapeDtypeStruct(s, d) for s, d in out_shapes],
        in_specs=[vmem] * len(arrays),
        out_specs=[vmem] * len(out_shapes),
        scratch_shapes=[
            pltpu.SemaphoreType.DMA((n,)),
            pltpu.SemaphoreType.DMA((n,)),
            pltpu.SemaphoreType.DMA((n,)),
        ],
        compiler_params=pltpu.CompilerParams(collective_id=collective, has_side_effects=True),
    )(*arrays)


def send_all(src, dst, nd):
    return Send(
        src, dst,
        lambda ref, s, t: ref,
        lambda ref, s, t: ref.at[s],
        lambda ref, n: None, lambda ref, n: ref.at[pl.ds(0, n)],
        (0, nd), (0, nd),
    )


def send_blocks(src, dst, nd):
    return Send(
        src, dst,
        lambda ref, s, t: ref.at[t],
        lambda ref, s, t: ref.at[s],
        lambda ref, n: ref.at[pl.ds(0, n)], lambda ref, n: ref.at[pl.ds(0, n)],
        (0, nd), (0, nd),
    )


def stack_pairs(pieces, store):
    rows = pieces[0].shape[0]
    for i in range(0, len(pieces), 2):
        store(i * rows, jnp.concatenate(pieces[i : i + 2], axis=0))


def gather_body(rows, blocks, table_ref, ids_ref, out_ref, stacked):
    @pl.when(pl.program_id(0) == 0)
    def _():
        pieces = [
            table_ref[:, b * HASH : (b + 1) * HASH].astype(F32) for b in range(blocks)
        ]

        def store(row, value):
            stacked[row : row + value.shape[0], :] = value.astype(BF16)

        stack_pairs(pieces, store)

    ids = ids_ref[0]
    low = ids & (HASH - 1)
    high = ids >> (HASH.bit_length() - 1)
    width = ids.shape[1]
    hot = (lax.broadcasted_iota(jnp.int32, (HASH, width), 0) == low).astype(F32).astype(BF16)
    picked = jnp.dot(stacked[...], hot, preferred_element_type=F32)
    value = jnp.zeros((rows, width), F32)
    for b in range(blocks):
        value = jnp.where(high == b, picked[b * rows : (b + 1) * rows], value)
    out_ref[...] = value.astype(BF16)


def table_rows(table, ids):
    rows, total = table.shape
    tokens = ids.shape[0]
    tile = 512
    blocks = total // HASH
    return pl.pallas_call(
        functools.partial(gather_body, rows, blocks),
        grid=(tokens // tile,),
        out_shape=jax.ShapeDtypeStruct((rows, tokens), BF16),
        in_specs=[
            pl.BlockSpec((rows, total), lambda i: (0, 0)),
            pl.BlockSpec((1, 1, tile), lambda i: (i, 0, 0)),
        ],
        out_specs=pl.BlockSpec((rows, tile), lambda i: (0, i)),
        scratch_shapes=[pltpu.VMEM((blocks * rows, HASH), BF16)],
        name="table_rows",
    )(table, ids.reshape(tokens // tile, 1, tile))


def scatter_body(rows, blocks, values_ref, ids_ref, out_ref, spread, acc):
    step = pl.program_id(0)
    ids = ids_ref[0]
    low = ids & (HASH - 1)
    high = ids >> (HASH.bit_length() - 1)
    width = ids.shape[1]
    values = values_ref[...].astype(F32)
    pieces = [jnp.where(high == b, values, 0.0) for b in range(blocks)]

    def store(row, value):
        spread[row : row + value.shape[0], :] = value.astype(BF16)

    stack_pairs(pieces, store)
    hot = (lax.broadcasted_iota(jnp.int32, (HASH, width), 0) == low).astype(F32).astype(BF16)
    part = lax.dot_general(
        spread[...], hot, (((1,), (1,)), ((), ())), preferred_element_type=F32
    )

    @pl.when(step == 0)
    def _():
        acc[...] = part

    @pl.when(step > 0)
    def _():
        acc[...] += part

    @pl.when(step == pl.num_programs(0) - 1)
    def _():
        for b in range(blocks):
            out_ref[:, b * HASH : (b + 1) * HASH] = acc[b * rows : (b + 1) * rows, :]


def table_sums(values, ids, total):
    rows, tokens = values.shape
    tile = 1024
    blocks = total // HASH
    return pl.pallas_call(
        functools.partial(scatter_body, rows, blocks),
        grid=(tokens // tile,),
        out_shape=jax.ShapeDtypeStruct((rows, total), F32),
        in_specs=[
            pl.BlockSpec((rows, tile), lambda i: (0, i)),
            pl.BlockSpec((1, 1, tile), lambda i: (i, 0, 0)),
        ],
        out_specs=pl.BlockSpec((rows, total), lambda i: (0, 0)),
        scratch_shapes=[
            pltpu.VMEM((blocks * rows, tile), BF16),
            pltpu.VMEM((blocks * rows, HASH), F32),
        ],
        name="table_sums",
    )(values, ids.reshape(tokens // tile, 1, tile))


def head_mask(dtype):
    rows = lax.broadcasted_iota(jnp.int32, (H, D), 0)
    cols = lax.broadcasted_iota(jnp.int32, (H, D), 1)
    return (cols // HD == rows).astype(dtype)


def spread_heads(row):
    return row[None, :] * head_mask(row.dtype)


def encode_front(emb_t, w_in, w_out, gain, bias, length):
    width = emb_t.shape[1]
    center = emb_t - jnp.mean(emb_t, axis=0, keepdims=True)
    spread = jnp.mean(center * center, axis=0, keepdims=True)
    scale = lax.rsqrt(spread + NORM_EPS)
    hat = center * scale
    x0 = hat * gain[0][:, None] + bias[O_EMB : O_EMB + D][:, None]
    x_low = x0.astype(BF16)
    first_low = x_low[:, 0]
    q = (dot(first_low[None], w_in[:, :D], ((1,), (0,)))[0] + bias[O_Q : O_Q + D]).astype(BF16)
    k = dot(w_in[:, D : 2 * D], x_low, ((0,), (0,))).astype(BF16)
    v = (
        dot(w_in[:, 2 * D :], x_low, ((0,), (0,))) + bias[O_V : O_V + D][:, None]
    ).astype(BF16)
    q_heads = spread_heads(q)
    s = dot(q_heads, k, ((1,), (0,))) * 0.125
    if length < width:
        live = lax.broadcasted_iota(jnp.int32, (1, width), 1) < length
        s = jnp.where(live, s, -1e30)
    peak = jnp.max(s, axis=1, keepdims=True)
    e = jnp.exp(s - peak)
    p = e / jnp.sum(e, axis=1, keepdims=True)
    p_low = p.astype(BF16)
    mixed = dot(p_low, v, ((1,), (1,)))
    a = jnp.sum(mixed * head_mask(F32), axis=0).astype(BF16)
    o = dot(a[None], w_out, ((1,), (0,)))[0] + bias[O_O : O_O + D]
    return x0[:, 0] + o, (hat, scale, x_low, q, k, v, p, p_low, a)


def encode_back(kept, row_grad, w_in, w_out, gain):
    hat, scale, x_low, q, k, v, p, p_low, a = kept
    do = row_grad.astype(BF16)
    da = dot(do[None], w_out, ((1,), (1,)))[0].astype(BF16)
    da_heads = spread_heads(da)
    q_heads = spread_heads(q)
    dp = dot(da_heads, v, ((1,), (0,)))
    ds = (p * (dp - jnp.sum(dp * p, axis=1, keepdims=True))).astype(BF16)
    dq_heads = dot(ds, k, ((1,), (1,)))
    dq = (jnp.sum(dq_heads * head_mask(F32), axis=0) * 0.125).astype(BF16)
    t = dot(ds, x_low, ((1,), (1,))) * 0.125
    w = dot(p_low, x_low, ((1,), (1,)))
    gk = (dot(q_heads, w_in[:, D : 2 * D], ((1,), (1,))) * 0.125).astype(BF16)
    ev = dot(da_heads, w_in[:, 2 * D :], ((1,), (1,))).astype(BF16)
    gx = dot(gk, ds, ((0,), (0,))) + dot(ev, p_low, ((0,), (0,)))
    first = row_grad + dot(dq[None], w_in[:, :D], ((1,), (1,)))[0]
    is_first = lax.broadcasted_iota(jnp.int32, (1, gx.shape[1]), 1) == 0
    gx = gx + jnp.where(is_first, first[:, None], 0.0)
    p_sum = jnp.sum(p_low.astype(F32), axis=1)
    dbv = jnp.repeat(p_sum, HD) * da.astype(F32)
    g_gain = jnp.sum(gx * hat, axis=1)
    g_shift = jnp.sum(gx, axis=1)
    scaled = gx * gain[0][:, None]
    mean_one = jnp.mean(scaled, axis=0, keepdims=True)
    mean_two = jnp.mean(scaled * hat, axis=0, keepdims=True)
    g_emb = scale * (scaled - mean_one - hat * mean_two)
    return g_emb, (t.astype(BF16), w.astype(BF16), q, da, dq, dbv, g_gain, g_shift)


NN = (((1,), (0,)), ((), ()))
NT = (((1,), (1,)), ((), ()))
TN = (((0,), (0,)), ((), ()))
HIGH = lax.Precision.HIGHEST


def mm(left, right, dims, precision=None):
    return lax.dot_general(
        left, right, dims, preferred_element_type=F32, precision=precision
    )


def iota(shape, dim):
    return lax.broadcasted_iota(jnp.int32, shape, dim)


def as_bf16(mask):
    return mask.astype(F32).astype(BF16)


class Flow:
    def __init__(self, take, put, many, sources, targets):
        self.take, self.put, self.many = take, put, many
        self.sources, self.targets = sources, targets


class Net:
    def __init__(self, nd, narrow, send_sem, recv_sem, own_sem):
        self.nd, self.narrow = nd, narrow
        self.send_sem, self.recv_sem, self.own_sem = send_sem, recv_sem, own_sem
        self.me = lax.axis_index("wide") * narrow + lax.axis_index("narrow")
        self.used = 0

    def where(self, t):
        return (t // self.narrow, lax.rem(t, self.narrow))

    def barrier(self):
        sem = pltpu.get_barrier_semaphore()

        def greet(k, carry):
            t = lax.rem(self.me + k, self.nd)
            pl.semaphore_signal(sem, inc=1, device_id=self.where(t), device_id_type=MESH)
            return carry

        lax.fori_loop(1, self.nd, greet, 0)
        pl.semaphore_wait(sem, self.nd - 1)

    def start(self, flows):
        me, nd = self.me, self.nd
        base = self.used
        self.used += len(flows)

        def push(k, carry):
            t = lax.rem(me + k, nd)
            for i, f in enumerate(flows):

                @pl.when(jnp.logical_and(inside(me, f.sources), inside(t, f.targets)))
                def _():
                    pltpu.make_async_remote_copy(
                        src_ref=f.take(me, t),
                        dst_ref=f.put(me, t),
                        send_sem=self.send_sem.at[base + i],
                        recv_sem=self.recv_sem.at[base + i],
                        device_id=self.where(t),
                        device_id_type=MESH,
                    ).start()

            return carry

        for i, f in enumerate(flows):

            @pl.when(jnp.logical_and(inside(me, f.sources), inside(me, f.targets)))
            def _():
                pltpu.make_async_copy(
                    f.take(me, me), f.put(me, me), self.own_sem.at[base + i]
                ).start()

        lax.fori_loop(1, nd, push, 0)
        return base

    def finish(self, flows, base):
        me = self.me
        for i, f in enumerate(flows):
            n_t = f.targets[1] - f.targets[0]
            n_s = f.sources[1] - f.sources[0]
            is_s, is_t = inside(me, f.sources), inside(me, f.targets)

            @pl.when(jnp.logical_and(is_s, is_t))
            def _():
                pltpu.make_async_copy(
                    f.take(me, me), f.put(me, me), self.own_sem.at[base + i]
                ).wait()

            for own in (0, 1):
                mine = is_s if own else jnp.logical_not(is_s)
                if n_s - own > 0:

                    @pl.when(jnp.logical_and(is_t, mine))
                    def _():
                        view = f.many(n_s - own)
                        pltpu.make_async_copy(view, view, self.recv_sem.at[base + i]).wait()

            for own in (0, 1):
                mine = is_t if own else jnp.logical_not(is_t)
                if n_t - own > 0:

                    @pl.when(jnp.logical_and(is_s, mine))
                    def _():
                        view = f.many(n_t - own)
                        pltpu.make_async_copy(view, view, self.send_sem.at[base + i]).wait()


class Unit:
    def __init__(self, count, length):
        self.count, self.length = count, length
        self.tokens = count * length
        self.bits = count.bit_length() - 1
        self.rows = max(16, H * count)
        self.seqs = max(8, count)

    def pick(self):
        lane = iota((self.seqs, self.tokens), 1)
        seq = iota((self.seqs, self.tokens), 0)
        return lane == seq * self.length

    def spread(self):
        row, seq = iota((self.rows, self.seqs), 0), iota((self.rows, self.seqs), 1)
        return as_bf16((row & (self.count - 1)) == seq)

    def collect(self):
        row, seq = iota((self.seqs, self.rows), 1), iota((self.seqs, self.rows), 0)
        return as_bf16((row & (self.count - 1)) == seq)

    def heads(self):
        row, col = iota((self.rows, D), 0), iota((self.rows, D), 1)
        return ((row >> self.bits) == (col >> 6)).astype(F32)

    def live(self):
        row, lane = iota((self.rows, self.tokens), 0), iota((self.rows, self.tokens), 1)
        return (lane >> 5) == (row & (self.count - 1))


def unit_front(unit, emb, e, w_in, w_out, cv, rv, keep):
    center = emb - jnp.mean(emb, axis=0, keepdims=True)
    spread = jnp.mean(center * center, axis=0, keepdims=True)
    scale = lax.rsqrt(spread + NORM_EPS)
    hat = center * scale
    x0 = hat * cv[:, 3 * e : 3 * e + 1] + cv[:, 3 * e + 1 : 3 * e + 2]
    x_low = x0.astype(BF16)
    pick = unit.pick()
    x_first = mm(as_bf16(pick), x_low, NT).astype(BF16)
    x0_first = mm(pick.astype(F32), x0, NT, HIGH)
    q = (mm(x_first, w_in[e, :, 0:D], NN) + rv[8 * e : 8 * e + 1, :]).astype(BF16)
    k = mm(w_in[e, :, D : 2 * D], x_low, TN).astype(BF16)
    v = (mm(w_in[e, :, 2 * D : 3 * D], x_low, TN) + cv[:, 3 * e + 2 : 3 * e + 3]).astype(BF16)
    heads = unit.heads()
    q_heads = (mm(unit.spread(), q, NN) * heads).astype(BF16)
    s = mm(q_heads, k, NN) * 0.125
    if unit.count > 1:
        s = jnp.where(unit.live(), s, -1e30)
    peak = jnp.max(s, axis=1, keepdims=True)
    ex = jnp.exp(s - peak)
    p = ex / jnp.sum(ex, axis=1, keepdims=True)
    mixed = (mm(p.astype(BF16), v, NT) * heads).astype(BF16)
    a = mm(unit.collect(), mixed, NN).astype(BF16)
    o = mm(a, w_out[e], NN) + rv[8 * e + 1 : 8 * e + 2, :]
    keep(hat, scale, x_low, x_first, q, k, v, p, a)
    return x0_first + o


def unit_back(unit, row_grad, e, w_in, w_out, cv, kept):
    hat, scale, x_low, x_first, q, k, v, p, a = kept
    heads = unit.heads()
    spread, collect = unit.spread(), unit.collect()
    p_low = p.astype(BF16)
    do = row_grad.astype(BF16)
    da = mm(do, w_out[e], NT).astype(BF16)
    q_heads = (mm(spread, q, NN) * heads).astype(BF16)
    da_heads = (mm(spread, da, NN) * heads).astype(BF16)
    dp = mm(da_heads, v, NN)
    ds = (p * (dp - jnp.sum(dp * p, axis=1, keepdims=True))).astype(BF16)
    dq_heads = (mm(ds, k, NT) * heads * 0.125).astype(BF16)
    dq = mm(collect, dq_heads, NN).astype(BF16)
    t = mm(ds, x_low, NT) * 0.125
    w = mm(p_low, x_low, NT)
    gk = (mm(q_heads, w_in[e, :, D : 2 * D], NT) * 0.125).astype(BF16)
    ev = mm(da_heads, w_in[e, :, 2 * D : 3 * D], NT).astype(BF16)
    first = row_grad + mm(dq, w_in[e, :, 0:D], NT)
    gx = mm(gk, ds, TN) + mm(ev, p_low, TN)
    gx = gx + mm(first, unit.pick().astype(F32), TN, HIGH)
    p_sum = jnp.sum(p_low.astype(F32), axis=1, keepdims=True)
    dbv = jnp.sum(p_sum * da_heads.astype(F32), axis=0, keepdims=True)
    g_gain = jnp.sum(gx * hat, axis=1, keepdims=True)
    g_shift = jnp.sum(gx, axis=1, keepdims=True)
    scaled = gx * cv[:, 3 * e : 3 * e + 1]
    mean_one = jnp.mean(scaled, axis=0, keepdims=True)
    mean_two = jnp.mean(scaled * hat, axis=0, keepdims=True)
    g_emb = scale * (scaled - mean_one - hat * mean_two)
    return g_emb, t, w, da, dq, do, dbv, g_gain, g_shift


def load_rows(ref, count):
    return jnp.concatenate(
        [ref[pl.ds(j, count, stride=8), :] for j in range(D // LANE)], axis=1
    )


def store_rows(ref, value):
    for j in range(D // LANE):
        ref[pl.ds(j, value.shape[0], stride=8), :] = value[:, j * LANE : (j + 1) * LANE]


def middle_body(
    n_valid, nq, nd, narrow, cols, query_home, token_total,
    mine, mine_q, pos, w_in, w_out, w_up, w_down, cv, rv, b_in, slots,
    o_tok, o_fac, o_facq, o_line, o_lineq, o_du, o_shrink, o_h, o_rows, o_loss,
    hat_s, scale_s, xl_s, xf_s, q_s, k_s, v_s, p_s, a_s,
    hat_q, scale_q, xl_q, xf_q, q_q, k_q, v_q, p_q, a_q,
    r1_own, r1_ownq, r1_all, y_send, y_recv, y_sum, y_all, h_send, h_recv, h_recvq,
    du_own, du_f, gtok, gtok_q, fac, fac_q, line, line_q, f_s, slope_s, hlow_s, g_top_s, sums_s,
    size48,
    send_sem, recv_sem, own_sem,
):
    cap = -(-n_valid // nd)
    rows = n_valid + nq
    net = Net(nd, narrow, send_sem, recv_sem, own_sem)
    me = net.me
    everyone = (0, nd)
    home = (query_home, query_home + 1)
    q_owner = nd - nq
    q_owners = (q_owner, nd)

    def span(c):
        return (0, min(nd, n_valid - c * nd))

    net.barrier()
    passage = Unit(1, LP)
    queries = Unit(nq, LQ)
    n_mine = jnp.where(me < n_valid - (cap - 1) * nd, cap, cap - 1)

    def front(c, carry):
        at = pl.ds(pl.multiple_of(c * LP, LANE), LP)
        emb = (mine[:, :, at].astype(F32) + pos[...].astype(F32)).reshape(D, LP)

        def keep(hat, scale, x_low, x_first, q, k, v, p, a):
            hat_s[c], scale_s[c], xl_s[c], xf_s[c] = hat, scale, x_low, x_first
            q_s[c], k_s[c], v_s[c], p_s[c], a_s[c] = q, k, v, p, a

        r1 = unit_front(passage, emb, 1, w_in, w_out, cv, rv, keep)
        for j in range(D // LANE):
            r1_own[c, j : j + 1, :] = r1[0:1, j * LANE : (j + 1) * LANE]
        return carry

    lax.fori_loop(0, n_mine, front, 0)

    @pl.when(me == query_home)
    def _():
        parts = pos[:, :, 0:LANE].astype(F32).reshape(D, LANE)[:, 0:LQ]
        emb = mine_q[...].astype(F32).reshape(D, nq * LQ) + jnp.concatenate([parts] * nq, axis=1)

        def keep(hat, scale, x_low, x_first, q, k, v, p, a):
            hat_q[...], scale_q[...], xl_q[...], xf_q[...] = hat, scale, x_low, x_first
            q_q[...], k_q[...], v_q[...], p_q[...], a_q[...] = q, k, v, p, a

        store_rows(r1_ownq, unit_front(queries, emb, 0, w_in, w_out, cv, rv, keep))

    flows = [
        Flow(
            lambda s, t, c=c: r1_own.at[c],
            lambda s, t, c=c: r1_all.at[pl.ds(pl.multiple_of(8 * (c * nd + s), 8), 8), :],
            lambda n: r1_all.at[pl.ds(0, 8 * n), :],
            span(c), everyone,
        )
        for c in range(cap)
    ] + [
        Flow(
            lambda s, t: r1_ownq,
            lambda s, t: r1_all.at[pl.ds(8 * n_valid, 8 * nq), :],
            lambda n: y_recv_q(n),
            home, everyone,
        )
    ]

    def y_recv_q(n):
        return h_recvq.at[pl.ds(0, n)]

    base = net.start(flows)
    net.finish(flows, base)

    part = {1: (0, n_valid), 0: (n_valid, nq)}
    y_parts = []
    for e in (1, 0):
        at, n = part[e]
        r1 = load_rows(r1_all.at[pl.ds(8 * at, 8 * n), :], n)
        h, hat1, scale1 = norm_rows(r1, rv[8 * e + 5 : 8 * e + 6, :], rv[8 * e + 2 : 8 * e + 3, :])
        h_low = h.astype(BF16)
        hlow_s[at : at + n, :] = h
        o_h[at : at + n, :] = h_low.astype(F32)
        upper = mm(h_low, w_up[e], NN) + b_in[e : e + 1, :]
        active, slope = gelu_both(upper)
        f_low = active.astype(BF16)
        f_s[at : at + n, :] = f_low.astype(F32)
        slope_s[at : at + n, :] = slope
        y_parts.append(mm(f_low, w_down[e], NN))
    store_rows(y_send, jnp.concatenate(y_parts, axis=0))
    flows = [
        Flow(
            lambda s, t, c=c: y_send.at[pl.ds(pl.multiple_of(8 * (c * nd + t), 8), 8), :],
            lambda s, t, c=c: y_recv.at[s, c],
            lambda n, c=c: y_recv.at[pl.ds(0, n), c],
            everyone, span(c),
        )
        for c in range(cap)
    ] + [
        Flow(
            lambda s, t: y_send.at[pl.ds(pl.multiple_of(8 * (n_valid + t - q_owner), 8), 8), :],
            lambda s, t: y_recv.at[s, cap],
            lambda n: y_recv.at[pl.ds(0, n), cap],
            everyone, q_owners,
        )
    ]
    base = net.start(flows)
    net.finish(flows, base)
    y_sum[...] = jnp.sum(y_recv[...], axis=0)
    flows = [
        Flow(
            lambda s, t, c=c: y_sum.at[c],
            lambda s, t, c=c: y_all.at[pl.ds(pl.multiple_of(8 * (c * nd + s), 8), 8), :],
            lambda n: y_all.at[pl.ds(0, 8 * n), :],
            span(c), everyone,
        )
        for c in range(cap)
    ] + [
        Flow(
            lambda s, t: y_sum.at[cap],
            lambda s, t: y_all.at[pl.ds(pl.multiple_of(8 * (n_valid + s - q_owner), 8), 8), :],
            lambda n: y_all.at[pl.ds(0, 8 * n), :],
            q_owners, everyone,
        )
    ]
    base = net.start(flows)
    net.finish(flows, base)

    tops, vecs = {}, {}
    for e in (1, 0):
        at, n = part[e]
        y = load_rows(y_all.at[pl.ds(8 * at, 8 * n), :], n)
        top = hlow_s[at : at + n, :] + y + rv[8 * e + 3 : 8 * e + 4, :]
        z, hat2, scale2 = norm_rows(
            top, rv[8 * e + 6 : 8 * e + 7, :], rv[8 * e + 4 : 8 * e + 5, :]
        )
        tops[e] = (hat2, scale2)
        vecs[e] = z.astype(BF16)
    qvec, pvec = vecs[0], vecs[1]
    owner = slots[0:1, 0:n_valid]
    is_first = slots[1:2, 0:n_valid] == 1
    kept_slot = slots[2:3, 0:n_valid] == 1
    member = owner == iota((nq, n_valid), 0)
    valid = jnp.broadcast_to(owner >= 0, (nq, n_valid))
    positive = jnp.logical_and(member, is_first)
    negative = jnp.logical_and(member, jnp.logical_and(jnp.logical_not(is_first), kept_slot))
    counts = jnp.sum(member.astype(F32), axis=1, keepdims=True) - 1.0
    score_scale = 2.0 * D ** (-0.5)
    scores = mm(qvec, pvec, NT) * score_scale
    masked = jnp.where(valid, scores, -1e30)
    peak = jnp.max(masked, axis=1, keepdims=True)
    summed = jnp.sum(jnp.where(valid, jnp.exp(masked - peak), 0.0), axis=1, keepdims=True)
    logsum = peak + jnp.log(summed)
    pos_score = jnp.sum(jnp.where(positive, scores, 0.0), axis=1, keepdims=True)
    margins = MARGIN - pos_score + scores
    active = jnp.logical_and(negative, margins > 0)
    hinge = jnp.sum(jnp.where(active, margins, 0.0), axis=1, keepdims=True) / counts
    active_total = jnp.sum(active.astype(F32), axis=1, keepdims=True)
    loss = jnp.sum(logsum - pos_score + hinge, axis=0, keepdims=True)
    o_loss[...] = jnp.broadcast_to(loss, (8, LANE))
    score_grad = (
        jnp.where(valid, jnp.exp(scores - logsum), 0.0)
        - positive.astype(F32) * (1.0 + active_total / counts)
        + active.astype(F32) / counts
    )
    score_low = score_grad.astype(BF16)
    vec_grads = {
        0: (mm(score_low, pvec, NN) * score_scale).astype(BF16).astype(F32),
        1: (mm(score_low, qvec, TN) * score_scale).astype(BF16).astype(F32),
    }
    h_parts, out_rows = [], {}
    for e in (1, 0):
        at, n = part[e]
        hat2, scale2 = tops[e]
        grad = vec_grads[e]
        g_top = norm_rows_back(grad, rv[8 * e + 6 : 8 * e + 7, :], hat2, scale2)
        dy = g_top.astype(BF16)
        g_top_s[at : at + n, :] = g_top
        out_rows[e] = [
            jnp.sum(grad * hat2, axis=0, keepdims=True),
            jnp.sum(grad, axis=0, keepdims=True),
            jnp.sum(dy.astype(F32), axis=0, keepdims=True),
        ]
        f_low = f_s[at : at + n, :].astype(BF16)
        o_shrink[e] = mm(f_low, dy, TN)
        df = mm(dy, w_down[e], NT)
        du = (slope_s[at : at + n, :] * df).astype(BF16)
        du_f[at : at + n, :] = du.astype(F32)
        h_parts.append(mm(du, w_up[e], NT))
    for e in (0, 1):
        for j in range(3):
            o_rows[3 * e + j : 3 * e + j + 1, :] = out_rows[e][j]
    du_own[...] = du_f[...].astype(BF16)
    store_rows(h_send, jnp.concatenate(h_parts, axis=0))
    flows = [
        Flow(
            lambda s, t, c=c: h_send.at[pl.ds(pl.multiple_of(8 * (c * nd + t), 8), 8), :],
            lambda s, t, c=c: h_recv.at[s, c],
            lambda n, c=c: h_recv.at[pl.ds(0, n), c],
            everyone, span(c),
        )
        for c in range(cap)
    ] + [
        Flow(
            lambda s, t: h_send.at[pl.ds(8 * n_valid, 8 * nq), :],
            lambda s, t: h_recvq.at[s],
            lambda n: h_recvq.at[pl.ds(0, n)],
            everyone, home,
        )
    ]
    du_flows = [
        Flow(
            lambda s, t: du_own,
            lambda s, t: o_du.at[s],
            lambda n: o_du.at[pl.ds(0, n)],
            everyone, everyone,
        )
    ]
    base = net.start(flows)
    du_base = net.start(du_flows)
    fac[...] = jnp.zeros_like(fac)
    line[...] = jnp.zeros_like(line)
    sums_s[...] = jnp.zeros_like(sums_s)
    o_tok[:, n_valid * LP + nq * LQ :] = jnp.zeros(
        (cols, token_total - n_valid * LP - nq * LQ), BF16
    )
    net.finish(flows, base)

    def load_rows_sum(ref, count):
        total = jnp.sum(ref[...], axis=0)
        h_send[0 : 8 * count, :] = total
        return load_rows(h_send.at[pl.ds(0, 8 * count), :], count)

    lane = iota((D, LANE), 1)

    def back(c, carry):
        slot = c * nd + me
        tile = jnp.sum(h_recv[:, c], axis=0)
        dh = jnp.concatenate([tile[j : j + 1, :] for j in range(D // LANE)], axis=1)
        top = g_top_s[pl.ds(slot, 1), :]
        g_h = top + dh
        r1 = jnp.concatenate([r1_own[c, j : j + 1, :] for j in range(D // LANE)], axis=1)
        gain1 = rv[8 + 5 : 8 + 6, :]
        _, hat1, scale1 = norm_rows(r1, gain1, gain1)
        g_mid = norm_rows_back(g_h, gain1, hat1, scale1)
        row_grad = jnp.where(iota((8, D), 0) == 0, jnp.broadcast_to(g_mid, (8, D)), 0.0)
        kept = (
            hat_s[c], scale_s[c], xl_s[c], xf_s[c], q_s[c], k_s[c], v_s[c], p_s[c], a_s[c]
        )
        g_emb, t, w, da, dq, do, dbv, g_gain, g_shift = unit_back(
            passage, row_grad, 1, w_in, w_out, cv, kept
        )
        gtok[c] = g_emb.reshape(nd, cols, LP).astype(BF16)
        tw = jnp.concatenate([t, w, xf_s[c].astype(F32), a_s[c].astype(F32)], axis=0)
        tw = jnp.concatenate([tw, jnp.zeros((LANE - 48, D), F32)], axis=0)
        tw_t = jnp.transpose(tw)
        moved = jnp.where(lane < 48, tw_t, 0.0)
        placed = pltpu.roll(moved, 64 * c, 1)
        fac[...] = (fac[...].astype(F32) + placed.reshape(nd, cols, LANE)).astype(BF16)
        which = iota((16, D), 0)
        new = jnp.zeros((16, D), F32)
        for j, row in enumerate((q_s[c], da, dq, do)):
            new = new + jnp.where(which == 2 * j + c, row.astype(F32)[0:1, :], 0.0)
        line[...] = line[...] + new
        columns = jnp.where(lane == 0, g_gain, jnp.where(lane == 1, g_shift, 0.0))
        flat = jnp.transpose(columns)[0:8, :]
        extra = (
            jnp.where(iota((8, D), 0) == 2, dbv, 0.0)
            + jnp.where(iota((8, D), 0) == 3, g_h * hat1, 0.0)
            + jnp.where(iota((8, D), 0) == 4, g_h, 0.0)
        )
        sums_s[...] = sums_s[...] + flat + extra
        return carry

    lax.fori_loop(0, n_mine, back, 0)
    line_q[0:16, :] = (line[...] + jnp.concatenate([jnp.zeros((8, D), F32), sums_s[...]], axis=0)).astype(BF16)

    @pl.when(me == query_home)
    def _():
        dh = load_rows_sum(h_recvq, nq)
        at, n = part[0]
        g_h = g_top_s[at : at + n, :] + dh
        r1 = load_rows(r1_ownq, nq)
        gain1 = rv[5:6, :]
        _, hat1, scale1 = norm_rows(r1, gain1, gain1)
        g_mid = norm_rows_back(g_h, gain1, hat1, scale1)
        kept = (
            hat_q[...], scale_q[...], xl_q[...], xf_q[...], q_q[...], k_q[...], v_q[...],
            p_q[...], a_q[...],
        )
        g_emb, t, w, da, dq, do, dbv, g_gain, g_shift = unit_back(
            queries, g_mid, 0, w_in, w_out, cv, kept
        )
        gtok_q[...] = g_emb.reshape(nd, cols, nq * LQ).astype(BF16)
        tw = jnp.concatenate([t, w, xf_q[...].astype(F32), a_q[...].astype(F32)], axis=0)
        n_tw = tw.shape[0]
        tw = jnp.concatenate([tw, jnp.zeros((fac_q.shape[2] - n_tw, D), F32)], axis=0)
        fac_q[...] = jnp.transpose(tw).reshape(nd, cols, fac_q.shape[2]).astype(BF16)
        columns = jnp.where(lane == 0, g_gain, jnp.where(lane == 1, g_shift, 0.0))
        flat = jnp.transpose(columns)[0:8, :]
        extra = (
            jnp.where(iota((8, D), 0) == 2, dbv, 0.0)
            + jnp.where(iota((8, D), 0) == 3, jnp.sum(g_h * hat1, axis=0, keepdims=True), 0.0)
            + jnp.where(iota((8, D), 0) == 4, jnp.sum(g_h, axis=0, keepdims=True), 0.0)
        )
        block = jnp.concatenate(
            [q_q[...].astype(F32), da.astype(F32), dq.astype(F32), do.astype(F32), flat + extra,
             jnp.zeros((8, D), F32)],
            axis=0,
        )
        line_q[16:64, :] = block.astype(BF16)

    flows = [
        Flow(
            lambda s, t, c=c: gtok.at[c, t],
            lambda s, t, c=c: o_tok.at[:, pl.ds(pl.multiple_of((c * nd + s) * LP, LANE), LP)],
            lambda n: o_tok.at[:, pl.ds(0, n * LP)],
            span(c), everyone,
        )
        for c in range(cap)
    ] + [
        Flow(
            lambda s, t: gtok_q.at[t],
            lambda s, t: o_tok.at[:, pl.ds(n_valid * LP, nq * LQ)],
            lambda n: o_tok.at[:, pl.ds(0, n * nq * LQ)],
            home, everyone,
        ),
        Flow(
            lambda s, t: fac.at[t],
            lambda s, t: o_fac.at[s],
            lambda n: o_fac.at[pl.ds(0, n)],
            everyone, everyone,
        ),
        Flow(
            lambda s, t: fac_q.at[t],
            lambda s, t: o_facq,
            lambda n: fac_q.at[pl.ds(0, n)],
            home, everyone,
        ),
        Flow(
            lambda s, t: line_q.at[pl.ds(0, 16), :],
            lambda s, t: o_line.at[s],
            lambda n: o_line.at[pl.ds(0, n)],
            everyone, everyone,
        ),
        Flow(
            lambda s, t: line_q.at[pl.ds(16, 48), :],
            lambda s, t: o_lineq,
            lambda n: o_line48(n),
            home, everyone,
        ),
    ]

    def o_line48(n):
        return size48.at[pl.ds(0, n)]

    base = net.start(flows)
    net.finish(flows, base)
    net.finish(du_flows, du_base)


def middle(n_valid, nq, nd, narrow, cols, query_home, token_total, arrays):
    cap = -(-n_valid // nd)
    rows = n_valid + nq
    tq = nq * LQ
    unit, unit_q = Unit(1, LP), Unit(nq, LQ)
    fac_lanes = -(-(2 * unit_q.rows + 2 * unit_q.seqs) // LANE) * LANE
    vmem = pl.BlockSpec(memory_space=pltpu.VMEM)

    def like(*shape, dtype=F32):
        return jax.ShapeDtypeStruct(shape, dtype)

    def kept(lead, u):
        return [
            pltpu.VMEM(lead + (D, u.tokens), F32),
            pltpu.VMEM(lead + (1, u.tokens), F32),
            pltpu.VMEM(lead + (D, u.tokens), BF16),
            pltpu.VMEM(lead + (u.seqs, D), BF16),
            pltpu.VMEM(lead + (u.seqs, D), BF16),
            pltpu.VMEM(lead + (D, u.tokens), BF16),
            pltpu.VMEM(lead + (D, u.tokens), BF16),
            pltpu.VMEM(lead + (u.rows, u.tokens), F32),
            pltpu.VMEM(lead + (u.seqs, D), BF16),
        ]

    flows = 5 * (cap + 1) + 5
    return pl.pallas_call(
        functools.partial(
            middle_body, n_valid, nq, nd, narrow, cols, query_home, token_total
        ),
        out_shape=[
            like(cols, token_total, dtype=BF16),
            like(nd, cols, LANE, dtype=BF16),
            like(cols, fac_lanes, dtype=BF16),
            like(nd, 16, D, dtype=BF16),
            like(48, D, dtype=BF16),
            like(nd, rows, LANE, dtype=BF16),
            like(2, LANE, D),
            like(rows, D),
            like(8, D),
            like(8, LANE),
        ],
        in_specs=[vmem] * len(arrays),
        out_specs=[vmem] * 10,
        scratch_shapes=kept((cap,), unit)
        + kept((), unit_q)
        + [
            pltpu.VMEM((cap, 8, LANE), F32),
            pltpu.VMEM((8 * nq, LANE), F32),
            pltpu.VMEM((8 * rows, LANE), F32),
            pltpu.VMEM((8 * rows, LANE), F32),
            pltpu.VMEM((nd, cap + 1, 8, LANE), F32),
            pltpu.VMEM((cap + 1, 8, LANE), F32),
            pltpu.VMEM((8 * rows, LANE), F32),
            pltpu.VMEM((8 * rows, LANE), F32),
            pltpu.VMEM((nd, cap, 8, LANE), F32),
            pltpu.VMEM((nd, 8 * nq, LANE), F32),
            pltpu.VMEM((rows, LANE), BF16),
            pltpu.VMEM((rows, LANE), F32),
            pltpu.VMEM((cap, nd, cols, LP), BF16),
            pltpu.VMEM((nd, cols, tq), BF16),
            pltpu.VMEM((nd, cols, LANE), BF16),
            pltpu.VMEM((nd, cols, fac_lanes), BF16),
            pltpu.VMEM((16, D), F32),
            pltpu.VMEM((64, D), BF16),
            pltpu.VMEM((rows, LANE), F32),
            pltpu.VMEM((rows, LANE), F32),
            pltpu.VMEM((rows, D), F32),
            pltpu.VMEM((rows, D), F32),
            pltpu.VMEM((8, D), F32),
            pltpu.VMEM((nd, 48, D), BF16),
            pltpu.SemaphoreType.DMA((flows,)),
            pltpu.SemaphoreType.DMA((flows,)),
            pltpu.SemaphoreType.DMA((flows,)),
        ],
        compiler_params=pltpu.CompilerParams(
            collective_id=3, has_side_effects=True, vmem_limit_bytes=62 * 1024 * 1024
        ),
        name="middle",
    )(*arrays)


def on_device_rows(
    passage_ids, query_ids, passage_query, kept_mask, neg_count, step_count,
    embed_table, attend_in, attend_out, expand_weight, shrink_weight, norm_gains, bias_terms,
    embed_first, embed_second, attend_in_first, attend_in_second,
    attend_out_first, attend_out_second, expand_first, expand_second,
    shrink_first, shrink_second, gains_first, gains_second, bias_first, bias_second,
):
    narrow = lax.axis_size("narrow")
    nd = lax.axis_size("wide") * narrow
    me = lax.axis_index("wide") * narrow + lax.axis_index("narrow")
    cols = embed_table.shape[1]
    n_slots = passage_query.shape[0]
    nq = query_ids.shape[0] * lax.axis_size("wide")
    n_valid = VALID_PER_QUERY * nq
    cap = -(-n_valid // nd)
    rows_p = cap * nd
    ff_cols = FF // nd

    exch = functools.partial(comm, nd=nd, narrow=narrow)
    rows_c = -(-cols // 8) * 8
    n_ids = passage_ids.shape[0] + query_ids.shape[0]
    small_width = max(cols, bias_terms.shape[1], 1)
    small_width = -(-small_width // LANE) * LANE

    def widen(value, width):
        return jnp.pad(value, ((0, 0), (0, width - value.shape[1])))

    ids_mine = jnp.concatenate([passage_ids, widen(query_ids, LP)])
    small_mine = jnp.concatenate(
        [widen(norm_gains.reshape(6, cols), small_width), widen(bias_terms, small_width)]
    ).astype(BF16)
    ids_got, small_got = exch(
        1,
        [ids_mine, small_mine],
        [((nd, n_ids, LP), jnp.int32), ((nd, 8, small_width), BF16)],
        [send_all(0, 0, nd), send_all(1, 1, nd)],
    )
    n_own = passage_ids.shape[0]
    pid = ids_got[:, :n_own].reshape(n_slots, LP)[:n_valid]
    qid = ids_got.reshape(-1, narrow, n_ids, LP)[:, 0, n_own:, :LANE].reshape(nq, LANE)
    all_ids = jnp.concatenate([pid.reshape(-1), qid.reshape(-1)])
    gains = small_got[:, :6, :cols].transpose(1, 0, 2).reshape(2, 3, D).astype(F32)
    bias = small_got[:, 6:, : bias_terms.shape[1]].transpose(1, 0, 2).reshape(2, -1).astype(F32)

    table_t = embed_table.T
    table_low = table_t.astype(BF16)
    vocab = V + LP
    total = -(-vocab // HASH) * HASH
    table_pad = jnp.pad(table_low, ((0, rows_c - cols), (0, total - vocab)))
    got = table_rows(table_pad, all_ids)
    pos_mine = table_pad[:, V : V + LP]
    up_mine = expand_weight.astype(BF16).reshape(2 * cols, nd, ff_cols).transpose(1, 0, 2)
    q_from = n_valid * LP
    width = cap * LP + LANE

    def passage_move(c, forward):
        span = (0, min(nd, n_valid - c * nd))
        if forward:
            return Send(
                0, 0,
                lambda ref, s, t: ref.at[:, pl.ds(pl.multiple_of((c * nd + t) * LP, LANE), LP)],
                lambda ref, s, t: ref.at[s, :, pl.ds(c * LP, LP)],
                lambda ref, n: ref.at[:, pl.ds(0, n * LP)],
                lambda ref, n: ref.at[pl.ds(0, n), :, pl.ds(0, LP)],
                (0, nd), span,
            )
        return Send(
            0, 0,
            lambda ref, s, t: ref.at[t, :, pl.ds(c * LP, LP)],
            lambda ref, s, t: ref.at[:, pl.ds(pl.multiple_of((c * nd + s) * LP, LANE), LP)],
            lambda ref, n: ref.at[pl.ds(0, n), :, pl.ds(0, LP)],
            lambda ref, n: ref.at[:, pl.ds(0, n * LP)],
            span, (0, nd),
        )

    def query_move(forward):
        span = (nd - nq, nd)
        if forward:
            return Send(
                0, 0,
                lambda ref, s, t: ref.at[
                    :, pl.ds(pl.multiple_of(q_from + (t - (nd - nq)) * LANE, LANE), LANE)
                ],
                lambda ref, s, t: ref.at[s, :, pl.ds(cap * LP, LANE)],
                lambda ref, n: ref.at[:, pl.ds(0, n * LANE)],
                lambda ref, n: ref.at[pl.ds(0, n), :, pl.ds(0, LANE)],
                (0, nd), span,
            )
        return Send(
            0, 0,
            lambda ref, s, t: ref.at[t, :, pl.ds(cap * LP, LANE)],
            lambda ref, s, t: ref.at[
                :, pl.ds(pl.multiple_of(q_from + (s - (nd - nq)) * LANE, LANE), LANE)
            ],
            lambda ref, n: ref.at[pl.ds(0, n), :, pl.ds(0, LANE)],
            lambda ref, n: ref.at[:, pl.ds(0, n * LANE)],
            span, (0, nd),
        )

    mine, pos, w_up = exch(
        2,
        [got, pos_mine, up_mine],
        [((nd, rows_c, width), BF16), ((nd, rows_c, LP), BF16), ((nd, 2 * cols, ff_cols), BF16)],
        [passage_move(c, True) for c in range(cap)]
        + [query_move(True), send_all(1, 1, nd), send_blocks(2, 2, nd)],
    )
    live = jnp.concatenate(
        [jnp.broadcast_to(c * nd + me < n_valid, (LP,)) for c in range(cap)]
        + [jnp.broadcast_to(me >= nd - nq, (LANE,))]
    )
    mine = jnp.where(live, mine[:, :cols].reshape(D, width), 0)
    pos = pos[:, :cols].reshape(D, LP).astype(F32)
    w_up = w_up.reshape(nd, 2, cols, ff_cols).transpose(1, 0, 2, 3).reshape(2, D, ff_cols)
    w_down = shrink_weight.astype(BF16)
    w_in = lax.all_gather(attend_in.astype(BF16), AXES, axis=1, tiled=True)
    w_out = lax.all_gather(attend_out.astype(BF16), AXES, axis=1, tiled=True)

    fronts = []
    for c in range(cap):
        emb = mine[:, c * LP : (c + 1) * LP].astype(F32) + pos
        fronts.append(encode_front(emb, w_in[1], w_out[1], gains[1], bias[1], LP))
    emb = mine[:, cap * LP :].astype(F32) + pos[:, :LANE]
    fronts.append(encode_front(emb, w_in[0], w_out[0], gains[0], bias[0], LQ))
    (rows,) = exch(
        3, [jnp.stack([f[0] for f in fronts])], [((nd, cap + 1, D), F32)], [send_all(0, 0, nd)]
    )
    row_in = (rows[nd - nq :, cap], rows[:, :cap].transpose(1, 0, 2).reshape(rows_p, D))

    def by_owner(queries, passages):
        q_part = jnp.pad(queries, ((nd - nq, 0), (0, 0)))[:, None]
        return jnp.concatenate([passages.reshape(cap, nd, D).transpose(1, 0, 2), q_part], axis=1)

    def to_rows(blocks):
        return (
            blocks[nd - nq :, cap],
            blocks[:, :cap].transpose(1, 0, 2).reshape(rows_p, D),
        )


    mids, ups = [], []
    partial_y = []
    b_in_all = bias[:, O_IN : O_IN + FF].reshape(2, nd, ff_cols)
    b_in = lax.dynamic_index_in_dim(b_in_all, me, 1, False)
    for e in range(2):
        h, hat1, scale1 = norm_rows(row_in[e], gains[e, 1], bias[e, O_1 : O_1 + D])
        h_low = h.astype(BF16)
        upper = dot(h_low, w_up[e], ((1,), (0,))) + b_in[e]
        active, slope = gelu_both(upper)
        f_low = active.astype(BF16)
        partial_y.append(dot(f_low, w_down[e], ((1,), (0,))))
        mids.append((h, hat1, scale1, h_low))
        ups.append((f_low, slope))
    (y_parts,) = exch(
        4, [by_owner(*partial_y)], [((nd, cap + 1, D), F32)], [send_blocks(0, 0, nd)]
    )
    (y_all,) = exch(
        5, [jnp.sum(y_parts, axis=0)], [((nd, cap + 1, D), F32)], [send_all(0, 0, nd)]
    )
    y = to_rows(y_all)
    tops = []
    vecs = []
    for e in range(2):
        z, hat2, scale2 = norm_rows(
            mids[e][0] + y[e] + bias[e, O_OUT : O_OUT + D], gains[e, 2], bias[e, O_2 : O_2 + D]
        )
        tops.append((hat2, scale2))
        vecs.append(z.astype(BF16))
    qvec, pvec = vecs

    owner = passage_query[:rows_p]
    kept = kept_mask[:rows_p] == 1
    earlier = jnp.concatenate([jnp.full((1,), -1, jnp.int32), owner[:-1]])
    valid = owner >= 0
    first = valid & (owner != earlier)
    member = owner[None, :] == jnp.arange(nq, dtype=jnp.int32)[:, None]
    positive = member & first[None, :]
    negative = member & jnp.logical_not(first)[None, :] & kept[None, :]
    counts = jnp.sum(member.astype(F32), axis=1) - 1.0
    score_scale = 2.0 * D ** (-0.5)
    scores = dot(qvec, pvec, ((1,), (1,))) * score_scale
    masked = jnp.where(valid[None, :], scores, -1e30)
    peak = jnp.max(masked, axis=1)
    summed = jnp.sum(jnp.where(valid[None, :], jnp.exp(masked - peak[:, None]), 0.0), axis=1)
    logsum = peak + jnp.log(summed)
    pos_score = jnp.sum(jnp.where(positive, scores, 0.0), axis=1)
    margins = MARGIN - pos_score[:, None] + scores
    active_neg = negative & (margins > 0)
    hinge = jnp.sum(jnp.where(active_neg, margins, 0.0), axis=1) / counts
    active_total = jnp.sum(active_neg.astype(F32), axis=1)
    loss = jnp.sum(logsum - pos_score + hinge)
    score_grad = (
        jnp.where(valid[None, :], jnp.exp(scores - logsum[:, None]), 0.0)
        - positive.astype(F32) * (1.0 + active_total / counts)[:, None]
        + active_neg.astype(F32) / counts[:, None]
    )
    score_low = score_grad.astype(BF16)
    vec_grads = (
        (dot(score_low, pvec, ((1,), (0,))) * score_scale).astype(BF16).astype(F32),
        (dot(score_low, qvec, ((0,), (0,))) * score_scale).astype(BF16).astype(F32),
    )

    partial_h = []
    gain_grads = [[None] * 3 for _ in range(2)]
    shifts = [dict() for _ in range(2)]
    top_grads, shrink_grads, du_parts = [], [], []
    for e in range(2):
        hat2, scale2 = tops[e]
        gain_grads[e][2] = jnp.sum(vec_grads[e] * hat2, axis=0)
        shifts[e]["2"] = jnp.sum(vec_grads[e], axis=0)
        g_top = norm_rows_back(vec_grads[e], gains[e, 2], hat2, scale2)
        dy = g_top.astype(BF16)
        shifts[e]["out"] = jnp.sum(dy.astype(F32), axis=0)
        f_low, slope = ups[e]
        shrink_grads.append(dot(f_low, dy, ((0,), (0,))))
        df = dot(dy, w_down[e], ((1,), (1,)))
        du = (slope * df).astype(BF16)
        du_parts.append(du)
        partial_h.append(dot(du, w_up[e], ((1,), (1,))))
        top_grads.append(g_top)
    du_mine = jnp.concatenate(du_parts)
    h_parts, du_all = exch(
        6,
        [by_owner(*partial_h), du_mine],
        [((nd, cap + 1, D), F32), ((nd, nq + rows_p, ff_cols), BF16)],
        [send_blocks(0, 0, nd), send_all(1, 1, nd)],
    )
    h_mine = jnp.sum(h_parts, axis=0)
    top_mine = lax.dynamic_index_in_dim(by_owner(*top_grads), me, 0, False)
    rows_mine = lax.dynamic_index_in_dim(rows, me, 0, False)
    is_q = (me >= nd - nq).astype(F32)
    has = jnp.stack([(c * nd + me < n_valid).astype(F32) for c in range(cap)] + [is_q])
    g_h = (top_mine + h_mine) * has[:, None]
    gain_one = jnp.stack([gains[1, 1]] * cap + [gains[0, 1]])
    shift_one = jnp.stack([bias[1, O_1 : O_1 + D]] * cap + [bias[0, O_1 : O_1 + D]])
    _, hat_mine, scale_mine = norm_rows(rows_mine, gain_one, shift_one)
    g_mid = norm_rows_back(g_h, gain_one, hat_mine, scale_mine)
    gain_mid = g_h * hat_mine
    do_mine = g_mid.astype(BF16)
    backs = [
        encode_back(
            fronts[c][1], g_mid[c], w_in[1 if c < cap else 0], w_out[1 if c < cap else 0],
            gains[1 if c < cap else 0],
        )
        for c in range(cap + 1)
    ]

    def both_encoders(pick):
        return jnp.stack([pick(cap), sum(pick(c) for c in range(cap))])

    sums = jnp.concatenate(
        [both_encoders(lambda i, j=j: backs[i][1][j]) for j in (5, 6, 7)]
        + [both_encoders(lambda i: gain_mid[i]), both_encoders(lambda i: g_h[i])]
    )
    line = jnp.concatenate(
        [jnp.stack([b[1][j] for b in backs]) for j in (2, 3, 4)] + [do_mine, sums.astype(BF16)]
    )
    n_line = 4 * (cap + 1) + 10
    factor_t = jnp.concatenate(
        [b[1][0] for b in backs] + [b[1][1] for b in backs]
        + [f[1][2][:, 0][None] for f in fronts] + [f[1][8][None] for f in fronts]
    )
    n_factor = factor_t.shape[0]
    f_pad = -(-n_factor // LANE) * LANE
    factor_cols = jnp.pad(factor_t, ((0, f_pad - n_factor), (0, 0))).T

    def pad_rows(value):
        value = value.reshape(nd, cols, value.shape[1])
        return jnp.pad(value, ((0, 0), (0, rows_c - cols), (0, 0)))

    send = pad_rows(jnp.concatenate([b[0] for b in backs], axis=1).astype(BF16))
    token_grads, factors, lines = exch(
        7,
        [send, pad_rows(factor_cols), line],
        [
            ((rows_c, n_valid * LP + nq * LANE), BF16),
            ((nd, rows_c, f_pad), BF16),
            ((nd, n_line, D), BF16),
        ],
        [passage_move(c, False) for c in range(cap)]
        + [query_move(False), send_blocks(1, 1, nd), send_all(2, 2, nd)],
    )
    table_grad = table_sums(token_grads, all_ids, total)[:cols, :vocab]
    token_grads = token_grads[:cols].astype(F32)
    pos_grad = jnp.sum(token_grads[:, :q_from].reshape(cols, n_valid, LP), axis=1)
    pos_grad = pos_grad.at[:, :LANE].add(
        jnp.sum(token_grads[:, q_from:].reshape(cols, nq, LANE), axis=1)
    )
    table_grad = table_grad.at[:, V:].add(pos_grad)

    step_h = (cap + 1) * H
    factors = factors[:, :cols].transpose(0, 2, 1)
    t_all = factors[:, :step_h].reshape(nd, cap + 1, H, cols)
    w_all = factors[:, step_h : 2 * step_h].reshape(nd, cap + 1, H, cols)
    x_all = factors[:, 2 * step_h : 2 * step_h + cap + 1]
    a_all = factors[:, 2 * step_h + cap + 1 : 2 * step_h + 2 * (cap + 1)]
    q_all, da_all, dq_all, do_all = (
        lines[:, j * (cap + 1) : (j + 1) * (cap + 1)] for j in range(4)
    )
    sums = jnp.sum(lines[:, 4 * (cap + 1) :].astype(F32), axis=0).reshape(5, 2, D)

    def of_encoder(value, e):
        if e == 0:
            return value[nd - nq :, cap]
        return value[:, :cap].reshape((nd * cap,) + value.shape[2:])

    du_all = du_all.transpose(1, 0, 2).reshape(nq + rows_p, FF)
    in_grads, out_grads, expand_grads = [], [], []
    for e in range(2):
        du_full = du_all[:nq] if e == 0 else du_all[nq:]
        shifts[e]["in"] = jnp.sum(du_full.astype(F32), axis=0)
        h_cols = lax.dynamic_slice_in_dim(mids[e][3], me * cols, cols, 1)
        expand_grads.append(dot(h_cols, du_full, ((0,), (0,))))
        t, w, x, a = (of_encoder(u, e) for u in (t_all, w_all, x_all, a_all))
        q, da, dq, do = (of_encoder(u, e) for u in (q_all, da_all, dq_all, do_all))
        rows_e = q.shape[0]
        qh = q.reshape(rows_e, H, HD)
        dah = da.reshape(rows_e, H, HD)
        g_q = dot(x, dq, ((0,), (0,)))
        g_k = jnp.einsum("phi,phd->ihd", t, qh, preferred_element_type=F32).reshape(cols, D)
        g_v = jnp.einsum("phi,phd->ihd", w, dah, preferred_element_type=F32).reshape(cols, D)
        in_grads.append(jnp.concatenate([g_q, g_k, g_v], axis=1))
        out_grads.append(dot(a, do, ((0,), (0,))))
        shifts[e]["q"] = jnp.sum(dq.astype(F32), axis=0)
        shifts[e]["o"] = jnp.sum(do.astype(F32), axis=0)
    gain_grad = jnp.stack(
        [jnp.stack([sums[1, e], sums[3, e], gain_grads[e][2]]) for e in range(2)]
    )
    bias_grad = jnp.stack(
        [
            jnp.concatenate(
                [shifts[e]["q"], sums[0, e], shifts[e]["o"], sums[4, e], shifts[e]["in"],
                 shifts[e]["out"], shifts[e]["2"], sums[2, e]]
            )
            for e in range(2)
        ]
    )
    grads = (
        table_grad.T,
        jnp.stack(in_grads),
        jnp.stack(out_grads),
        jnp.stack(expand_grads),
        jnp.stack(shrink_grads),
        lax.dynamic_slice_in_dim(gain_grad, me * cols, cols, 2),
        lax.dynamic_slice_in_dim(bias_grad, me * bias_terms.shape[1], bias_terms.shape[1], 1),
    )
    local_squares = sum(jnp.sum(g * g) for g in grads)
    (squares,) = exch(
        8, [jnp.broadcast_to(local_squares, (8, LANE))], [((nd, 8, LANE), F32)],
        [send_all(0, 0, nd)],
    )
    grad_norm = jnp.sqrt(jnp.sum(squares[:, 0, 0]))
    factor = CLIP / jnp.maximum(grad_norm, CLIP)
    step = step_count[0].astype(F32)
    masters = (embed_table, attend_in, attend_out, expand_weight, shrink_weight, norm_gains, bias_terms)
    firsts = (embed_first, attend_in_first, attend_out_first, expand_first, shrink_first, gains_first, bias_first)
    seconds = (embed_second, attend_in_second, attend_out_second, expand_second, shrink_second, gains_second, bias_second)
    results = [loss, grad_norm]
    for index in range(7):
        results.extend(
            adam_update(masters[index], grads[index] * factor, firsts[index], seconds[index], step, LEARN_RATES[index])
        )
    return tuple(results)


def on_device(
    passage_ids, query_ids, passage_query, kept_mask, neg_count, step_count,
    embed_table, attend_in, attend_out, expand_weight, shrink_weight, norm_gains, bias_terms,
    embed_first, embed_second, attend_in_first, attend_in_second,
    attend_out_first, attend_out_second, expand_first, expand_second,
    shrink_first, shrink_second, gains_first, gains_second, bias_first, bias_second,
):
    if embed_table.shape[1] % 8 != 0:
        return on_device_rows(
            passage_ids, query_ids, passage_query, kept_mask, neg_count, step_count,
            embed_table, attend_in, attend_out, expand_weight, shrink_weight, norm_gains,
            bias_terms, embed_first, embed_second, attend_in_first, attend_in_second,
            attend_out_first, attend_out_second, expand_first, expand_second,
            shrink_first, shrink_second, gains_first, gains_second, bias_first, bias_second,
        )
    narrow = lax.axis_size("narrow")
    nd = lax.axis_size("wide") * narrow
    me = lax.axis_index("wide") * narrow + lax.axis_index("narrow")
    cols = embed_table.shape[1]
    n_slots = passage_query.shape[0]
    per_wide = query_ids.shape[0]
    nq = per_wide * lax.axis_size("wide")
    n_valid = VALID_PER_QUERY * nq
    cap = -(-n_valid // nd)
    ff_cols = FF // nd
    rows = n_valid + nq
    tq = nq * LQ
    query_home = nd * 5 // 8 - 1
    exch = functools.partial(comm, nd=nd, narrow=narrow)
    small_width = -(-max(cols, bias_terms.shape[1]) // LANE) * LANE
    ids_width = max(LP, -(-tq // LANE) * LANE)

    def widen(value, width):
        return jnp.pad(value, ((0, 0), (0, width - value.shape[1])))

    spot = jnp.arange(tq) // (LQ * per_wide) == lax.axis_index("wide")
    spot = spot & (lax.axis_index("narrow") == 0)
    q_line = jnp.where(spot, jnp.tile(query_ids.reshape(-1), tq // (LQ * per_wide)), 0)
    ids_mine = jnp.concatenate([widen(passage_ids, ids_width), widen(q_line[None], ids_width)])
    small_mine = jnp.concatenate(
        [widen(norm_gains.reshape(6, cols), small_width), widen(bias_terms, small_width)]
    ).astype(BF16)
    n_own = passage_ids.shape[0]
    ids_got, small_got = exch(
        1,
        [ids_mine, small_mine],
        [((nd, n_own + 1, ids_width), jnp.int32), ((nd, 8, small_width), BF16)],
        [send_all(0, 0, nd), send_all(1, 1, nd)],
    )
    pid = ids_got[:, :n_own, :LP].reshape(n_slots, LP)[:n_valid]
    qid = jnp.sum(ids_got[:, n_own, :tq], axis=0)
    q_from = n_valid * LP
    token_total = -(-(q_from + tq) // 1024) * 1024
    all_ids = jnp.pad(jnp.concatenate([pid.reshape(-1), qid]), (0, token_total - q_from - tq))
    gains = small_got[:, :6, :cols].transpose(1, 0, 2).reshape(2, 3, D).astype(F32)
    bias = small_got[:, 6:, : bias_terms.shape[1]].transpose(1, 0, 2).reshape(2, -1).astype(F32)

    vocab = V + LP
    total = -(-vocab // HASH) * HASH
    table_low = jnp.pad(embed_table.T.astype(BF16), ((0, 0), (0, total - vocab)))
    got = table_rows(table_low, all_ids)
    pos_mine = table_low[:, V : V + LP]
    up_mine = expand_weight.astype(BF16).reshape(2 * cols, nd, ff_cols).transpose(1, 0, 2)

    def passage_move(c):
        return Send(
            0, 0,
            lambda ref, s, t: ref.at[:, pl.ds(pl.multiple_of((c * nd + t) * LP, LANE), LP)],
            lambda ref, s, t: ref.at[s, :, pl.ds(c * LP, LP)],
            lambda ref, n: ref.at[:, pl.ds(0, n * LP)],
            lambda ref, n: ref.at[pl.ds(0, n), :, pl.ds(0, LP)],
            (0, nd), (0, min(nd, n_valid - c * nd)),
        )

    query_move = Send(
        0, 1,
        lambda ref, s, t: ref.at[:, pl.ds(q_from, tq)],
        lambda ref, s, t: ref.at[s],
        lambda ref, n: ref.at[:, pl.ds(0, n * tq)],
        lambda ref, n: ref.at[pl.ds(0, n)],
        (0, nd), (query_home, query_home + 1),
    )
    mine, mine_q, pos, w_up = exch(
        2,
        [got, pos_mine, up_mine],
        [
            ((nd, cols, cap * LP), BF16), ((nd, cols, tq), BF16), ((nd, cols, LP), BF16),
            ((nd, 2 * cols, ff_cols), BF16),
        ],
        [passage_move(c) for c in range(cap)]
        + [query_move, send_all(1, 2, nd), send_blocks(2, 3, nd)],
    )
    w_up = w_up.reshape(nd, 2, cols, ff_cols).transpose(1, 0, 2, 3).reshape(2, D, ff_cols)
    w_up = jnp.pad(w_up, ((0, 0), (0, 0), (0, LANE - ff_cols)))
    w_down = jnp.pad(shrink_weight.astype(BF16), ((0, 0), (0, LANE - ff_cols), (0, 0)))
    w_in = lax.all_gather(attend_in.astype(BF16), AXES, axis=1, tiled=True)
    w_out = lax.all_gather(attend_out.astype(BF16), AXES, axis=1, tiled=True)
    cv = jnp.stack(
        [v for e in range(2) for v in (
            gains[e, 0], bias[e, O_EMB : O_EMB + D], bias[e, O_V : O_V + D])]
        + [jnp.zeros((D,), F32)] * 2,
        axis=1,
    )
    rv = jnp.stack(
        [v for e in range(2) for v in (
            bias[e, O_Q : O_Q + D], bias[e, O_O : O_O + D], bias[e, O_1 : O_1 + D],
            bias[e, O_OUT : O_OUT + D], bias[e, O_2 : O_2 + D], gains[e, 1], gains[e, 2],
            jnp.zeros((D,), F32))]
    )
    b_in = lax.dynamic_index_in_dim(
        bias[:, O_IN : O_IN + FF].reshape(2, nd, ff_cols), me, 1, False
    )
    b_in = jnp.pad(b_in, ((0, 6), (0, LANE - ff_cols)))
    earlier = jnp.concatenate([jnp.full((1,), -1, jnp.int32), passage_query[:-1]])
    first_slot = ((passage_query >= 0) & (passage_query != earlier)).astype(jnp.int32)
    slots = jnp.pad(
        jnp.stack([passage_query, first_slot, kept_mask])[:, :n_valid],
        ((0, 5), (0, -(-n_valid // LANE) * LANE - n_valid)),
    )
    tok, fac, fac_q, line, line_q, du_all, shrink_g, h_low, out_rows, loss = middle(
        n_valid, nq, nd, narrow, cols, query_home, token_total,
        [mine, mine_q, pos, w_in, w_out, w_up, w_down, cv, rv, b_in, slots],
    )
    loss = loss[0, 0]

    table_grad = table_sums(tok, all_ids, total)[:, :vocab]
    tok = tok.astype(F32)
    pos_grad = jnp.sum(tok[:, :q_from].reshape(cols, n_valid, LP), axis=1)
    q_pos = jnp.sum(tok[:, q_from : q_from + tq].reshape(cols, nq, LQ), axis=1)
    pos_grad = pos_grad.at[:, :LQ].add(q_pos)
    table_grad = table_grad.at[:, V:].add(pos_grad)

    by_lane = fac.transpose(0, 2, 1).reshape(nd, 2, 64, cols)[:, :cap]
    q_rows = H * nq
    q_lane = fac_q.T
    heads_q = lambda v: v.reshape(H, nq, cols).transpose(1, 0, 2)
    factors = {
        1: tuple(
            v.reshape((nd * cap,) + v.shape[2:])
            for v in (by_lane[:, :, 0:H], by_lane[:, :, 16 : 16 + H], by_lane[:, :, 32],
                      by_lane[:, :, 40])
        ),
        0: (
            heads_q(q_lane[:q_rows]), heads_q(q_lane[q_rows : 2 * q_rows]),
            q_lane[2 * q_rows : 2 * q_rows + nq], q_lane[2 * q_rows + nq : 2 * q_rows + 2 * nq],
        ),
    }
    lines = {
        1: tuple(line[:, 2 * j : 2 * j + cap].reshape(nd * cap, D) for j in range(4)),
        0: tuple(line_q[nq * j : nq * (j + 1)] for j in range(4)),
    }
    sums = {1: jnp.sum(line[:, 8:13].astype(F32), axis=0), 0: line_q[32:37].astype(F32)}
    du_rows = du_all[:, :, :ff_cols].transpose(1, 0, 2).reshape(rows, FF)
    h_cols = lax.dynamic_slice_in_dim(h_low, me * cols, cols, 1).astype(BF16)
    in_grads, out_grads, expand_grads, bias_parts, gain_parts = [], [], [], [], []
    for e in range(2):
        at, n = (n_valid, nq) if e == 0 else (0, n_valid)
        du_e = du_rows[at : at + n]
        expand_grads.append(dot(h_cols[at : at + n], du_e, ((0,), (0,))))
        t, w, x, a = factors[e]
        q, da, dq, do = lines[e]
        n_e = q.shape[0]
        g_q = dot(x, dq, ((0,), (0,)))
        g_k = jnp.einsum(
            "phi,phd->ihd", t, q.reshape(n_e, H, HD), preferred_element_type=F32
        ).reshape(cols, D)
        g_v = jnp.einsum(
            "phi,phd->ihd", w, da.reshape(n_e, H, HD), preferred_element_type=F32
        ).reshape(cols, D)
        in_grads.append(jnp.concatenate([g_q, g_k, g_v], axis=1))
        out_grads.append(dot(a, do, ((0,), (0,))))
        s = sums[e]
        gain_parts.append(jnp.stack([s[0], s[3], out_rows[3 * e]]))
        bias_parts.append(
            jnp.concatenate(
                [jnp.sum(dq.astype(F32), axis=0), s[2], jnp.sum(do.astype(F32), axis=0), s[4],
                 jnp.sum(du_e.astype(F32), axis=0), out_rows[3 * e + 2], out_rows[3 * e + 1], s[1]]
            )
        )
    grads = (
        table_grad.T,
        jnp.stack(in_grads),
        jnp.stack(out_grads),
        jnp.stack(expand_grads),
        shrink_g[:, :ff_cols],
        lax.dynamic_slice_in_dim(jnp.stack(gain_parts), me * cols, cols, 2),
        lax.dynamic_slice_in_dim(
            jnp.stack(bias_parts), me * bias_terms.shape[1], bias_terms.shape[1], 1
        ),
    )
    local_squares = sum(jnp.sum(g * g) for g in grads)
    (squares,) = exch(
        8, [jnp.broadcast_to(local_squares, (8, LANE))], [((nd, 8, LANE), F32)],
        [send_all(0, 0, nd)],
    )
    grad_norm = jnp.sqrt(jnp.sum(squares[:, 0, 0]))
    factor = CLIP / jnp.maximum(grad_norm, CLIP)
    step = step_count[0].astype(F32)
    masters = (embed_table, attend_in, attend_out, expand_weight, shrink_weight, norm_gains, bias_terms)
    firsts = (embed_first, attend_in_first, attend_out_first, expand_first, shrink_first, gains_first, bias_first)
    seconds = (embed_second, attend_in_second, attend_out_second, expand_second, shrink_second, gains_second, bias_second)
    results = [loss, grad_norm]
    for index in range(7):
        results.extend(
            adam_update(masters[index], grads[index] * factor, firsts[index], seconds[index], step, LEARN_RATES[index])
        )
    return tuple(results)


def solution(mesh):
    both = ("wide", "narrow")
    weight_specs = (P(None, both),) + (P(None, both, None),) * 4 + (P(None, None, both), P(None, both))
    pairs = tuple(s for spec in weight_specs for s in (spec, spec))
    in_specs = (P(both, None), P("wide", None), P(), P(), P("wide"), P()) + weight_specs + pairs
    out_specs = (P(), P()) + tuple(s for spec in weight_specs for s in (spec, spec, spec))
    return jax.shard_map(on_device, mesh=mesh, in_specs=in_specs, out_specs=out_specs, check_vma=False)
```

profile of v0, /device:TPU:0, one launch (start us, length us, event | category | flops | bytes accessed | tf_op | source)
XLA Modules:
  0.0 385.0 jit_solution(2599382601055292296)
XLA Ops:
  7.2 1.7 convert_element_type.92
  9.0 1.7 convert_element_type.91
  12.9 1.3 pad_add_fusion.1.refs_0_
  14.8 16.4 %shard_map.425 = (s32[32,3,384]{2,1,0:T(4,128)}, bf16[32,8,384]{2,1,0:T(8,128)(2,1)}) custom-call(s32[3,384]{1,0:T(4,128)} %pad_add_fusion.1.refs_0_, bf16[8,384]{1,0:T(8,128)(2,1)} %fusion.18.refs_1_), custom_call_target="tpu_custom_call" | custom-call | tf_op jit(solution)/shard_map/pallas_call | solution.py:157
  31.3 1.0 convert_bitcast_fusion.2
  32.4 0.9 convert_bitcast_fusion.1
  33.6 0.9 copy.115.cv
  35.2 0.9 slice.268
  36.2 1.0 slice_reduce_fusion
  38.6 1.0 pad.42.table_ref
  39.9 0.9 copy.172
  40.8 23.0 %table_rows.1.refs_0_ = bf16[24,16384]{1,0:T(8,128)(2,1)} custom-call(bf16[24,18432]{1,0:T(8,128)(2,1)} %pad.42.table_ref, s32[32,1,512]{2,1,0:T(1,128)} %bitcast.117), custom_call_target="tpu_custom_call" | custom-call | tf_op jit(solution)/shard_map/table_rows/pallas_call | solution.py:226
  63.9 41.1 %shard_map.426 = (bf16[32,24,768]{2,1,0:T(8,128)(2,1)}, bf16[32,24,256]{2,1,0:T(8,128)(2,1)}, bf16[32,24,384]{2,1,0:T(8,128)(2,1)}, bf16[32,48,96]{2,1,0:T(8,128)(2,1)}) custom-call(bf16[24,16384]{1,0:T(8,128)(2,1)} %table_rows.1.refs_0_, bf16[24,384]{1,0:T(8,128)(2,1)} %slice.345.refs_1_, bf16[32,48,96]{2,1,0:T(8,128)(2,1)} %bitcast.113), custom_call_target="tpu_custom_call" | custom-call | tf_op jit(solution)/shard_map/pallas_call | solution.py:157
  105.0 1.0 copy.111
  109.1 1.3 stack.77.rv
  111.1 53.3 %all-gather.3.cloned.1.call-done.w_in = bf16[2,768,2304]{2,1,0:T(8,128)(2,1)} async-done(((bf16[2,24,2304]{2,1,0:T(8,128)(2,1)}), bf16[2,768,2304]{2,1,0:T(8,128)(2,1)}) %all-gather.3.cloned.1.call-update) | async-done | bytes 7077904 | tf_op jit(solution)/shard_map/all_gather | solution.py:1477
  164.4 97.7 %middle.1 = (bf16[24,16384]{1,0:T(8,128)(2,1)}, bf16[32,24,128]{2,1,0:T(8,128)(2,1)}, bf16[24,256]{1,0:T(8,128)(2,1)}, bf16[32,16,768]{2,1,0:T(8,128)(2,1)}, bf1...) custom-call(bf16[32,24,768]{2,1,0:T(8,128)(2,1)} %get-tuple-element., ...), custom_call_target="tpu_custom_call" | custom-call | tf_op jit(solution)/shard_map/middle/pallas_call | solution.py:962
  262.2 2.1 convert_reduce_fusion.2
  264.2 1.1 convert_reduce_fusion
  265.3 1.3 convert_reduce_fusion.5
  267.4 1.0 slice_bitcast_fusion
  269.1 1.0 fusion.40
  270.3 1.8 fusion.41
  272.1 1.5 fusion.42
  273.6 0.8 convolution_bitcast_fusion.7
  276.6 1.2 slice.369
  282.5 0.9 dynamic-slice_convert_fusion
  283.4 0.9 convolution_bitcast_fusion.1
  284.3 0.9 convolution_bitcast_fusion
  285.3 2.1 copy.147
  287.3 1.6 reshape.264
  288.9 1.2 copy.144
  292.7 1.3 copy.146
  294.0 1.2 reshape_reshape.7
  295.2 1.2 convolution_bitcast_fusion.2
  303.5 22.9 %table_sums.1 = f32[24,18432]{1,0:T(8,128)} custom-call(bf16[24,16384]{1,0:T(8,128)(2,1)} %get-tuple-element.70.values_ref, s32[16,1,1024]{2,1,0:T(1,128)} %bitcast.118), custom_call_target="tpu_custom_call" | custom-call | tf_op jit(solution)/shard_map/table_sums/pallas_call | solution.py:276
  326.5 1.0 slice_add_fusion
  327.5 1.6 scatter-add.9
  329.1 2.6 multiply_reduce_fusion
  331.7 1.9 multiply_reduce_fusion.1
  342.7 16.7 %shard_map.427 = f32[32,8,128]{2,1,0:T(8,128)} custom-call(f32[8,128]{1,0:T(8,128)} %broadcast_in_dim.6.refs_0_), custom_call_target="tpu_custom_call" | custom-call | tf_op jit(solution)/shard_map/pallas_call | solution.py:157
  359.4 1.5 slice_reduce_fusion.1
  364.2 1.2 slice.296
  365.4 3.0 multiply_subtract_fusion
  368.6 1.5 multiply_subtract_fusion.1
  371.0 1.3 multiply_subtract_fusion.2
  372.2 0.9 copy-done
  373.1 3.3 add_subtract_fusion
  (245 shorter events, 35.3 us)
Async XLA Ops:
  7.2 30.6 %copy-start.1 = (f32[18384,24]{0,1:T(8,128)S(1)}, f32[18384,24]{0,1:T(8,128)}, u32[]{:S(2)}) copy-start(f32[18384,24]{0,1:T(8,128)} %param.36) | copy-start | bytes 5294596
  7.2 103.9 %all-gather.5.cloned.1.call-start = ((), (), s32[]{:S(2)}) async-start(), calls=%async_computation.1 | async-start | bytes 2433024 | tf_op jit(solution)/shard_map/all_gather | solution.py:1478
  8.9 155.4 %all-gather.3.cloned.1.call-start = ((), (), s32[]{:S(2)}) async-start(), calls=%async_computation | async-start | bytes 7299072 | tf_op jit(solution)/shard_map/all_gather | solution.py:1477
  63.9 43.0 %copy-start.7 = (f32[2,96,768]{2,1,0:T(8,128)S(1)}, f32[2,96,768]{2,1,0:T(8,128)}, u32[]{:S(2)}) copy-start(f32[2,96,768]{2,1,0:T(8,128)} %param.40) | copy-start | bytes 1769476
  262.1 7.0 %copy-start.17 = (bf16[32,16,768]{2,1,0:T(8,128)(2,1)S(1)}, bf16[32,16,768]{2,1,0:T(8,128)(2,1)}, u32[]{:S(2)}) copy-start(bf16[32,16,768]{2,1,0:T(8,128)(2,1)} %get-tuple-element.74) | copy-start | bytes 2359300
  262.2 7.9 %copy-start.33 = (bf16[32,24,128]{2,1,0:T(8,128)(2,1)S(1)}, bf16[32,24,128]{2,1,0:T(8,128)(2,1)}, u32[]{:S(2)}) copy-start(bf16[32,24,128]{2,1,0:T(8,128)(2,1)} %get-tuple-element.73) | copy-start | bytes 589828
  270.1 3.5 copy-start.38
  270.1 3.5 copy-start.42
  270.3 5.6 %copy-start.43 = (bf16[24,256]{1,0:T(8,128)(2,1)S(1)}, bf16[24,256]{1,0:T(8,128)(2,1)}, u32[]{:S(2)}) copy-start(bf16[24,256]{1,0:T(8,128)(2,1)} %get-tuple-element.71) | copy-start | bytes 36868
  270.3 6.3 %copy-start.2 = (bf16[24,16384]{1,0:T(8,128)(2,1)S(1)}, bf16[24,16384]{1,0:T(8,128)(2,1)}, u32[]{:S(2)}) copy-start(bf16[24,16384]{1,0:T(8,128)(2,1)} %get-tuple-element.70.values_ref) | copy-start | bytes 2359300
  273.6 5.5 %copy-start.51 = (f32[8,768]{1,0:T(8,128)S(1)}, f32[8,768]{1,0:T(8,128)}, u32[]{:S(2)}) copy-start(f32[8,768]{1,0:T(8,128)} %get-tuple-element.78) | copy-start | bytes 73732
  273.6 6.8 %copy-start.46 = (f32[8448]{0:T(1024)S(1)}, f32[8448]{0:T(1024)}, u32[]{:S(2)}) copy-start(f32[8448]{0:T(1024)} %custom-call) | copy-start | bytes 101380
  273.6 6.8 %copy-start.48 = (f32[768]{0:T(1024)S(1)}, f32[768]{0:T(1024)}, u32[]{:S(2)}) copy-start(f32[768]{0:T(1024)} %get-tuple-element.149) | copy-start | bytes 9220
  273.6 6.8 %copy-start.47 = (f32[768]{0:T(1024)S(1)}, f32[768]{0:T(1024)}, u32[]{:S(2)}) copy-start(f32[768]{0:T(1024)} %get-tuple-element.148) | copy-start | bytes 9220
  273.6 6.9 %copy-start.45 = (f32[8448]{0:T(1024)S(1)}, f32[8448]{0:T(1024)}, u32[]{:S(2)}) copy-start(f32[8448]{0:T(1024)} %custom-call.1) | copy-start | bytes 101380
  273.6 6.9 %copy-start.50 = (f32[768]{0:T(1024)S(1)}, f32[768]{0:T(1024)}, u32[]{:S(2)}) copy-start(f32[768]{0:T(1024)} %get-tuple-element.151) | copy-start | bytes 9220
  273.6 6.9 %copy-start.49 = (f32[768]{0:T(1024)S(1)}, f32[768]{0:T(1024)}, u32[]{:S(2)}) copy-start(f32[768]{0:T(1024)} %get-tuple-element.150) | copy-start | bytes 9220
  275.9 5.9 %slice-start = ((bf16[48,32,96]{2,0,1:T(8,128)(2,1)}), bf16[40,32,96]{2,0,1:T(8,128)(2,1)S(1)}, s32[]{:S(2)}) async-start(bf16[48,32,96]{2,0,1:T(8,128)(2,1)} %copy-done.4), calls=%async_computation.2 | async-start | bytes 655360 | tf_op jit(solution)/shard_map/slice | solution.py:1539
  276.6 5.7 %slice-start.1 = ((bf16[48,32,96]{2,0,1:T(8,128)(2,1)}), bf16[8,32,96]{2,0,1:T(8,128)(2,1)S(1)}, s32[]{:S(2)}) async-start(bf16[48,32,96]{2,0,1:T(8,128)(2,1)} %copy-done.4), calls=%async_computation.3 | async-start | bytes 131072 | tf_op jit(solution)/shard_map/slice | solution.py:1539
  278.4 10.5 %copy-start.16 = (bf16[32,2,1,24]{2,1,3,0:T(2,128)(2,1)S(1)}, bf16[32,2,1,24]{2,1,3,0:T(2,128)(2,1)}, u32[]{:S(2)}) copy-start(bf16[32,2,1,24]{2,1,3,0:T(2,128)(2,1)} %get-tuple-element.192) | copy-start | bytes 9220
  281.9 8.9 %copy-start.15 = (bf16[32,2,12,24]{2,1,3,0:T(2,128)(2,1)S(1)}, bf16[32,2,12,24]{2,1,3,0:T(2,128)(2,1)}, u32[]{:S(2)}) copy-start(bf16[32,2,12,24]{2,1,3,0:T(2,128)(2,1)} %get-tuple-element.193) | copy-start | bytes 110596
  284.3 8.3 %copy-start.14 = (bf16[32,2,12,24]{2,1,3,0:T(2,128)(2,1)S(1)}, bf16[32,2,12,24]{2,1,3,0:T(2,128)(2,1)}, u32[]{:S(2)}) copy-start(bf16[32,2,12,24]{2,1,3,0:T(2,128)(2,1)} %get-tuple-element.194) | copy-start | bytes 110596
  291.9 7.9 %copy-start.44 = (bf16[8,768]{1,0:T(8,128)(2,1)S(1)}, bf16[8,768]{1,0:T(8,128)(2,1)}, u32[]{:S(2)}) copy-start(bf16[8,768]{1,0:T(8,128)(2,1)} %get-tuple-element.196) | copy-start | bytes 36868
  294.0 7.7 %copy-start.3 = (f32[24,15360]{1,0:T(8,128)S(1)}, f32[24,15360]{1,0:T(8,128)}, u32[]{:S(2)}) copy-start(f32[24,15360]{1,0:T(8,128)} %slice.369) | copy-start | bytes 4423684
  326.4 7.2 %copy-start.53 = (f32[1,768]{1,0:T(1,128)S(1)}, f32[1,768]{1,0:T(1,128)}, u32[]{:S(2)}) copy-start(f32[1,768]{1,0:T(1,128)} %get-tuple-element.215) | copy-start | bytes 9220
  326.4 7.2 %copy-start.54 = (f32[1,768]{1,0:T(1,128)S(1)}, f32[1,768]{1,0:T(1,128)}, u32[]{:S(2)}) copy-start(f32[1,768]{1,0:T(1,128)} %get-tuple-element.216) | copy-start | bytes 9220
  326.4 7.2 %copy-start.55 = (f32[1,768]{1,0:T(1,128)S(1)}, f32[1,768]{1,0:T(1,128)}, u32[]{:S(2)}) copy-start(f32[1,768]{1,0:T(1,128)} %get-tuple-element.213) | copy-start | bytes 9220
  326.4 7.2 %copy-start.56 = (f32[1,768]{1,0:T(1,128)S(1)}, f32[1,768]{1,0:T(1,128)}, u32[]{:S(2)}) copy-start(f32[1,768]{1,0:T(1,128)} %get-tuple-element.214) | copy-start | bytes 9220
  326.4 7.2 %copy-start.57 = (f32[1,768]{1,0:T(1,128)S(1)}, f32[1,768]{1,0:T(1,128)}, u32[]{:S(2)}) copy-start(f32[1,768]{1,0:T(1,128)} %get-tuple-element.211) | copy-start | bytes 9220
  326.4 7.2 %copy-start.58 = (f32[1,768]{1,0:T(1,128)S(1)}, f32[1,768]{1,0:T(1,128)}, u32[]{:S(2)}) copy-start(f32[1,768]{1,0:T(1,128)} %get-tuple-element.212) | copy-start | bytes 9220
  326.4 7.9 %copy-start.5 = (f32[1,24,3072]{2,1,0:T(8,128)S(1)}, f32[1,24,3072]{2,1,0:T(8,128)}, u32[]{:S(2)}) copy-start(f32[1,24,3072]{2,1,0:T(8,128)} %convolution_bitcast_fusion.1) | copy-start | bytes 884740
  326.4 7.9 %copy-start.6 = (f32[1,24,3072]{2,1,0:T(8,128)S(1)}, f32[1,24,3072]{2,1,0:T(8,128)}, u32[]{:S(2)}) copy-start(f32[1,24,3072]{2,1,0:T(8,128)} %convolution_bitcast_fusion) | copy-start | bytes 884740
  326.4 8.6 %copy-start.26 = (bf16[64,768]{1,0:T(8,128)(2,1)S(1)}, bf16[64,768]{1,0:T(8,128)(2,1)}, u32[]{:S(2)}) copy-start(bf16[64,768]{1,0:T(8,128)(2,1)} %reshape.264) | copy-start | bytes 294916
  326.5 8.6 %copy-start.40 = (bf16[32,2,1,24]{3,1,0,2:T(2,128)(2,1)S(1)}, bf16[32,2,1,24]{3,1,0,2:T(2,128)(2,1)}, u32[]{:S(2)}) copy-start(bf16[32,2,1,24]{3,1,0,2:T(2,128)(2,1)} %copy.147) | copy-start | bytes 9220
  326.5 8.8 %copy-start.18 = (f32[1,24,768]{2,1,0:T(8,128)S(1)}, f32[1,24,768]{2,1,0:T(8,128)}, u32[]{:S(2)}) copy-start(f32[1,24,768]{2,1,0:T(8,128)} %convolution_bitcast_fusion.7) | copy-start | bytes 221188
  326.5 9.4 %copy-start.27 = (bf16[64,768]{1,0:T(8,128)(2,1)S(1)}, bf16[64,768]{1,0:T(8,128)(2,1)}, u32[]{:S(2)}) copy-start(bf16[64,768]{1,0:T(8,128)(2,1)} %reshape.259) | copy-start | bytes 294916
  326.5 9.4 %copy-start.41 = (bf16[32,2,1,24]{3,1,0,2:T(2,128)(2,1)S(1)}, bf16[32,2,1,24]{3,1,0,2:T(2,128)(2,1)}, u32[]{:S(2)}) copy-start(bf16[32,2,1,24]{3,1,0,2:T(2,128)(2,1)} %copy.144) | copy-start | bytes 9220
  329.0 7.0 %copy-start.28 = (f32[24,768]{1,0:T(8,128)S(1)}, f32[24,768]{1,0:T(8,128)}, u32[]{:S(2)}) copy-start(f32[24,768]{1,0:T(8,128)} %fusion.15) | copy-start | bytes 221188
  329.0 7.0 %copy-start.29 = (f32[24,768]{1,0:T(8,128)S(1)}, f32[24,768]{1,0:T(8,128)}, u32[]{:S(2)}) copy-start(f32[24,768]{1,0:T(8,128)} %reshape.261) | copy-start | bytes 221188
  329.0 7.0 %copy-start.30 = (f32[24,768]{1,0:T(8,128)S(1)}, f32[24,768]{1,0:T(8,128)}, u32[]{:S(2)}) copy-start(f32[24,768]{1,0:T(8,128)} %reshape.263) | copy-start | bytes 221188
  329.1 7.0 %copy-start.31 = (f32[24,768]{1,0:T(8,128)S(1)}, f32[24,768]{1,0:T(8,128)}, u32[]{:S(2)}) copy-start(f32[24,768]{1,0:T(8,128)} %reshape.254) | copy-start | bytes 221188
  329.1 7.0 %copy-start.32 = (f32[24,768]{1,0:T(8,128)S(1)}, f32[24,768]{1,0:T(8,128)}, u32[]{:S(2)}) copy-start(f32[24,768]{1,0:T(8,128)} %reshape.257) | copy-start | bytes 221188
  331.7 9.1 %copy-start.36 = (f32[1,8448]{1,0:T(1,128)S(1)}, f32[1,8448]{1,0:T(1,128)}, u32[]{:S(2)}) copy-start(f32[1,8448]{1,0:T(1,128)} %stack.97) | copy-start | bytes 101380
  331.7 9.1 %copy-start.37 = (f32[1,8448]{1,0:T(1,128)S(1)}, f32[1,8448]{1,0:T(1,128)}, u32[]{:S(2)}) copy-start(f32[1,8448]{1,0:T(1,128)} %stack.98) | copy-start | bytes 101380
  331.7 33.7 %copy-start.8 = (f32[2,96,768]{2,1,0:T(8,128)S(1)}, f32[2,96,768]{2,1,0:T(8,128)}, u32[]{:S(2)}) copy-start(f32[2,96,768]{2,1,0:T(8,128)} %param.40) | copy-start | bytes 1769476
  368.5 3.7 copy-start.12
  373.1 3.3 copy-start.60
  373.1 3.3 copy-start.61
  (19 other events, 39.8 us)
Sparse Core Ops, SparseCore 0:
  11.5 61.2 all-gather.4
  76.3 88.0 all-gather.2
where the time goes:
time: 387 us; the launch traced here: 385 us
  Pallas kernels  218 us (56%)
  waiting for transfers between devices  53.4 us (14%)
  local copies, waits for them, and re-layouts  47.5 us (12%)
  other arithmetic  38.2 us (10%)
  between operations  22.1 us (6%)
  matrix products  5.73 us (1%)
    pallas_call x1, Pallas kernels, middle(): pl.pallas_call(functools.partial(middle_body, n_valid, nq, nd, narrow, co...  97.7 us
    pallas_call x3, Pallas kernels, comm(): pl.pallas_call(functools.partial(comm_body, sends, len(arrays), len(out_s...  74.3 us
    all_gather x1, waiting for transfers between devices, on_device(): w_in = lax.all_gather(attend_in.astype(BF16), AXES, axis=1, tiled=True)  53.3 us
    pallas_call x1, Pallas kernels, table_rows(): pl.pallas_call(functools.partial(gather_body, rows, blocks), grid=(tokens...  23 us
    pallas_call x1, Pallas kernels, table_sums(): pl.pallas_call(functools.partial(scatter_body, rows, blocks), grid=(token...  22.9 us
    sub x7, other arithmetic, adam_update(): weight - rate * (first_hat / (jnp.sqrt(second_hat) + ADAM_EPS) + WEIGHT_D...  11.3 us
    unnamed x147, local copies, waits for them, and re-layouts  9.45 us
    reduce_sum x7, other arithmetic, on_device(): local_squares = sum((jnp.sum(g * g) for g in grads))  7.94 us
  transfers between devices with their start and end apart: 2, of which 1 were waited for; matrix products, arithmetic and copies ran while one was open for 5% of the time, Pallas kernels for 21%

commit v1 on v0

--- a/solution.py
+++ b/solution.py
@@ -500,7 +500,7 @@
         return (lane >> 5) == (row & (self.count - 1))
 
 
-def unit_front(unit, emb, e, w_in, w_out, cv, rv, keep):
+def unit_front(unit, emb, e, w, cv, rv, keep):
     center = emb - jnp.mean(emb, axis=0, keepdims=True)
     spread = jnp.mean(center * center, axis=0, keepdims=True)
     scale = lax.rsqrt(spread + NORM_EPS)
@@ -510,9 +510,9 @@
     pick = unit.pick()
     x_first = mm(as_bf16(pick), x_low, NT).astype(BF16)
     x0_first = mm(pick.astype(F32), x0, NT, HIGH)
-    q = (mm(x_first, w_in[e, :, 0:D], NN) + rv[8 * e : 8 * e + 1, :]).astype(BF16)
-    k = mm(w_in[e, :, D : 2 * D], x_low, TN).astype(BF16)
-    v = (mm(w_in[e, :, 2 * D : 3 * D], x_low, TN) + cv[:, 3 * e + 2 : 3 * e + 3]).astype(BF16)
+    q = (mm(x_first, w[:, 0:D], NN) + rv[8 * e : 8 * e + 1, :]).astype(BF16)
+    k = mm(w[:, D : 2 * D], x_low, TN).astype(BF16)
+    v = (mm(w[:, 2 * D : 3 * D], x_low, TN) + cv[:, 3 * e + 2 : 3 * e + 3]).astype(BF16)
     heads = unit.heads()
     q_heads = (mm(unit.spread(), q, NN) * heads).astype(BF16)
     s = mm(q_heads, k, NN) * 0.125
@@ -523,18 +523,18 @@
     p = ex / jnp.sum(ex, axis=1, keepdims=True)
     mixed = (mm(p.astype(BF16), v, NT) * heads).astype(BF16)
     a = mm(unit.collect(), mixed, NN).astype(BF16)
-    o = mm(a, w_out[e], NN) + rv[8 * e + 1 : 8 * e + 2, :]
+    o = mm(a, w[:, 3 * D : 4 * D], NN) + rv[8 * e + 1 : 8 * e + 2, :]
     keep(hat, scale, x_low, x_first, q, k, v, p, a)
     return x0_first + o
 
 
-def unit_back(unit, row_grad, e, w_in, w_out, cv, kept):
+def unit_back(unit, row_grad, e, w, cv, kept):
     hat, scale, x_low, x_first, q, k, v, p, a = kept
     heads = unit.heads()
     spread, collect = unit.spread(), unit.collect()
     p_low = p.astype(BF16)
     do = row_grad.astype(BF16)
-    da = mm(do, w_out[e], NT).astype(BF16)
+    da = mm(do, w[:, 3 * D : 4 * D], NT).astype(BF16)
     q_heads = (mm(spread, q, NN) * heads).astype(BF16)
     da_heads = (mm(spread, da, NN) * heads).astype(BF16)
     dp = mm(da_heads, v, NN)
@@ -542,10 +542,10 @@
     dq_heads = (mm(ds, k, NT) * heads * 0.125).astype(BF16)
     dq = mm(collect, dq_heads, NN).astype(BF16)
     t = mm(ds, x_low, NT) * 0.125
-    w = mm(p_low, x_low, NT)
-    gk = (mm(q_heads, w_in[e, :, D : 2 * D], NT) * 0.125).astype(BF16)
-    ev = mm(da_heads, w_in[e, :, 2 * D : 3 * D], NT).astype(BF16)
-    first = row_grad + mm(dq, w_in[e, :, 0:D], NT)
+    wx = mm(p_low, x_low, NT)
+    gk = (mm(q_heads, w[:, D : 2 * D], NT) * 0.125).astype(BF16)
+    ev = mm(da_heads, w[:, 2 * D : 3 * D], NT).astype(BF16)
+    first = row_grad + mm(dq, w[:, 0:D], NT)
     gx = mm(gk, ds, TN) + mm(ev, p_low, TN)
     gx = gx + mm(first, unit.pick().astype(F32), TN, HIGH)
     p_sum = jnp.sum(p_low.astype(F32), axis=1, keepdims=True)
@@ -556,7 +556,7 @@
     mean_one = jnp.mean(scaled, axis=0, keepdims=True)
     mean_two = jnp.mean(scaled * hat, axis=0, keepdims=True)
     g_emb = scale * (scaled - mean_one - hat * mean_two)
-    return g_emb, t, w, da, dq, do, dbv, g_gain, g_shift
+    return g_emb, t, wx, da, dq, do, dbv, g_gain, g_shift
 
 
 def load_rows(ref, count):
@@ -572,7 +572,7 @@
 
 def middle_body(
     n_valid, nq, nd, narrow, cols, query_home, token_total,
-    mine, mine_q, pos, w_in, w_out, w_up, w_down, cv, rv, b_in, slots,
+    mine, mine_q, w_one, w_zero, w_up, w_down, cv, rv, b_in, slots,
     o_tok, o_fac, o_facq, o_line, o_lineq, o_du, o_shrink, o_h, o_rows, o_loss,
     hat_s, scale_s, xl_s, xf_s, q_s, k_s, v_s, p_s, a_s,
     hat_q, scale_q, xl_q, xf_q, q_q, k_q, v_q, p_q, a_q,
@@ -600,13 +600,13 @@
 
     def front(c, carry):
         at = pl.ds(pl.multiple_of(c * LP, LANE), LP)
-        emb = (mine[:, :, at].astype(F32) + pos[...].astype(F32)).reshape(D, LP)
+        emb = mine[:, :, at].astype(F32).reshape(D, LP) + w_one[:, 4 * D :].astype(F32)
 
         def keep(hat, scale, x_low, x_first, q, k, v, p, a):
             hat_s[c], scale_s[c], xl_s[c], xf_s[c] = hat, scale, x_low, x_first
             q_s[c], k_s[c], v_s[c], p_s[c], a_s[c] = q, k, v, p, a
 
-        r1 = unit_front(passage, emb, 1, w_in, w_out, cv, rv, keep)
+        r1 = unit_front(passage, emb, 1, w_one, cv, rv, keep)
         for j in range(D // LANE):
             r1_own[c, j : j + 1, :] = r1[0:1, j * LANE : (j + 1) * LANE]
         return carry
@@ -615,14 +615,14 @@
 
     @pl.when(me == query_home)
     def _():
-        parts = pos[:, :, 0:LANE].astype(F32).reshape(D, LANE)[:, 0:LQ]
+        parts = w_one[:, 4 * D : 4 * D + LANE].astype(F32)[:, 0:LQ]
         emb = mine_q[...].astype(F32).reshape(D, nq * LQ) + jnp.concatenate([parts] * nq, axis=1)
 
         def keep(hat, scale, x_low, x_first, q, k, v, p, a):
             hat_q[...], scale_q[...], xl_q[...], xf_q[...] = hat, scale, x_low, x_first
             q_q[...], k_q[...], v_q[...], p_q[...], a_q[...] = q, k, v, p, a
 
-        store_rows(r1_ownq, unit_front(queries, emb, 0, w_in, w_out, cv, rv, keep))
+        store_rows(r1_ownq, unit_front(queries, emb, 0, w_zero, cv, rv, keep))
 
     flows = [
         Flow(
@@ -823,7 +823,7 @@
             hat_s[c], scale_s[c], xl_s[c], xf_s[c], q_s[c], k_s[c], v_s[c], p_s[c], a_s[c]
         )
         g_emb, t, w, da, dq, do, dbv, g_gain, g_shift = unit_back(
-            passage, row_grad, 1, w_in, w_out, cv, kept
+            passage, row_grad, 1, w_one, cv, kept
         )
         gtok[c] = g_emb.reshape(nd, cols, LP).astype(BF16)
         tw = jnp.concatenate([t, w, xf_s[c].astype(F32), a_s[c].astype(F32)], axis=0)
@@ -864,7 +864,7 @@
             p_q[...], a_q[...],
         )
         g_emb, t, w, da, dq, do, dbv, g_gain, g_shift = unit_back(
-            queries, g_mid, 0, w_in, w_out, cv, kept
+            queries, g_mid, 0, w_zero, cv, kept
         )
         gtok_q[...] = g_emb.reshape(nd, cols, nq * LQ).astype(BF16)
         tw = jnp.concatenate([t, w, xf_q[...].astype(F32), a_q[...].astype(F32)], axis=0)
@@ -1015,6 +1015,260 @@
     )(*arrays)
 
 
+def stack_table(rows, blocks, table, stacked):
+    last = (V - (blocks - 1) * HASH + LANE - 1) // LANE * LANE
+
+    def piece(b):
+        if b >= blocks:
+            return []
+        if b == blocks - 1:
+            part = table[:, b * HASH : b * HASH + last].astype(F32)
+            return [jnp.concatenate([part, jnp.zeros((rows, HASH - last), F32)], axis=1)]
+        return [table[:, b * HASH : (b + 1) * HASH].astype(F32)]
+
+    for b in range(0, blocks, 2):
+        both = jnp.concatenate(piece(b) + piece(b + 1), axis=0)
+        stacked[b * rows : b * rows + both.shape[0], :] = both.astype(BF16)
+
+
+def pick_tokens(rows, blocks, stacked, ids):
+    low = ids & (HASH - 1)
+    high = ids >> (HASH.bit_length() - 1)
+    width = ids.shape[1]
+    hot = as_bf16(iota((HASH, width), 0) == low)
+    picked = jnp.dot(stacked[...], hot, preferred_element_type=F32)
+    value = jnp.zeros((rows, width), F32)
+    for b in range(blocks):
+        value = jnp.where(high == b, picked[b * rows : (b + 1) * rows], value)
+    return value.astype(BF16)
+
+
+def first_body(
+    n_valid, nq, nd, narrow, cols, home_at, blocks, forward_from,
+    ids_mine, small_mine, table, win, wout, pos_mine, up_mine,
+    ids_got, small_got, mine, mine_q, wall, w0, up_got,
+    stacked, tokens, tokens_q, p0,
+    send_sem, recv_sem, own_sem, wide_send, wide_recv, x_send, x_recv, c_send, c_recv,
+):
+    cap = -(-n_valid // nd)
+    wide = nd // narrow
+    tq = nq * LQ
+    n_own = ids_mine.shape[0] - 1
+    net = Net(nd, narrow, send_sem, recv_sem, own_sem)
+    me = net.me
+    w_at, n_at = lax.axis_index("wide"), lax.axis_index("narrow")
+    x_at, c_at = n_at ^ 2, n_at ^ 1
+    everyone = (0, nd)
+    home = (home_at, home_at + 1)
+
+    wall[w_at, n_at] = jnp.concatenate([win[1], wout[1], pos_mine[...]], axis=1).astype(BF16)
+    p0[...] = jnp.concatenate([win[0], wout[0]], axis=1).astype(BF16)
+
+    net.barrier()
+    small = [
+        Flow(
+            lambda s, t: ids_mine, lambda s, t: ids_got.at[s],
+            lambda n: ids_got.at[pl.ds(0, n)], everyone, everyone,
+        ),
+        Flow(
+            lambda s, t: small_mine, lambda s, t: small_got.at[s],
+            lambda n: small_got.at[pl.ds(0, n)], everyone, everyone,
+        ),
+    ]
+    small_base = net.start(small)
+
+    def wide_copy(k, carry):
+        t = lax.rem(w_at + k, wide)
+        pltpu.make_async_remote_copy(
+            src_ref=wall.at[w_at, n_at], dst_ref=wall.at[w_at, n_at],
+            send_sem=wide_send, recv_sem=wide_recv.at[w_at],
+            device_id=(t, n_at), device_id_type=MESH,
+        ).start()
+        return carry
+
+    lax.fori_loop(1, wide, wide_copy, 0)
+
+    def to_x(row):
+        return pltpu.make_async_remote_copy(
+            src_ref=wall.at[row, n_at], dst_ref=wall.at[row, n_at],
+            send_sem=x_send, recv_sem=x_recv.at[row],
+            device_id=(w_at, x_at), device_id_type=MESH,
+        )
+
+    def to_core(row, col, which):
+        return pltpu.make_async_remote_copy(
+            src_ref=wall.at[row, col], dst_ref=wall.at[row, col],
+            send_sem=c_send, recv_sem=c_recv.at[which, row],
+            device_id=(w_at, c_at), device_id_type=MESH,
+        )
+
+    def forward(k):
+        row = lax.rem(w_at - k + wide, wide)
+
+        @pl.when(k > 0)
+        def _():
+            pltpu.make_async_copy(
+                wall.at[row, n_at], wall.at[row, n_at], wide_recv.at[row]
+            ).wait()
+
+        to_x(row).start()
+        to_core(row, n_at, 0).start()
+
+    stack_table(cols, blocks, table, stacked)
+    net.finish(small, small_base)
+
+    pairs = n_valid // n_own
+    moves = [
+        Flow(
+            lambda s, t, c=c: tokens.at[(c * nd + t) // n_own, lax.rem(c * nd + t, n_own)],
+            lambda s, t, c=c: mine.at[s, :, pl.ds(c * LP, LP)],
+            lambda n: mine.at[pl.ds(0, n), :, pl.ds(0, LP)],
+            everyone, (0, min(nd, n_valid - c * nd)),
+        )
+        for c in range(cap)
+    ]
+    base = net.used
+    net.used += cap
+
+    def send_pair(at):
+        for j in range(n_own):
+            slot = at * n_own + j
+            c = slot // nd
+            t = lax.rem(slot, nd)
+            dst = mine.at[me, :, pl.ds(pl.multiple_of(c * LP, LANE), LP)]
+
+            @pl.when(t != me)
+            def _():
+                pltpu.make_async_remote_copy(
+                    src_ref=tokens.at[at, j], dst_ref=dst,
+                    send_sem=send_sem.at[base + c], recv_sem=recv_sem.at[base + c],
+                    device_id=net.where(t), device_id_type=MESH,
+                ).start()
+
+            @pl.when(t == me)
+            def _():
+                pltpu.make_async_copy(tokens.at[at, j], dst, own_sem.at[base + c]).start()
+
+    def gather(i, carry):
+        at = lax.rem(i + me, pairs)
+        ids = jnp.concatenate([ids_got[at, j : j + 1, 0:LP] for j in range(n_own)], axis=1)
+        rows = pick_tokens(cols, blocks, stacked, ids)
+        for j in range(n_own):
+            tokens[at, j] = rows[:, j * LP : (j + 1) * LP]
+
+        @pl.when(i > 0)
+        def _():
+            send_pair(lax.rem(i - 1 + me, pairs))
+
+        @pl.when(jnp.logical_and(i >= forward_from, i < forward_from + wide))
+        def _():
+            forward(i - forward_from)
+
+        return carry
+
+    q_ids = jnp.zeros((1, tq), jnp.int32)
+    for d in range(0, nd, narrow):
+        q_ids = q_ids + ids_got[d, n_own : n_own + 1, 0:tq]
+    tokens_q[...] = pick_tokens(cols, blocks, stacked, q_ids)
+    q_moves = [
+        Flow(
+            lambda s, t: tokens_q, lambda s, t: mine_q.at[s],
+            lambda n: mine_q.at[pl.ds(0, n)], everyone, home,
+        ),
+    ]
+    home_moves = [
+        Flow(
+            lambda s, t: p0, lambda s, t: w0.at[s],
+            lambda n: w0.at[pl.ds(0, n)], everyone, home,
+        ),
+    ]
+    q_base = net.start(q_moves)
+    home_base = net.start(home_moves)
+    lax.fori_loop(0, pairs, gather, 0)
+    send_pair(lax.rem(pairs - 1 + me, pairs))
+    up_moves = [
+        Flow(
+            lambda s, t: up_mine.at[t], lambda s, t: up_got.at[s],
+            lambda n: up_got.at[pl.ds(0, n)], everyone, everyone,
+        )
+    ]
+    up_base = net.start(up_moves)
+    for k in range(wide):
+        if forward_from + k >= pairs:
+            forward(k)
+
+    def second(k, carry):
+        row = lax.rem(w_at - k + wide, wide)
+        pltpu.make_async_copy(wall.at[row, x_at], wall.at[row, x_at], x_recv.at[row]).wait()
+        to_core(row, x_at, 1).start()
+        return carry
+
+    lax.fori_loop(0, wide, second, 0)
+    net.finish(moves, base)
+    net.finish(q_moves, q_base)
+    net.finish(up_moves, up_base)
+    net.finish(home_moves, home_base)
+
+    def last(row, carry):
+        for which, col in ((0, c_at), (1, c_at ^ 2)):
+            pltpu.make_async_copy(
+                wall.at[row, col], wall.at[row, col], c_recv.at[which, row]
+            ).wait()
+        return carry
+
+    lax.fori_loop(0, wide, last, 0)
+    many = wall.at[pl.ds(0, wide - 1), 0]
+    pltpu.make_async_copy(many, many, wide_send).wait()
+    many = wall.at[:, 0]
+    pltpu.make_async_copy(many, many, x_send).wait()
+    many = wall.at[:, pl.ds(0, 2)]
+    pltpu.make_async_copy(many, many, c_send).wait()
+
+
+def first(n_valid, nq, nd, narrow, cols, home_at, arrays, forward_from):
+    cap = -(-n_valid // nd)
+    wide = nd // narrow
+    tq = nq * LQ
+    ids_mine, small_mine, up_mine = arrays[0], arrays[1], arrays[6]
+    n_own = ids_mine.shape[0] - 1
+    blocks = -(-V // HASH)
+    vmem = pl.BlockSpec(memory_space=pltpu.VMEM)
+    flows = 5 + cap
+
+    def like(*shape, dtype=BF16):
+        return jax.ShapeDtypeStruct(shape, dtype)
+
+    dma = pltpu.SemaphoreType.DMA
+    return pl.pallas_call(
+        functools.partial(
+            first_body, n_valid, nq, nd, narrow, cols, home_at, blocks, forward_from
+        ),
+        out_shape=[
+            like(nd, *ids_mine.shape, dtype=jnp.int32),
+            like(nd, *small_mine.shape),
+            like(nd, cols, cap * LP),
+            like(nd, cols, tq),
+            like(wide, narrow, cols, 4 * D + LP),
+            like(nd, cols, 4 * D),
+            like(*up_mine.shape),
+        ],
+        in_specs=[vmem] * len(arrays),
+        out_specs=[vmem] * 7,
+        scratch_shapes=[
+            pltpu.VMEM((blocks * cols, HASH), BF16),
+            pltpu.VMEM((n_valid // n_own, n_own, cols, LP), BF16),
+            pltpu.VMEM((cols, tq), BF16),
+            pltpu.VMEM((cols, 4 * D), BF16),
+            dma((flows,)), dma((flows,)), dma((flows,)),
+            dma(()), dma((wide,)), dma(()), dma((wide,)), dma(()), dma((2, wide)),
+        ],
+        compiler_params=pltpu.CompilerParams(
+            collective_id=2, has_side_effects=True, vmem_limit_bytes=62 * 1024 * 1024
+        ),
+        name="first",
+    )(*arrays)
+
+
 def on_device_rows(
     passage_ids, query_ids, passage_query, kept_mask, neg_count, step_count,
     embed_table, attend_in, attend_out, expand_weight, shrink_weight, norm_gains, bias_terms,
@@ -1386,7 +1640,7 @@
     attend_out_first, attend_out_second, expand_first, expand_second,
     shrink_first, shrink_second, gains_first, gains_second, bias_first, bias_second,
 ):
-    if embed_table.shape[1] % 8 != 0:
+    if embed_table.shape[1] % 8 != 0 or lax.axis_size("narrow") != 4 or passage_ids.shape[0] != 2:
         return on_device_rows(
             passage_ids, query_ids, passage_query, kept_mask, neg_count, step_count,
             embed_table, attend_in, attend_out, expand_weight, shrink_weight, norm_gains,
@@ -1422,12 +1676,15 @@
         [widen(norm_gains.reshape(6, cols), small_width), widen(bias_terms, small_width)]
     ).astype(BF16)
     n_own = passage_ids.shape[0]
-    ids_got, small_got = exch(
-        1,
-        [ids_mine, small_mine],
-        [((nd, n_own + 1, ids_width), jnp.int32), ((nd, 8, small_width), BF16)],
-        [send_all(0, 0, nd), send_all(1, 1, nd)],
-    )
+    table_t = embed_table.T
+    up_mine = expand_weight.astype(BF16).reshape(2 * cols, nd, ff_cols).transpose(1, 0, 2)
+    ids_got, small_got, mine, mine_q, w_one, w_zero, w_up = first(
+        n_valid, nq, nd, narrow, cols, query_home,
+        [ids_mine, small_mine, table_t, attend_in, attend_out, table_t[:, V : V + LP], up_mine],
+        12,
+    )
+    w_one = w_one.reshape(D, 4 * D + LP)
+    w_zero = w_zero.reshape(D, 4 * D)
     pid = ids_got[:, :n_own, :LP].reshape(n_slots, LP)[:n_valid]
     qid = jnp.sum(ids_got[:, n_own, :tq], axis=0)
     q_from = n_valid * LP
@@ -1438,44 +1695,9 @@
 
     vocab = V + LP
     total = -(-vocab // HASH) * HASH
-    table_low = jnp.pad(embed_table.T.astype(BF16), ((0, 0), (0, total - vocab)))
-    got = table_rows(table_low, all_ids)
-    pos_mine = table_low[:, V : V + LP]
-    up_mine = expand_weight.astype(BF16).reshape(2 * cols, nd, ff_cols).transpose(1, 0, 2)
-
-    def passage_move(c):
-        return Send(
-            0, 0,
-            lambda ref, s, t: ref.at[:, pl.ds(pl.multiple_of((c * nd + t) * LP, LANE), LP)],
-            lambda ref, s, t: ref.at[s, :, pl.ds(c * LP, LP)],
-            lambda ref, n: ref.at[:, pl.ds(0, n * LP)],
-            lambda ref, n: ref.at[pl.ds(0, n), :, pl.ds(0, LP)],
-            (0, nd), (0, min(nd, n_valid - c * nd)),
-        )
-
-    query_move = Send(
-        0, 1,
-        lambda ref, s, t: ref.at[:, pl.ds(q_from, tq)],
-        lambda ref, s, t: ref.at[s],
-        lambda ref, n: ref.at[:, pl.ds(0, n * tq)],
-        lambda ref, n: ref.at[pl.ds(0, n)],
-        (0, nd), (query_home, query_home + 1),
-    )
-    mine, mine_q, pos, w_up = exch(
-        2,
-        [got, pos_mine, up_mine],
-        [
-            ((nd, cols, cap * LP), BF16), ((nd, cols, tq), BF16), ((nd, cols, LP), BF16),
-            ((nd, 2 * cols, ff_cols), BF16),
-        ],
-        [passage_move(c) for c in range(cap)]
-        + [query_move, send_all(1, 2, nd), send_blocks(2, 3, nd)],
-    )
     w_up = w_up.reshape(nd, 2, cols, ff_cols).transpose(1, 0, 2, 3).reshape(2, D, ff_cols)
     w_up = jnp.pad(w_up, ((0, 0), (0, 0), (0, LANE - ff_cols)))
     w_down = jnp.pad(shrink_weight.astype(BF16), ((0, 0), (0, LANE - ff_cols), (0, 0)))
-    w_in = lax.all_gather(attend_in.astype(BF16), AXES, axis=1, tiled=True)
-    w_out = lax.all_gather(attend_out.astype(BF16), AXES, axis=1, tiled=True)
     cv = jnp.stack(
         [v for e in range(2) for v in (
             gains[e, 0], bias[e, O_EMB : O_EMB + D], bias[e, O_V : O_V + D])]
@@ -1500,7 +1722,7 @@
     )
     tok, fac, fac_q, line, line_q, du_all, shrink_g, h_low, out_rows, loss = middle(
         n_valid, nq, nd, narrow, cols, query_home, token_total,
-        [mine, mine_q, pos, w_in, w_out, w_up, w_down, cv, rv, b_in, slots],
+        [mine, mine_q, w_one, w_zero, w_up, w_down, cv, rv, b_in, slots],
     )
     loss = loss[0, 0]
 

time: 387 us -> 316 us (0.82)
  waiting for transfers between devices: 53.4 us -> 0 us
  Pallas kernels: 218 us -> 236 us
  local copies, waits for them, and re-layouts: 47.5 us -> 31.9 us
  between operations: 22.1 us -> 8.58 us
    pallas_call x1, Pallas kernels: 23 us -> 84.5 us  [first(): pl.pallas_call(functools.partial(first_body, n_valid, nq, nd, narrow, col...]
    pallas_call x3 -> x1, Pallas kernels: 74.3 us -> 17 us  [comm(): pl.pallas_call(functools.partial(comm_body, sends, len(arrays), len(out_s...]
    all_gather x2 -> x0, waiting for transfers between devices: 53.3 us -> none  [the longest x1 53.3 us: on_device(): w_in = lax.all_gather(attend_in.astype(BF16), AXES, axis=1, tiled=True)]
    pallas_call x1, Pallas kernels: 97.7 us -> 112 us  [middle(): pl.pallas_call(functools.partial(middle_body, n_valid, nq, nd, narrow, co...]
    unnamed x147 -> x79, local copies, waits for them, and re-layouts: 9.45 us -> 6.94 us
  transfers between devices with their start and end apart: 2 -> 0, of which waited for: 1 -> 0; matrix products, arithmetic and copies ran while one was open for 5% -> 0% of each run, Pallas kernels for 21% -> 0%
where the time goes in v1:
time: 316 us; the launch traced here: 315 us
  Pallas kernels  236 us (75%)
  other arithmetic  35.5 us (11%)
  local copies, waits for them, and re-layouts  31.9 us (10%)
  between operations  8.58 us (3%)
    pallas_call x1, Pallas kernels, middle(): pl.pallas_call(functools.partial(middle_body, n_valid, nq, nd, narrow, co...  112 us
    pallas_call x1, Pallas kernels, first(): pl.pallas_call(functools.partial(first_body, n_valid, nq, nd, narrow, col...  84.5 us
    pallas_call x1, Pallas kernels, table_sums(): pl.pallas_call(functools.partial(scatter_body, rows, blocks), grid=(token...  22.9 us
    pallas_call x1, Pallas kernels, comm(): pl.pallas_call(functools.partial(comm_body, sends, len(arrays), len(out_s...  17 us
    sub x7, other arithmetic, adam_update(): weight - rate * (first_hat / (jnp.sqrt(second_hat) + ADAM_EPS) + WEIGHT_D...  9.88 us
    reduce_sum x7, other arithmetic, on_device(): local_squares = sum((jnp.sum(g * g) for g in grads))  8.49 us
    unnamed x79, local copies, waits for them, and re-layouts  6.94 us

profile of v1, /device:TPU:0, one launch (start us, length us, event | category | flops | bytes accessed | tf_op | source)
XLA Modules:
  0.0 314.9 jit_solution(2504572837150093816)
XLA Ops:
  2.0 0.8 fusion.28
  3.5 0.7 convert.16
  6.9 1.3 pad_add_fusion.1.ids_mine
  8.2 1.5 slice.344.pos_mine
  9.7 1.1 convert_element_type.74
  11.1 0.9 copy.172
  12.1 0.8 pad.42.w_down
  12.9 84.5 %first.1 = (s32[32,3,384]{2,1,0:T(4,128)}, bf16[32,8,384]{2,1,0:T(8,128)(2,1)}, bf16[32,24,768]{2,1,0:T(8,128)(2,1)}, bf16[32,24,256]{2,1,0:T(8,128)(2,1)}, bf16...) custom-call(s32[3,384]{1,0:T(4,128)} %pad_add_fusion.1.ids_mine, ...), custom_call_target="tpu_custom_call" | custom-call | tf_op jit(solution)/shard_map/first/pallas_call | solution.py:1242
  97.4 1.0 slice_reduce_fusion
  98.4 0.9 slice.294
  100.0 1.0 convert_bitcast_fusion.1
  101.0 0.9 convert_bitcast_fusion
  102.3 1.3 stack.77.rv
  104.3 0.9 copy.115.cv
  105.3 0.8 pad.41.w_up
  106.1 111.7 %middle.1 = (bf16[24,16384]{1,0:T(8,128)(2,1)}, bf16[32,24,128]{2,1,0:T(8,128)(2,1)}, bf16[24,256]{1,0:T(8,128)(2,1)}, bf16[32,16,768]{2,1,0:T(8,128)(2,1)}, bf1...) custom-call(bf16[32,24,768]{2,1,0:T(8,128)(2,1)} %get-tuple-element., ...), custom_call_target="tpu_custom_call" | custom-call | tf_op jit(solution)/shard_map/middle/pallas_call | solution.py:962
  217.8 1.9 multiply_reduce_fusion.1
  219.7 1.2 slice.293
  220.9 1.4 convert_reduce_fusion.2
  222.3 0.7 convert_reduce_fusion.5
  223.1 0.9 dynamic-slice_convert_fusion
  224.0 0.9 fusion.45
  224.9 1.0 slice_reduce_fusion.8
  226.0 0.7 slice.370
  226.8 1.1 convert_reduce_fusion
  229.5 0.8 fusion.15
  230.7 0.7 reshape.261
  231.7 0.7 reshape.258
  233.3 1.3 multiply_reduce_fusion.6
  235.7 0.8 multiply_reduce_fusion.2
  236.7 0.7 fusion.42
  238.4 0.7 reshape.265
  240.0 0.7 reshape.267
  240.8 0.9 fusion.41
  243.8 1.1 maximum_bitcast_fusion
  244.9 0.7 multiply_reduce_fusion.3
  247.2 22.9 %table_sums.1 = f32[24,18432]{1,0:T(8,128)} custom-call(bf16[24,16384]{1,0:T(8,128)(2,1)} %get-tuple-element.71.values_ref, s32[16,1,1024]{2,1,0:T(1,128)} %bitcast.122), custom_call_target="tpu_custom_call" | custom-call | tf_op jit(solution)/shard_map/table_sums/pallas_call | solution.py:276
  270.2 1.0 slice_add_fusion
  271.2 1.6 scatter-add.9
  272.7 2.5 multiply_reduce_fusion
  280.4 17.0 %shard_map.425 = f32[32,8,128]{2,1,0:T(8,128)} custom-call(f32[8,128]{1,0:T(8,128)} %broadcast_in_dim.6.refs_0_), custom_call_target="tpu_custom_call" | custom-call | tf_op jit(solution)/shard_map/pallas_call | solution.py:157
  297.4 1.5 slice_reduce_fusion.1
  302.2 1.8 multiply_subtract_fusion.3
  304.0 1.3 multiply_subtract_fusion.2
  305.9 1.5 multiply_subtract_fusion
  307.4 1.5 multiply_subtract_fusion.1
  309.1 0.9 copy-done
  310.6 3.2 %add_subtract_fusion = (f32[18384,24]{0,1:T(8,128)}, f32[18384,24]{0,1:T(8,128)}, f32[18384,24]{0,1:T(8,128)}) fusion(f32[18384,24]{0,1:T(8,128)S(1)} %copy-done.1, f32[]{:T(128)} %bitcast.51, f32[]{:T(128)} %bitcast.50, f32[24,18384]{1,0:T(8,128)S(1)} %copy-done, f32[]{:T(128)S(6)} %div.104, f32[18384,24]{0,1:T(8,128)S(1)} %copy-done.6, ...), kind=kLoop, calls=%fused_computation.6 | loop fusion | flops 6618240 | bytes 12354060 | tf_op jit(solution)/shard_map/sub | solution.py:66
  (163 shorter events, 20.6 us)
Async XLA Ops:
  0.7 11.4 %copy-start.3 = (f32[2,96,768]{2,1,0:T(8,128)S(1)}, f32[2,96,768]{2,1,0:T(8,128)}, u32[]{:S(2)}) copy-start(f32[2,96,768]{2,1,0:T(8,128)} %param.40) | copy-start | bytes 1769476
  97.4 7.9 %copy-start.18 = (bf16[32,48,96]{2,1,0:T(8,128)(2,1)S(1)}, bf16[32,48,96]{2,1,0:T(8,128)(2,1)}, u32[]{:S(2)}) copy-start(bf16[32,48,96]{2,1,0:T(8,128)(2,1)} %get-tuple-element.68) | copy-start | bytes 884740
  217.8 10.1 %copy-start.9 = (bf16[32,16,768]{2,1,0:T(8,128)(2,1)S(1)}, bf16[32,16,768]{2,1,0:T(8,128)(2,1)}, u32[]{:S(2)}) copy-start(bf16[32,16,768]{2,1,0:T(8,128)(2,1)} %get-tuple-element.76) | copy-start | bytes 2359300
  217.8 10.5 %copy-start.20 = (bf16[48,768]{1,0:T(8,128)(2,1)S(1)}, bf16[48,768]{1,0:T(8,128)(2,1)}, u32[]{:S(2)}) copy-start(bf16[48,768]{1,0:T(8,128)(2,1)} %get-tuple-element.74) | copy-start | bytes 221188
  217.8 11.5 %copy-start.21 = (bf16[24,256]{1,0:T(8,128)(2,1)S(1)}, bf16[24,256]{1,0:T(8,128)(2,1)}, u32[]{:S(2)}) copy-start(bf16[24,256]{1,0:T(8,128)(2,1)} %get-tuple-element.73) | copy-start | bytes 36868
  228.2 4.7 %copy-start.17 = (bf16[32,48,128]{2,1,0:T(8,128)(2,1)S(1)}, bf16[32,48,128]{2,1,0:T(8,128)(2,1)}, u32[]{:S(2)}) copy-start(bf16[32,48,128]{2,1,0:T(8,128)(2,1)} %get-tuple-element.78) | copy-start | bytes 1179652
  234.6 1.9 copy-start.19
  240.8 4.8 %copy-start.2 = (bf16[24,16384]{1,0:T(8,128)(2,1)S(1)}, bf16[24,16384]{1,0:T(8,128)(2,1)}, u32[]{:S(2)}) copy-start(bf16[24,16384]{1,0:T(8,128)(2,1)} %get-tuple-element.71.values_ref) | copy-start | bytes 2359300
  247.2 52.6 %copy-start.22 = (f32[2,264]{1,0:T(2,128)S(1)}, f32[2,264]{1,0:T(2,128)}, u32[]{:S(2)}) copy-start(f32[2,264]{1,0:T(2,128)} %get-tuple-element.186) | copy-start | bytes 6340
  247.2 52.6 %copy-start.23 = (f32[2,264]{1,0:T(2,128)S(1)}, f32[2,264]{1,0:T(2,128)}, u32[]{:S(2)}) copy-start(f32[2,264]{1,0:T(2,128)} %param.42) | copy-start | bytes 6340
  247.2 52.6 %copy-start.25 = (f32[2,264]{1,0:T(2,128)S(1)}, f32[2,264]{1,0:T(2,128)}, u32[]{:S(2)}) copy-start(f32[2,264]{1,0:T(2,128)} %param.56) | copy-start | bytes 6340
  247.2 52.6 %copy-start.26 = (f32[2,264]{1,0:T(2,128)S(1)}, f32[2,264]{1,0:T(2,128)}, u32[]{:S(2)}) copy-start(f32[2,264]{1,0:T(2,128)} %param.55) | copy-start | bytes 6340
  247.2 53.2 %copy-start.24 = (f32[2,3,24]{2,0,1:T(2,128)S(1)}, f32[2,3,24]{2,0,1:T(2,128)}, u32[]{:S(2)}) copy-start(f32[2,3,24]{2,0,1:T(2,128)} %param.41) | copy-start | bytes 1732
  247.2 53.2 %copy-start.27 = (f32[2,3,24]{2,0,1:T(2,128)S(1)}, f32[2,3,24]{2,0,1:T(2,128)}, u32[]{:S(2)}) copy-start(f32[2,3,24]{2,0,1:T(2,128)} %param.54) | copy-start | bytes 1732
  247.2 53.2 %copy-start.28 = (f32[2,3,24]{2,0,1:T(2,128)S(1)}, f32[2,3,24]{2,0,1:T(2,128)}, u32[]{:S(2)}) copy-start(f32[2,3,24]{2,0,1:T(2,128)} %param.53) | copy-start | bytes 1732
  247.2 54.9 %copy-start.14 = (f32[2,24,768]{2,1,0:T(8,128)S(1)}, f32[2,24,768]{2,1,0:T(8,128)}, u32[]{:S(2)}) copy-start(f32[2,24,768]{2,1,0:T(8,128)} %wout.1) | copy-start | bytes 442372
  270.2 33.8 %copy-start.8 = (f32[2,24,2304]{2,1,0:T(8,128)S(1)}, f32[2,24,2304]{2,1,0:T(8,128)}, u32[]{:S(2)}) copy-start(f32[2,24,2304]{2,1,0:T(8,128)} %win.1) | copy-start | bytes 1327108
  270.2 33.8 %copy-start.15 = (f32[2,24,2304]{2,1,0:T(8,128)S(1)}, f32[2,24,2304]{2,1,0:T(8,128)}, u32[]{:S(2)}) copy-start(f32[2,24,2304]{2,1,0:T(8,128)} %param.46) | copy-start | bytes 1327108
  270.2 33.8 %copy-start.16 = (f32[2,24,2304]{2,1,0:T(8,128)S(1)}, f32[2,24,2304]{2,1,0:T(8,128)}, u32[]{:S(2)}) copy-start(f32[2,24,2304]{2,1,0:T(8,128)} %param.45) | copy-start | bytes 1327108
  304.0 1.3 copy-start.5
  304.0 1.8 copy-start.10
  304.0 2.0 copy-start.11
  304.0 3.4 %copy-start.12 = (f32[2,24,3072]{2,1,0:T(8,128)S(1)}, f32[2,24,3072]{2,1,0:T(8,128)}, u32[]{:S(2)}) copy-start(f32[2,24,3072]{2,1,0:T(8,128)} %param.50) | copy-start | bytes 1769476
  304.0 3.4 %copy-start.13 = (f32[2,24,3072]{2,1,0:T(8,128)S(1)}, f32[2,24,3072]{2,1,0:T(8,128)}, u32[]{:S(2)}) copy-start(f32[2,24,3072]{2,1,0:T(8,128)} %param.49) | copy-start | bytes 1769476
  305.9 1.5 copy-start.4
  305.9 3.0 copy-start.6
  305.9 3.2 %copy-start.7 = (f32[18384,24]{0,1:T(8,128)S(1)}, f32[18384,24]{0,1:T(8,128)}, u32[]{:S(2)}) copy-start(f32[18384,24]{0,1:T(8,128)} %param.43) | copy-start | bytes 5294596
  307.4 2.6 copy-start
  307.4 3.2 %copy-start.1 = (f32[18384,24]{0,1:T(8,128)S(1)}, f32[18384,24]{0,1:T(8,128)}, u32[]{:S(2)}) copy-start(f32[18384,24]{0,1:T(8,128)} %param.36) | copy-start | bytes 5294596

commit v2 on v1

--- a/solution.py
+++ b/solution.py
@@ -572,13 +572,14 @@
 
 def middle_body(
     n_valid, nq, nd, narrow, cols, query_home, token_total,
-    mine, mine_q, w_one, w_zero, w_up, w_down, cv, rv, b_in, slots,
-    o_tok, o_fac, o_facq, o_line, o_lineq, o_du, o_shrink, o_h, o_rows, o_loss,
+    mine, mine_q, w_one, w_zero, up_mine, w_down, cv, rv, b_in, slots, ids,
+    o_shrink, o_loss, g_table, g_in, g_out, g_up, g_bin, g_small, o_norm,
     hat_s, scale_s, xl_s, xf_s, q_s, k_s, v_s, p_s, a_s,
     hat_q, scale_q, xl_q, xf_q, q_q, k_q, v_q, p_q, a_q,
     r1_own, r1_ownq, r1_all, y_send, y_recv, y_sum, y_all, h_send, h_recv, h_recvq,
     du_own, du_f, gtok, gtok_q, fac, fac_q, line, line_q, f_s, slope_s, hlow_s, g_top_s, sums_s,
-    size48,
+    size48, o_tok, o_fac, o_facq, o_line, o_lineq, o_du, o_h, up_got, w_up,
+    t_all, w_all, q_exp, d_exp, spread_s, acc_s, norm_own, norm_all,
     send_sem, recv_sem, own_sem,
 ):
     cap = -(-n_valid // nd)
@@ -598,6 +599,14 @@
     queries = Unit(nq, LQ)
     n_mine = jnp.where(me < n_valid - (cap - 1) * nd, cap, cap - 1)
 
+    up_flows = [
+        Flow(
+            lambda s, t: up_mine.at[t], lambda s, t: up_got.at[s],
+            lambda n: up_got.at[pl.ds(0, n)], everyone, everyone,
+        )
+    ]
+    up_base = net.start(up_flows)
+
     def front(c, carry):
         at = pl.ds(pl.multiple_of(c * LP, LANE), LP)
         emb = mine[:, :, at].astype(F32).reshape(D, LP) + w_one[:, 4 * D :].astype(F32)
@@ -646,6 +655,10 @@
 
     base = net.start(flows)
     net.finish(flows, base)
+
+    net.finish(up_flows, up_base)
+    for e in range(2):
+        w_up[e] = up_got[:, e].astype(F32).reshape(D, LANE).astype(BF16)
 
     part = {1: (0, n_valid), 0: (n_valid, nq)}
     y_parts = []
@@ -762,9 +775,6 @@
         du = (slope_s[at : at + n, :] * df).astype(BF16)
         du_f[at : at + n, :] = du.astype(F32)
         h_parts.append(mm(du, w_up[e], NT))
-    for e in (0, 1):
-        for j in range(3):
-            o_rows[3 * e + j : 3 * e + j + 1, :] = out_rows[e][j]
     du_own[...] = du_f[...].astype(BF16)
     store_rows(h_send, jnp.concatenate(h_parts, axis=0))
     flows = [
@@ -786,8 +796,8 @@
     du_flows = [
         Flow(
             lambda s, t: du_own,
-            lambda s, t: o_du.at[s],
-            lambda n: o_du.at[pl.ds(0, n)],
+            lambda s, t: o_du.at[:, pl.ds(pl.multiple_of(s * LANE, LANE), LANE)],
+            lambda n: o_du.at[:, pl.ds(0, n * LANE)],
             everyone, everyone,
         )
     ]
@@ -822,15 +832,19 @@
         kept = (
             hat_s[c], scale_s[c], xl_s[c], xf_s[c], q_s[c], k_s[c], v_s[c], p_s[c], a_s[c]
         )
-        g_emb, t, w, da, dq, do, dbv, g_gain, g_shift = unit_back(
+        g_emb, t, wx, da, dq, do, dbv, g_gain, g_shift = unit_back(
             passage, row_grad, 1, w_one, cv, kept
         )
         gtok[c] = g_emb.reshape(nd, cols, LP).astype(BF16)
-        tw = jnp.concatenate([t, w, xf_s[c].astype(F32), a_s[c].astype(F32)], axis=0)
-        tw = jnp.concatenate([tw, jnp.zeros((LANE - 48, D), F32)], axis=0)
-        tw_t = jnp.transpose(tw)
-        moved = jnp.where(lane < 48, tw_t, 0.0)
-        placed = pltpu.roll(moved, 64 * c, 1)
+        zero = jnp.zeros((16, D), F32)
+        xa = jnp.concatenate(
+            [xf_s[c].astype(F32)[0:1, :], jnp.zeros((15, D), F32), a_s[c].astype(F32)[0:1, :],
+             jnp.zeros((31, D), F32)],
+            axis=0,
+        )
+        tw = jnp.transpose(jnp.concatenate([t, zero, wx, zero, jnp.zeros((64, D), F32)], axis=0))
+        xa = jnp.transpose(jnp.concatenate([jnp.zeros((64, D), F32), xa, zero], axis=0))
+        placed = pltpu.roll(tw, 16 * c, 1) + pltpu.roll(xa, c, 1)
         fac[...] = (fac[...].astype(F32) + placed.reshape(nd, cols, LANE)).astype(BF16)
         which = iota((16, D), 0)
         new = jnp.zeros((16, D), F32)
@@ -930,8 +944,183 @@
         return size48.at[pl.ds(0, n)]
 
     base = net.start(flows)
+
+    net.finish(flows[cap + 1 :], base + cap + 1)
+    net.finish(du_flows, du_base)
+    lane1 = iota((cols, LANE), 1)
+    for g in range(nd // 4):
+        t_g = jnp.zeros((cols, LANE), F32)
+        w_g = jnp.zeros((cols, LANE), F32)
+        for j in range(4):
+            block = o_fac[4 * g + j].astype(F32)
+            t_part = jnp.where(lane1 < 32, block, 0.0)
+            w_part = jnp.where(jnp.logical_and(lane1 >= 32, lane1 < 64), block, 0.0)
+            t_g = t_g + (pltpu.roll(t_part, 32 * j, 1) if j else t_part)
+            w_g = w_g + (pltpu.roll(w_part, (32 * j - 32) % LANE, 1) if j != 1 else w_part)
+        t_all[:, g * LANE : (g + 1) * LANE] = t_g.astype(BF16)
+        w_all[:, g * LANE : (g + 1) * LANE] = w_g.astype(BF16)
+    x_all = jnp.zeros((cols, LANE), F32)
+    a_all = jnp.zeros((cols, LANE), F32)
+    for d in range(nd):
+        block = o_fac[d].astype(F32)
+        x_part = jnp.where(jnp.logical_and(lane1 >= 64, lane1 < 66), block, 0.0)
+        a_part = jnp.where(jnp.logical_and(lane1 >= 80, lane1 < 82), block, 0.0)
+        x_all = x_all + pltpu.roll(x_part, (2 * d - 64) % LANE, 1)
+        a_all = a_all + pltpu.roll(a_part, (2 * d - 80) % LANE, 1)
+    mask16 = ((iota((16, D), 0)) == (iota((16, D), 1) >> 6)).astype(F32)
+
+    def expand(d, carry):
+        for c in range(2):
+            at = pl.ds(pl.multiple_of(32 * d + 16 * c, 16), 16)
+            both = o_line[d].astype(F32)
+            q_exp[at, :] = (both[c : c + 1, :] * mask16).astype(BF16)
+            d_exp[at, :] = (both[2 + c : 3 + c, :] * mask16).astype(BF16)
+        return carry
+
+    lax.fori_loop(0, nd, expand, 0)
+    everything = o_line[...].reshape(nd * 16, D)
+    row, col = iota((272, nd * 16), 0), iota((272, nd * 16), 1)
+    kind = col & 15
+    pair = (col >> 4) * 2 + (col & 1)
+    dq_rows = jnp.logical_and(row < 128, jnp.logical_and((kind >> 1) == 2, pair == row))
+    do_rows = jnp.logical_and(
+        jnp.logical_and(row >= 128, row < 256),
+        jnp.logical_and((kind >> 1) == 3, pair == row - 128),
+    )
+    total_rows = jnp.logical_or(
+        jnp.logical_and(jnp.logical_and(row >= 256, row < 261), kind == row - 248),
+        jnp.logical_or(
+            jnp.logical_and(row == 261, (kind >> 1) == 2),
+            jnp.logical_and(row == 262, (kind >> 1) == 3),
+        ),
+    )
+    select = as_bf16(jnp.logical_or(dq_rows, jnp.logical_or(do_rows, total_rows)))
+    picked = mm(select, everything, NN)
+    g_in[1, :, 0:D] = mm(x_all.astype(BF16), picked[0:128].astype(BF16), NN)
+    g_in[1, :, D : 2 * D] = mm(t_all[...], q_exp[...], NN)
+    g_in[1, :, 2 * D : 3 * D] = mm(w_all[...], d_exp[...], NN)
+    g_out[1] = mm(a_all.astype(BF16), picked[128:256].astype(BF16), NN)
+    sums1 = picked[256:272]
+
+    fl = o_facq.shape[1]
+    row, col = iota((fl, 48), 0), iota((fl, 48), 1)
+    q_rows = H * nq
+    rown = iota((fl, D), 0)
+    headn = iota((fl, D), 1) >> 6
+
+    def rhs(first_row, last_row, first_col, by_head):
+        here = jnp.logical_and(row >= first_row, row < last_row)
+        hit = jnp.logical_and(here, col == first_col + (row & (nq - 1)))
+        out = mm(as_bf16(hit), o_lineq[...], NN)
+        if by_head:
+            out = jnp.where(((rown - first_row) >> (nq.bit_length() - 1)) == headn, out, 0.0)
+        return out.astype(BF16)
+
+    facq = o_facq[...]
+    g_in[0, :, 0:D] = mm(facq, rhs(2 * q_rows, 2 * q_rows + nq, 2 * nq, False), NN)
+    g_in[0, :, D : 2 * D] = mm(facq, rhs(0, q_rows, 0, True), NN)
+    g_in[0, :, 2 * D : 3 * D] = mm(facq, rhs(q_rows, 2 * q_rows, nq, True), NN)
+    g_out[0] = mm(facq, rhs(2 * q_rows + nq, 2 * q_rows + 2 * nq, 3 * nq, False), NN)
+    line0 = o_lineq[...].astype(F32)
+    sums0 = line0[4 * nq : 4 * nq + 8]
+    dq0 = jnp.sum(line0[2 * nq : 3 * nq], axis=0, keepdims=True)
+    do0 = jnp.sum(line0[3 * nq : 4 * nq], axis=0, keepdims=True)
+
+    mine_at = as_bf16(iota((cols, D), 1) == iota((cols, D), 0) + me * cols)
+    h_cols = mm(mine_at, o_h[...].astype(BF16), NT)
+    both = jnp.concatenate([h_cols, h_cols], axis=0)
+    r, c = iota((2 * cols, rows), 0), iota((2 * cols, rows), 1)
+    both = jnp.where((r < cols) == (c >= n_valid), both, 0.0).astype(BF16)
+    g_up[...] = mm(both, o_du[...], NN)
+    ones = iota((8, rows), 0)
+    which = iota((8, rows), 1)
+    e_rows = as_bf16(
+        jnp.logical_or(
+            jnp.logical_and(ones == 0, which >= n_valid),
+            jnp.logical_and(ones == 1, which < n_valid),
+        )
+    )
+    db_in = mm(e_rows, o_du[...], NN)
+    g_bin[...] = db_in
+    small_rows = {
+        0: (dq0, sums0[2:3], do0, sums0[4:5], out_rows[0][2], out_rows[0][1], sums0[1:2],
+            sums0[0:1], sums0[3:4], out_rows[0][0]),
+        1: (sums1[5:6], sums1[2:3], sums1[6:7], sums1[4:5], out_rows[1][2], out_rows[1][1],
+            sums1[1:2], sums1[0:1], sums1[3:4], out_rows[1][0]),
+    }
+    small_squares = jnp.sum(db_in * db_in)
+    for e in range(2):
+        for j, value in enumerate(small_rows[e]):
+            g_small[16 * e + j : 16 * e + j + 1, :] = value
+            small_squares = small_squares + jnp.sum(value * value)
+    squares = jnp.sum(g_in[...] * g_in[...]) + jnp.sum(g_out[...] * g_out[...])
+    squares = squares + jnp.sum(g_up[...] * g_up[...]) + jnp.sum(o_shrink[...] * o_shrink[...])
+
+    net.finish(flows[: cap + 1], base)
+    blocks = g_table.shape[1] // HASH
+    chunk = ids.shape[2]
+
+    def add_chunk(i, carry):
+        at = pl.ds(pl.multiple_of(i * chunk, LANE), chunk)
+        now = ids[i]
+        low = now & (HASH - 1)
+        high = now >> (HASH.bit_length() - 1)
+        values = o_tok[:, at].astype(F32)
+        for b in range(0, blocks, 2):
+            two = jnp.concatenate(
+                [jnp.where(high == b, values, 0.0), jnp.where(high == b + 1, values, 0.0)], axis=0
+            )
+            spread_s[b * cols : (b + 2) * cols, :] = two.astype(BF16)
+        hot = as_bf16(iota((HASH, chunk), 0) == low)
+        part = mm(spread_s[...], hot, NT)
+
+        @pl.when(i == 0)
+        def _():
+            acc_s[...] = part
+
+        @pl.when(i > 0)
+        def _():
+            acc_s[...] += part
+
+        return carry
+
+    lax.fori_loop(0, ids.shape[0], add_chunk, 0)
+
+    def add_slot(s, total):
+        return total + o_tok[:, pl.ds(pl.multiple_of(s * LP, LANE), LP)].astype(F32)
+
+    position = lax.fori_loop(0, n_valid, add_slot, jnp.zeros((cols, LP), F32))
+    tq = nq * LQ
+    q_tok = o_tok[:, n_valid * LP : n_valid * LP + tq].astype(F32)
+    folded = q_tok[:, 0:LANE]
+    for j in range(1, tq // LANE):
+        folded = folded + q_tok[:, j * LANE : (j + 1) * LANE]
+    around = folded
+    for j in range(1, LANE // LQ):
+        around = around + pltpu.roll(folded, LANE - LQ * j, 1)
+    around = jnp.where(lane1 < LQ, around, 0.0)
+    position = jnp.concatenate(
+        [position[:, 0:LANE] + around, position[:, LANE:], jnp.zeros((cols, HASH - LP), F32)],
+        axis=1,
+    )
+    shifted = pltpu.roll(position, V - (blocks - 1) * HASH, 1)
+    for b in range(blocks):
+        value = acc_s[b * cols : (b + 1) * cols, :]
+        if b == blocks - 1:
+            value = value + shifted
+        g_table[:, b * HASH : (b + 1) * HASH] = value
+        squares = squares + jnp.sum(value * value)
+
+    norm_own[...] = jnp.broadcast_to(squares.reshape(1, 1), (8, LANE))
+    flows = [
+        Flow(
+            lambda s, t: norm_own, lambda s, t: norm_all.at[s],
+            lambda n: norm_all.at[pl.ds(0, n)], everyone, everyone,
+        )
+    ]
+    base = net.start(flows)
     net.finish(flows, base)
-    net.finish(du_flows, du_base)
+    o_norm[...] = jnp.sqrt(jnp.sum(norm_all[...], axis=0) + small_squares)
 
 
 def middle(n_valid, nq, nd, narrow, cols, query_home, token_total, arrays):
@@ -958,25 +1147,26 @@
             pltpu.VMEM(lead + (u.seqs, D), BF16),
         ]
 
-    flows = 5 * (cap + 1) + 5
+    flows = 5 * (cap + 1) + 7
+    table_total = -(-(V + LP) // HASH) * HASH
+    chunk = arrays[10].shape[2]
     return pl.pallas_call(
         functools.partial(
             middle_body, n_valid, nq, nd, narrow, cols, query_home, token_total
         ),
         out_shape=[
-            like(cols, token_total, dtype=BF16),
-            like(nd, cols, LANE, dtype=BF16),
-            like(cols, fac_lanes, dtype=BF16),
-            like(nd, 16, D, dtype=BF16),
-            like(48, D, dtype=BF16),
-            like(nd, rows, LANE, dtype=BF16),
             like(2, LANE, D),
-            like(rows, D),
-            like(8, D),
+            like(8, LANE),
+            like(cols, table_total),
+            like(2, cols, 3 * D),
+            like(2, cols, D),
+            like(2 * cols, nd * LANE),
+            like(8, nd * LANE),
+            like(32, D),
             like(8, LANE),
         ],
         in_specs=[vmem] * len(arrays),
-        out_specs=[vmem] * 10,
+        out_specs=[vmem] * 9,
         scratch_shapes=kept((cap,), unit)
         + kept((), unit_q)
         + [
@@ -1004,6 +1194,23 @@
             pltpu.VMEM((rows, D), F32),
             pltpu.VMEM((8, D), F32),
             pltpu.VMEM((nd, 48, D), BF16),
+            pltpu.VMEM((cols, token_total), BF16),
+            pltpu.VMEM((nd, cols, LANE), BF16),
+            pltpu.VMEM((cols, fac_lanes), BF16),
+            pltpu.VMEM((nd, 16, D), BF16),
+            pltpu.VMEM((48, D), BF16),
+            pltpu.VMEM((rows, nd * LANE), BF16),
+            pltpu.VMEM((rows, D), F32),
+            pltpu.VMEM((nd, 2, cols, LANE), BF16),
+            pltpu.VMEM((2, D, LANE), BF16),
+            pltpu.VMEM((cols, nd * 32), BF16),
+            pltpu.VMEM((cols, nd * 32), BF16),
+            pltpu.VMEM((nd * 32, D), BF16),
+            pltpu.VMEM((nd * 32, D), BF16),
+            pltpu.VMEM((table_total // HASH * cols, chunk), BF16),
+            pltpu.VMEM((table_total // HASH * cols, HASH), F32),
+            pltpu.VMEM((8, LANE), F32),
+            pltpu.VMEM((nd, 8, LANE), F32),
             pltpu.SemaphoreType.DMA((flows,)),
             pltpu.SemaphoreType.DMA((flows,)),
             pltpu.SemaphoreType.DMA((flows,)),
@@ -1045,8 +1252,8 @@
 
 def first_body(
     n_valid, nq, nd, narrow, cols, home_at, blocks, forward_from,
-    ids_mine, small_mine, table, win, wout, pos_mine, up_mine,
-    ids_got, small_got, mine, mine_q, wall, w0, up_got,
+    ids_mine, small_mine, table, win, wout, pos_mine,
+    ids_got, small_got, mine, mine_q, wall, w0,
     stacked, tokens, tokens_q, p0,
     send_sem, recv_sem, own_sem, wide_send, wide_recv, x_send, x_recv, c_send, c_recv,
 ):
@@ -1186,13 +1393,6 @@
     home_base = net.start(home_moves)
     lax.fori_loop(0, pairs, gather, 0)
     send_pair(lax.rem(pairs - 1 + me, pairs))
-    up_moves = [
-        Flow(
-            lambda s, t: up_mine.at[t], lambda s, t: up_got.at[s],
-            lambda n: up_got.at[pl.ds(0, n)], everyone, everyone,
-        )
-    ]
-    up_base = net.start(up_moves)
     for k in range(wide):
         if forward_from + k >= pairs:
             forward(k)
@@ -1206,7 +1406,6 @@
     lax.fori_loop(0, wide, second, 0)
     net.finish(moves, base)
     net.finish(q_moves, q_base)
-    net.finish(up_moves, up_base)
     net.finish(home_moves, home_base)
 
     def last(row, carry):
@@ -1229,11 +1428,11 @@
     cap = -(-n_valid // nd)
     wide = nd // narrow
     tq = nq * LQ
-    ids_mine, small_mine, up_mine = arrays[0], arrays[1], arrays[6]
+    ids_mine, small_mine = arrays[0], arrays[1]
     n_own = ids_mine.shape[0] - 1
     blocks = -(-V // HASH)
     vmem = pl.BlockSpec(memory_space=pltpu.VMEM)
-    flows = 5 + cap
+    flows = 4 + cap
 
     def like(*shape, dtype=BF16):
         return jax.ShapeDtypeStruct(shape, dtype)
@@ -1250,10 +1449,9 @@
             like(nd, cols, tq),
             like(wide, narrow, cols, 4 * D + LP),
             like(nd, cols, 4 * D),
-            like(*up_mine.shape),
         ],
         in_specs=[vmem] * len(arrays),
-        out_specs=[vmem] * 7,
+        out_specs=[vmem] * 6,
         scratch_shapes=[
             pltpu.VMEM((blocks * cols, HASH), BF16),
             pltpu.VMEM((n_valid // n_own, n_own, cols, LP), BF16),
@@ -1677,10 +1875,9 @@
     ).astype(BF16)
     n_own = passage_ids.shape[0]
     table_t = embed_table.T
-    up_mine = expand_weight.astype(BF16).reshape(2 * cols, nd, ff_cols).transpose(1, 0, 2)
-    ids_got, small_got, mine, mine_q, w_one, w_zero, w_up = first(
+    ids_got, small_got, mine, mine_q, w_one, w_zero = first(
         n_valid, nq, nd, narrow, cols, query_home,
-        [ids_mine, small_mine, table_t, attend_in, attend_out, table_t[:, V : V + LP], up_mine],
+        [ids_mine, small_mine, table_t, attend_in, attend_out, table_t[:, V : V + LP]],
         12,
     )
     w_one = w_one.reshape(D, 4 * D + LP)
@@ -1695,8 +1892,8 @@
 
     vocab = V + LP
     total = -(-vocab // HASH) * HASH
-    w_up = w_up.reshape(nd, 2, cols, ff_cols).transpose(1, 0, 2, 3).reshape(2, D, ff_cols)
-    w_up = jnp.pad(w_up, ((0, 0), (0, 0), (0, LANE - ff_cols)))
+    up_mine = expand_weight.astype(BF16).reshape(2, cols, nd, ff_cols).transpose(2, 0, 1, 3)
+    up_mine = jnp.pad(up_mine, ((0, 0), (0, 0), (0, 0), (0, LANE - ff_cols)))
     w_down = jnp.pad(shrink_weight.astype(BF16), ((0, 0), (0, LANE - ff_cols), (0, 0)))
     cv = jnp.stack(
         [v for e in range(2) for v in (
@@ -1720,83 +1917,27 @@
         jnp.stack([passage_query, first_slot, kept_mask])[:, :n_valid],
         ((0, 5), (0, -(-n_valid // LANE) * LANE - n_valid)),
     )
-    tok, fac, fac_q, line, line_q, du_all, shrink_g, h_low, out_rows, loss = middle(
+    shrink_g, loss, g_table, g_in, g_out, g_up, g_bin, g_small, norm = middle(
         n_valid, nq, nd, narrow, cols, query_home, token_total,
-        [mine, mine_q, w_one, w_zero, w_up, w_down, cv, rv, b_in, slots],
+        [mine, mine_q, w_one, w_zero, up_mine, w_down, cv, rv, b_in, slots,
+         all_ids.reshape(-1, 1, 1024)],
     )
     loss = loss[0, 0]
-
-    table_grad = table_sums(tok, all_ids, total)[:, :vocab]
-    tok = tok.astype(F32)
-    pos_grad = jnp.sum(tok[:, :q_from].reshape(cols, n_valid, LP), axis=1)
-    q_pos = jnp.sum(tok[:, q_from : q_from + tq].reshape(cols, nq, LQ), axis=1)
-    pos_grad = pos_grad.at[:, :LQ].add(q_pos)
-    table_grad = table_grad.at[:, V:].add(pos_grad)
-
-    by_lane = fac.transpose(0, 2, 1).reshape(nd, 2, 64, cols)[:, :cap]
-    q_rows = H * nq
-    q_lane = fac_q.T
-    heads_q = lambda v: v.reshape(H, nq, cols).transpose(1, 0, 2)
-    factors = {
-        1: tuple(
-            v.reshape((nd * cap,) + v.shape[2:])
-            for v in (by_lane[:, :, 0:H], by_lane[:, :, 16 : 16 + H], by_lane[:, :, 32],
-                      by_lane[:, :, 40])
-        ),
-        0: (
-            heads_q(q_lane[:q_rows]), heads_q(q_lane[q_rows : 2 * q_rows]),
-            q_lane[2 * q_rows : 2 * q_rows + nq], q_lane[2 * q_rows + nq : 2 * q_rows + 2 * nq],
-        ),
-    }
-    lines = {
-        1: tuple(line[:, 2 * j : 2 * j + cap].reshape(nd * cap, D) for j in range(4)),
-        0: tuple(line_q[nq * j : nq * (j + 1)] for j in range(4)),
-    }
-    sums = {1: jnp.sum(line[:, 8:13].astype(F32), axis=0), 0: line_q[32:37].astype(F32)}
-    du_rows = du_all[:, :, :ff_cols].transpose(1, 0, 2).reshape(rows, FF)
-    h_cols = lax.dynamic_slice_in_dim(h_low, me * cols, cols, 1).astype(BF16)
-    in_grads, out_grads, expand_grads, bias_parts, gain_parts = [], [], [], [], []
-    for e in range(2):
-        at, n = (n_valid, nq) if e == 0 else (0, n_valid)
-        du_e = du_rows[at : at + n]
-        expand_grads.append(dot(h_cols[at : at + n], du_e, ((0,), (0,))))
-        t, w, x, a = factors[e]
-        q, da, dq, do = lines[e]
-        n_e = q.shape[0]
-        g_q = dot(x, dq, ((0,), (0,)))
-        g_k = jnp.einsum(
-            "phi,phd->ihd", t, q.reshape(n_e, H, HD), preferred_element_type=F32
-        ).reshape(cols, D)
-        g_v = jnp.einsum(
-            "phi,phd->ihd", w, da.reshape(n_e, H, HD), preferred_element_type=F32
-        ).reshape(cols, D)
-        in_grads.append(jnp.concatenate([g_q, g_k, g_v], axis=1))
-        out_grads.append(dot(a, do, ((0,), (0,))))
-        s = sums[e]
-        gain_parts.append(jnp.stack([s[0], s[3], out_rows[3 * e]]))
-        bias_parts.append(
-            jnp.concatenate(
-                [jnp.sum(dq.astype(F32), axis=0), s[2], jnp.sum(do.astype(F32), axis=0), s[4],
-                 jnp.sum(du_e.astype(F32), axis=0), out_rows[3 * e + 2], out_rows[3 * e + 1], s[1]]
-            )
-        )
+    grad_norm = norm[0, 0]
+    g_small = g_small.reshape(2, 16, D)
+    g_bin = g_bin[:2].reshape(2, nd, LANE)[:, :, :ff_cols].reshape(2, FF)
+    bias_grad = jnp.concatenate(
+        [g_small[:, :4].reshape(2, 4 * D), g_bin, g_small[:, 4:7].reshape(2, 3 * D)], axis=1
+    )
     grads = (
-        table_grad.T,
-        jnp.stack(in_grads),
-        jnp.stack(out_grads),
-        jnp.stack(expand_grads),
+        g_table[:, : V + LP].T,
+        g_in,
+        g_out,
+        g_up.reshape(2, cols, nd, LANE)[..., :ff_cols].reshape(2, cols, FF),
         shrink_g[:, :ff_cols],
-        lax.dynamic_slice_in_dim(jnp.stack(gain_parts), me * cols, cols, 2),
-        lax.dynamic_slice_in_dim(
-            jnp.stack(bias_parts), me * bias_terms.shape[1], bias_terms.shape[1], 1
-        ),
-    )
-    local_squares = sum(jnp.sum(g * g) for g in grads)
-    (squares,) = exch(
-        8, [jnp.broadcast_to(local_squares, (8, LANE))], [((nd, 8, LANE), F32)],
-        [send_all(0, 0, nd)],
-    )
-    grad_norm = jnp.sqrt(jnp.sum(squares[:, 0, 0]))
+        lax.dynamic_slice_in_dim(g_small[:, 7:10], me * cols, cols, 2),
+        lax.dynamic_slice_in_dim(bias_grad, me * bias_terms.shape[1], bias_terms.shape[1], 1),
+    )
     factor = CLIP / jnp.maximum(grad_norm, CLIP)
     step = step_count[0].astype(F32)
     masters = (embed_table, attend_in, attend_out, expand_weight, shrink_weight, norm_gains, bias_terms)

time: 316 us -> 271 us (0.86)
  other arithmetic: 35.5 us -> 20 us
  local copies, waits for them, and re-layouts: 31.9 us -> 16.6 us
  between operations: 8.58 us -> 2.42 us
  Pallas kernels: 236 us -> 232 us
    pallas_call x1, Pallas kernels: 112 us -> 153 us  [middle(): pl.pallas_call(functools.partial(middle_body, n_valid, nq, nd, narrow, co...]
    pallas_call x2 -> x0, Pallas kernels: 40 us -> none  [the longest x1 22.9 us: table_sums(): pl.pallas_call(functools.partial(scatter_body, rows, blocks), grid=(token...]
    reduce_sum x15 -> x0, other arithmetic: 13.5 us -> none  [the longest x7 8.49 us: on_device(): local_squares = sum((jnp.sum(g * g) for g in grads))]
    pallas_call x1, Pallas kernels: 84.5 us -> 78.7 us  [first(): pl.pallas_call(functools.partial(first_body, n_valid, nq, nd, narrow, col...]
    slice x18 -> x1, local copies, waits for them, and re-layouts: 5.49 us -> 1.19 us  [on_device(): grad_norm = norm[0, 0]]
    reshape x13 -> x3, local copies, waits for them, and re-layouts: 4.75 us -> 0.62 us  [the longest x2 0.52 us: on_device(): expand_weight.astype(BF16).reshape(2, cols, nd, ff_cols)]
    sub x7, other arithmetic: 9.88 us -> 13.6 us  [adam_update(): weight - rate * (first_hat / (jnp.sqrt(second_hat) + ADAM_EPS) + WEIGHT_D...]
    unnamed x79 -> x53, local copies, waits for them, and re-layouts: 6.94 us -> 3.71 us
where the time goes in v2:
time: 271 us; the launch traced here: 270 us
  Pallas kernels  232 us (86%)
  other arithmetic  20 us (7%)
  local copies, waits for them, and re-layouts  16.6 us (6%)
    pallas_call x1, Pallas kernels, middle(): pl.pallas_call(functools.partial(middle_body, n_valid, nq, nd, narrow, co...  153 us
    pallas_call x1, Pallas kernels, first(): pl.pallas_call(functools.partial(first_body, n_valid, nq, nd, narrow, col...  78.7 us
    sub x7, other arithmetic, adam_update(): weight - rate * (first_hat / (jnp.sqrt(second_hat) + ADAM_EPS) + WEIGHT_D...  13.6 us

profile of v2, /device:TPU:0, one launch (start us, length us, event | category | flops | bytes accessed | tf_op | source)
XLA Modules:
  0.0 270.5 jit_solution(8606881743430565652)
XLA Ops:
  0.7 0.7 tile.11
  1.3 0.1 tile.12
  1.4 1.3 pad_add_fusion.1.ids_mine
  2.7 1.5 slice.155.pos_mine
  4.2 0.7 convert.16
  4.9 0.7 convert.17
  5.6 0.6 fusion.8.small_mine
  6.2 78.7 %first.1 = (s32[32,3,384]{2,1,0:T(4,128)}, bf16[32,8,384]{2,1,0:T(8,128)(2,1)}, bf16[32,24,768]{2,1,0:T(8,128)(2,1)}, bf16[32,24,256]{2,1,0:T(8,128)(2,1)}, bf16...) custom-call(s32[3,384]{1,0:T(4,128)} %pad_add_fusion.1.ids_mine, bf16[8,384]{1,0:T(8,128)(2,1)} %fusion.8.small_mine, ...), custom_call_target="tpu_custom_call" | custom-call | tf_op jit(solution)/shard_map/first/pallas_call | solution.py:1441
  85.0 1.0 convert_bitcast_fusion.1
  86.0 0.2 reshape.171
  86.2 0.9 convert_bitcast_fusion
  87.1 0.1 reshape.170
  87.3 1.3 stack.26.rv
  88.6 0.9 copy.70.cv
  89.5 0.1 reshape.161
  89.6 0.6 pad.39.b_in
  90.2 0.9 slice.143
  91.2 0.1 reshape.162
  91.2 1.0 slice_reduce_fusion
  92.3 0.6 pad.41
  92.9 0.0 copy-start.17
  92.9 0.0 copy-start.22
  92.9 0.4 reshape.160
  93.3 0.2 copy.88
  93.5 0.8 pad.37.up_mine
  94.4 0.8 pad.38.w_down
  95.1 0.1 fusion.14
  95.2 0.6 pad.40.slots
  95.9 152.8 %middle.1 = (f32[2,128,768]{2,1,0:T(8,128)}, f32[8,128]{1,0:T(8,128)}, f32[24,18432]{1,0:T(8,128)}, f32[2,24,2304]{2,1,0:T(8,128)}, f32[2,24,768]{2,1,0:T(8,128)...) custom-call(bf16[32,24,768]{2,1,0:T(8,128)(2,1)} %get-tuple-element.38.mine, ...), custom_call_target="tpu_custom_call" | custom-call | tf_op jit(solution)/shard_map/middle/pallas_call | solution.py:1153
  248.7 0.9 slice_bitcast_fusion
  249.6 0.1 reshape.168
  249.7 1.0 slice_bitcast_fusion.1
  250.7 0.8 slice_bitcast_fusion.2
  251.5 1.2 slice.146
  254.2 0.7 multiply_subtract_fusion.4
  254.9 0.1 constant_dynamic-slice_fusion
  255.0 0.6 add_subtract_fusion.1
  255.6 2.8 %multiply_subtract_fusion = (f32[2,96,768]{2,1,0:T(8,128)}, f32[2,96,768]{2,1,0:T(8,128)}, f32[2,96,768]{2,1,0:T(8,128)}) fusion(f32[2,96,768]{2,1,0:T(8,128)S(1)} %copy-done.1, f32[]{:T(128)} %bitcast.26, f32[]{:T(128)} %bitcast.25, f32[]{:T(128)S(6)} %div.104, f32[2,128,768]{2,1,0:T(8,128)} %get-tuple-element.50, f32[2,96,768]{2,1,0:T(8,128)S(1)} %copy-done.8, ...), kind=kLoop, calls=%fused_computation.12 | loop fusion | flops 2359296 | bytes 4128780 | tf_op jit(solution)/shard_map/sub | solution.py:66
  258.4 0.1 copy.75
  258.5 0.1 slice_multiply_fusion.1
  258.6 0.4 mul.361
  259.0 0.5 copy-done.9
  259.6 0.2 copy-done.10
  259.8 1.5 multiply_subtract_fusion.1
  261.3 2.3 multiply_subtract_fusion.3
  263.6 2.5 multiply_subtract_fusion.2
  266.1 3.2 %add_subtract_fusion = (f32[18384,24]{0,1:T(8,128)}, f32[18384,24]{0,1:T(8,128)}, f32[18384,24]{0,1:T(8,128)}) fusion(f32[18384,24]{0,1:T(8,128)S(1)} %copy-done, f32[]{:T(128)} %bitcast.26, f32[]{:T(128)} %bitcast.25, f32[]{:T(128)S(6)} %div.104, f32[24,18432]{1,0:T(8,128)S(1)} %copy-done.5, f32[18384,24]{0,1:T(8,128)S(1)} %copy-done.3, ...), kind=kLoop, calls=%fused_computation.4 | loop fusion | flops 6618240 | bytes 12354060 | tf_op jit(solution)/shard_map/sub | solution.py:66
  269.3 1.2 slice.145
  (61 shorter events, 0.4 us)
Async XLA Ops:
  84.9 7.9 %copy-start.2 = (f32[2,24,3072]{2,1,0:T(8,128)S(1)}, f32[2,24,3072]{2,1,0:T(8,128)}, u32[]{:S(2)}) copy-start(f32[2,24,3072]{2,1,0:T(8,128)} %param.35) | copy-start | bytes 1769476
  91.2 3.2 %copy-start.1 = (f32[2,96,768]{2,1,0:T(8,128)S(1)}, f32[2,96,768]{2,1,0:T(8,128)}, u32[]{:S(2)}) copy-start(f32[2,96,768]{2,1,0:T(8,128)} %param.36) | copy-start | bytes 1769476
  92.9 2.2 copy-start.17
  92.9 2.3 copy-start.22
  95.8 158.3 %copy-start.15 = (f32[2,264]{1,0:T(2,128)S(1)}, f32[2,264]{1,0:T(2,128)}, u32[]{:S(2)}) copy-start(f32[2,264]{1,0:T(2,128)} %param.38) | copy-start | bytes 6340
  95.8 158.3 %copy-start.18 = (f32[2,264]{1,0:T(2,128)S(1)}, f32[2,264]{1,0:T(2,128)}, u32[]{:S(2)}) copy-start(f32[2,264]{1,0:T(2,128)} %param.52) | copy-start | bytes 6340
  95.8 158.3 %copy-start.19 = (f32[2,264]{1,0:T(2,128)S(1)}, f32[2,264]{1,0:T(2,128)}, u32[]{:S(2)}) copy-start(f32[2,264]{1,0:T(2,128)} %param.51) | copy-start | bytes 6340
  95.8 159.1 %copy-start.16 = (f32[2,3,24]{2,0,1:T(2,128)S(1)}, f32[2,3,24]{2,0,1:T(2,128)}, u32[]{:S(2)}) copy-start(f32[2,3,24]{2,0,1:T(2,128)} %param.37) | copy-start | bytes 1732
  95.8 159.1 %copy-start.20 = (f32[2,3,24]{2,0,1:T(2,128)S(1)}, f32[2,3,24]{2,0,1:T(2,128)}, u32[]{:S(2)}) copy-start(f32[2,3,24]{2,0,1:T(2,128)} %param.50) | copy-start | bytes 1732
  95.8 159.1 %copy-start.21 = (f32[2,3,24]{2,0,1:T(2,128)S(1)}, f32[2,3,24]{2,0,1:T(2,128)}, u32[]{:S(2)}) copy-start(f32[2,3,24]{2,0,1:T(2,128)} %param.49) | copy-start | bytes 1732
  95.9 159.7 %copy-start.8 = (f32[2,96,768]{2,1,0:T(8,128)S(1)}, f32[2,96,768]{2,1,0:T(8,128)}, u32[]{:S(2)}) copy-start(f32[2,96,768]{2,1,0:T(8,128)} %param.48) | copy-start | bytes 1769476
  255.6 2.8 %copy-start.7 = (f32[48,4096]{1,0:T(8,128)S(1)}, f32[48,4096]{1,0:T(8,128)}, u32[]{:S(2)}) copy-start(f32[48,4096]{1,0:T(8,128)} %get-tuple-element.49) | copy-start | bytes 2359300
  258.5 1.1 copy-start.9
  258.5 1.2 copy-start.10
  258.6 2.7 copy-start.13
  258.6 2.6 copy-start.14
  259.8 1.5 copy-start.11
  259.8 3.8 %copy-start.6 = (f32[2,24,2304]{2,1,0:T(8,128)S(1)}, f32[2,24,2304]{2,1,0:T(8,128)}, u32[]{:S(2)}) copy-start(f32[2,24,2304]{2,1,0:T(8,128)} %win.1) | copy-start | bytes 1327108
  259.8 3.8 %copy-start.12 = (f32[2,24,2304]{2,1,0:T(8,128)S(1)}, f32[2,24,2304]{2,1,0:T(8,128)}, u32[]{:S(2)}) copy-start(f32[2,24,2304]{2,1,0:T(8,128)} %param.42) | copy-start | bytes 1327108
  259.8 6.3 %copy-start.4 = (f32[18384,24]{0,1:T(8,128)S(1)}, f32[18384,24]{0,1:T(8,128)}, u32[]{:S(2)}) copy-start(f32[18384,24]{0,1:T(8,128)} %param.39) | copy-start | bytes 5294596
  259.8 6.3 %copy-start.5 = (f32[24,18432]{1,0:T(8,128)S(1)}, f32[24,18432]{1,0:T(8,128)}, u32[]{:S(2)}) copy-start(f32[24,18432]{1,0:T(8,128)} %get-tuple-element.46) | copy-start | bytes 5308420
  261.3 4.8 %copy-start.3 = (f32[18384,24]{0,1:T(8,128)S(1)}, f32[18384,24]{0,1:T(8,128)}, u32[]{:S(2)}) copy-start(f32[18384,24]{0,1:T(8,128)} %param.40) | copy-start | bytes 5294596
  263.6 2.6 copy-start

commit v3 on v2

--- a/solution.py
+++ b/solution.py
@@ -71,6 +71,7 @@
 
 MESH = pl.DeviceIdType.MESH
 HASH = 512
+FORWARD_PLAN = (0, 4, 7, 10, 12, 13, 14, 15) + (99,) * 8
 
 
 class Send:
@@ -378,6 +379,23 @@
     return mask.astype(F32).astype(BF16)
 
 
+def group(count, nd, first=0):
+    return (first, nd // count, count)
+
+
+def within(index, span):
+    first, stride, count = span
+    if count == 0:
+        return index < 0
+    if stride == 1:
+        return jnp.logical_and(index >= first, index < first + count)
+    return ((index - first) & (stride - 1)) == 0
+
+
+def place(index, span):
+    return (index - span[0]) // span[1]
+
+
 class Flow:
     def __init__(self, take, put, many, sources, targets):
         self.take, self.put, self.many = take, put, many
@@ -414,7 +432,7 @@
             t = lax.rem(me + k, nd)
             for i, f in enumerate(flows):
 
-                @pl.when(jnp.logical_and(inside(me, f.sources), inside(t, f.targets)))
+                @pl.when(jnp.logical_and(within(me, f.sources), within(t, f.targets)))
                 def _():
                     pltpu.make_async_remote_copy(
                         src_ref=f.take(me, t),
@@ -429,7 +447,7 @@
 
         for i, f in enumerate(flows):
 
-            @pl.when(jnp.logical_and(inside(me, f.sources), inside(me, f.targets)))
+            @pl.when(jnp.logical_and(within(me, f.sources), within(me, f.targets)))
             def _():
                 pltpu.make_async_copy(
                     f.take(me, me), f.put(me, me), self.own_sem.at[base + i]
@@ -441,9 +459,8 @@
     def finish(self, flows, base):
         me = self.me
         for i, f in enumerate(flows):
-            n_t = f.targets[1] - f.targets[0]
-            n_s = f.sources[1] - f.sources[0]
-            is_s, is_t = inside(me, f.sources), inside(me, f.targets)
+            n_t, n_s = f.targets[2], f.sources[2]
+            is_s, is_t = within(me, f.sources), within(me, f.targets)
 
             @pl.when(jnp.logical_and(is_s, is_t))
             def _():
@@ -571,33 +588,38 @@
 
 
 def middle_body(
-    n_valid, nq, nd, narrow, cols, query_home, token_total,
-    mine, mine_q, w_one, w_zero, up_mine, w_down, cv, rv, b_in, slots, ids,
+    n_valid, nq, nd, narrow, cols, query_home,
+    mine, mine_q, w_one, w_zero, up_mine, w_down, cv, rv, b_in, slots, ids, ids_q,
     o_shrink, o_loss, g_table, g_in, g_out, g_up, g_bin, g_small, o_norm,
     hat_s, scale_s, xl_s, xf_s, q_s, k_s, v_s, p_s, a_s,
     hat_q, scale_q, xl_q, xf_q, q_q, k_q, v_q, p_q, a_q,
     r1_own, r1_ownq, r1_all, y_send, y_recv, y_sum, y_all, h_send, h_recv, h_recvq,
     du_own, du_f, gtok, gtok_q, fac, fac_q, line, line_q, f_s, slope_s, hlow_s, g_top_s, sums_s,
-    size48, o_tok, o_fac, o_facq, o_line, o_lineq, o_du, o_h, up_got, w_up,
+    o_tok, o_fac, o_facq, o_line, o_lineq, o_du, o_h, up_got, w_up,
     t_all, w_all, q_exp, d_exp, spread_s, acc_s, norm_own, norm_all,
+    tok_send, tok_recv, twin_send, twin_recv, chain_send, chain_recv,
     send_sem, recv_sem, own_sem,
 ):
     cap = -(-n_valid // nd)
     rows = n_valid + nq
     net = Net(nd, narrow, send_sem, recv_sem, own_sem)
     me = net.me
-    everyone = (0, nd)
-    home = (query_home, query_home + 1)
-    q_owner = nd - nq
-    q_owners = (q_owner, nd)
+    everyone = group(nd, nd)
+    home = (query_home, 1, 1)
+    q_owners = group(nq, nd, 2)
+    core = me & 1
+    alike = (core, 2, nd // 2)
 
     def span(c):
-        return (0, min(nd, n_valid - c * nd))
+        return group(nd, nd) if c == 0 else group(n_valid - nd, nd, 1)
+
+    def slot_of(c, d):
+        return c * nd + place(d, span(c))
 
     net.barrier()
     passage = Unit(1, LP)
     queries = Unit(nq, LQ)
-    n_mine = jnp.where(me < n_valid - (cap - 1) * nd, cap, cap - 1)
+    n_mine = jnp.where(within(me, span(1)), 2, 1)
 
     up_flows = [
         Flow(
@@ -636,7 +658,7 @@
     flows = [
         Flow(
             lambda s, t, c=c: r1_own.at[c],
-            lambda s, t, c=c: r1_all.at[pl.ds(pl.multiple_of(8 * (c * nd + s), 8), 8), :],
+            lambda s, t, c=c: r1_all.at[pl.ds(pl.multiple_of(8 * slot_of(c, s), 8), 8), :],
             lambda n: r1_all.at[pl.ds(0, 8 * n), :],
             span(c), everyone,
         )
@@ -678,7 +700,7 @@
     store_rows(y_send, jnp.concatenate(y_parts, axis=0))
     flows = [
         Flow(
-            lambda s, t, c=c: y_send.at[pl.ds(pl.multiple_of(8 * (c * nd + t), 8), 8), :],
+            lambda s, t, c=c: y_send.at[pl.ds(pl.multiple_of(8 * slot_of(c, t), 8), 8), :],
             lambda s, t, c=c: y_recv.at[s, c],
             lambda n, c=c: y_recv.at[pl.ds(0, n), c],
             everyone, span(c),
@@ -686,7 +708,7 @@
         for c in range(cap)
     ] + [
         Flow(
-            lambda s, t: y_send.at[pl.ds(pl.multiple_of(8 * (n_valid + t - q_owner), 8), 8), :],
+            lambda s, t: y_send.at[pl.ds(pl.multiple_of(8 * (n_valid + place(t, q_owners)), 8), 8), :],
             lambda s, t: y_recv.at[s, cap],
             lambda n: y_recv.at[pl.ds(0, n), cap],
             everyone, q_owners,
@@ -698,7 +720,7 @@
     flows = [
         Flow(
             lambda s, t, c=c: y_sum.at[c],
-            lambda s, t, c=c: y_all.at[pl.ds(pl.multiple_of(8 * (c * nd + s), 8), 8), :],
+            lambda s, t, c=c: y_all.at[pl.ds(pl.multiple_of(8 * slot_of(c, s), 8), 8), :],
             lambda n: y_all.at[pl.ds(0, 8 * n), :],
             span(c), everyone,
         )
@@ -706,7 +728,7 @@
     ] + [
         Flow(
             lambda s, t: y_sum.at[cap],
-            lambda s, t: y_all.at[pl.ds(pl.multiple_of(8 * (n_valid + s - q_owner), 8), 8), :],
+            lambda s, t: y_all.at[pl.ds(pl.multiple_of(8 * (n_valid + place(s, q_owners)), 8), 8), :],
             lambda n: y_all.at[pl.ds(0, 8 * n), :],
             q_owners, everyone,
         )
@@ -779,7 +801,7 @@
     store_rows(h_send, jnp.concatenate(h_parts, axis=0))
     flows = [
         Flow(
-            lambda s, t, c=c: h_send.at[pl.ds(pl.multiple_of(8 * (c * nd + t), 8), 8), :],
+            lambda s, t, c=c: h_send.at[pl.ds(pl.multiple_of(8 * slot_of(c, t), 8), 8), :],
             lambda s, t, c=c: h_recv.at[s, c],
             lambda n, c=c: h_recv.at[pl.ds(0, n), c],
             everyone, span(c),
@@ -796,9 +818,11 @@
     du_flows = [
         Flow(
             lambda s, t: du_own,
-            lambda s, t: o_du.at[:, pl.ds(pl.multiple_of(s * LANE, LANE), LANE)],
+            lambda s, t: o_du.at[
+                :, pl.ds(pl.multiple_of(((s & 1) * (nd // 2) + s // 2) * LANE, LANE), LANE)
+            ],
             lambda n: o_du.at[:, pl.ds(0, n * LANE)],
-            everyone, everyone,
+            alike, alike,
         )
     ]
     base = net.start(flows)
@@ -806,9 +830,6 @@
     fac[...] = jnp.zeros_like(fac)
     line[...] = jnp.zeros_like(line)
     sums_s[...] = jnp.zeros_like(sums_s)
-    o_tok[:, n_valid * LP + nq * LQ :] = jnp.zeros(
-        (cols, token_total - n_valid * LP - nq * LQ), BF16
-    )
     net.finish(flows, base)
 
     def load_rows_sum(ref, count):
@@ -819,7 +840,7 @@
     lane = iota((D, LANE), 1)
 
     def back(c, carry):
-        slot = c * nd + me
+        slot = jnp.where(c == 0, me, slot_of(1, me))
         tile = jnp.sum(h_recv[:, c], axis=0)
         dh = jnp.concatenate([tile[j : j + 1, :] for j in range(D // LANE)], axis=1)
         top = g_top_s[pl.ds(slot, 1), :]
@@ -899,15 +920,51 @@
         )
         line_q[16:64, :] = block.astype(BF16)
 
+    half = nd // 2
+
+    def to_twin(src, sem):
+        return pltpu.make_async_remote_copy(
+            src_ref=src, dst_ref=src, send_sem=twin_send.at[sem], recv_sem=twin_recv.at[sem],
+            device_id=net.where(me ^ 1), device_id_type=MESH,
+        )
+
+    row_flows = [
+        Flow(
+            lambda s, t: line_q.at[pl.ds(0, 16), :],
+            lambda s, t: o_line.at[s & 1, s // 2],
+            lambda n: o_line.at[0, pl.ds(0, n)],
+            alike, alike,
+        ),
+    ]
+    plane, home_core = query_home // 8, query_home % 2
+    z_at = me // 8
+    on_core = core == home_core
+    query_rows = line_q.at[pl.ds(16, 48), :]
+
+    def pass_rows(src, t, sem):
+        pltpu.make_async_remote_copy(
+            src_ref=src, dst_ref=o_lineq, send_sem=chain_send.at[sem], recv_sem=chain_recv,
+            device_id=net.where(t), device_id_type=MESH,
+        ).start()
+
+    def rows_sent(sem):
+        pltpu.make_async_copy(o_lineq, o_lineq, chain_send.at[sem]).wait()
+
+    at_home = me == query_home
+    in_plane = jnp.logical_and(z_at == plane, on_core)
+    goes_up = jnp.logical_and(on_core, jnp.logical_and(z_at >= plane, z_at < nd // 8 - 1))
+    goes_down = jnp.logical_and(on_core, jnp.logical_and(z_at <= plane, z_at > 0))
+
+    @pl.when(at_home)
+    def _():
+        own = pltpu.make_async_copy(query_rows, o_lineq, own_sem.at[own_sem.shape[0] - 1])
+        own.start()
+        for j in range(1, 4):
+            pass_rows(query_rows, me ^ (2 * j), j)
+        own.wait()
+
+    row_base = net.start(row_flows)
     flows = [
-        Flow(
-            lambda s, t, c=c: gtok.at[c, t],
-            lambda s, t, c=c: o_tok.at[:, pl.ds(pl.multiple_of((c * nd + s) * LP, LANE), LP)],
-            lambda n: o_tok.at[:, pl.ds(0, n * LP)],
-            span(c), everyone,
-        )
-        for c in range(cap)
-    ] + [
         Flow(
             lambda s, t: gtok_q.at[t],
             lambda s, t: o_tok.at[:, pl.ds(n_valid * LP, nq * LQ)],
@@ -926,27 +983,59 @@
             lambda n: fac_q.at[pl.ds(0, n)],
             home, everyone,
         ),
-        Flow(
-            lambda s, t: line_q.at[pl.ds(0, 16), :],
-            lambda s, t: o_line.at[s],
-            lambda n: o_line.at[pl.ds(0, n)],
-            everyone, everyone,
-        ),
-        Flow(
-            lambda s, t: line_q.at[pl.ds(16, 48), :],
-            lambda s, t: o_lineq,
-            lambda n: o_line48(n),
-            home, everyone,
-        ),
     ]
-
-    def o_line48(n):
-        return size48.at[pl.ds(0, n)]
-
     base = net.start(flows)
 
-    net.finish(flows[cap + 1 :], base + cap + 1)
+    def tok_view(slot):
+        return o_tok.at[:, pl.ds(pl.multiple_of(slot * LP, LANE), LP)]
+
+    def push_tokens(k, carry):
+        t = lax.rem(me + k, nd)
+        for c in range(cap):
+
+            @pl.when(within(me, span(c)))
+            def _():
+                slot = slot_of(c, me)
+                pltpu.make_async_remote_copy(
+                    src_ref=gtok.at[c, t], dst_ref=tok_view(slot),
+                    send_sem=tok_send.at[c], recv_sem=tok_recv.at[slot],
+                    device_id=net.where(t), device_id_type=MESH,
+                ).start()
+
+        return carry
+
+    for c in range(cap):
+
+        @pl.when(within(me, span(c)))
+        def _():
+            slot = slot_of(c, me)
+            pltpu.make_async_copy(gtok.at[c, me], tok_view(slot), tok_recv.at[slot]).start()
+
+    lax.fori_loop(1, nd, push_tokens, 0)
+
+    @pl.when(jnp.logical_not(at_home))
+    def _():
+        pltpu.make_async_copy(o_lineq, o_lineq, chain_recv).wait()
+
+    @pl.when(goes_up)
+    def _():
+        pass_rows(o_lineq, me + 8, 4)
+
+    @pl.when(goes_down)
+    def _():
+        pass_rows(o_lineq, me - 8, 5)
+
+    @pl.when(on_core)
+    def _():
+        pass_rows(o_lineq, me ^ 1, 6)
+
     net.finish(du_flows, du_base)
+    du_half = o_du.at[:, pl.ds(pl.multiple_of(core * (half * LANE), LANE), half * LANE)]
+    to_twin(du_half, 0).start()
+    net.finish(row_flows, row_base)
+    to_twin(o_line.at[core], 1).start()
+
+    net.finish(flows[1:], base + 1)
     lane1 = iota((cols, LANE), 1)
     for g in range(nd // 4):
         t_g = jnp.zeros((cols, LANE), F32)
@@ -969,10 +1058,13 @@
         a_all = a_all + pltpu.roll(a_part, (2 * d - 80) % LANE, 1)
     mask16 = ((iota((16, D), 0)) == (iota((16, D), 1) >> 6)).astype(F32)
 
+    to_twin(du_half, 0).wait()
+    to_twin(o_line.at[core], 1).wait()
+
     def expand(d, carry):
+        both = o_line[d & 1, d // 2].astype(F32)
         for c in range(2):
             at = pl.ds(pl.multiple_of(32 * d + 16 * c, 16), 16)
-            both = o_line[d].astype(F32)
             q_exp[at, :] = (both[c : c + 1, :] * mask16).astype(BF16)
             d_exp[at, :] = (both[2 + c : 3 + c, :] * mask16).astype(BF16)
         return carry
@@ -981,7 +1073,9 @@
     everything = o_line[...].reshape(nd * 16, D)
     row, col = iota((272, nd * 16), 0), iota((272, nd * 16), 1)
     kind = col & 15
-    pair = (col >> 4) * 2 + (col & 1)
+    at_block = col >> 4
+    device = (at_block & (half - 1)) * 2 + (at_block // half)
+    pair = device * 2 + (col & 1)
     dq_rows = jnp.logical_and(row < 128, jnp.logical_and((kind >> 1) == 2, pair == row))
     do_rows = jnp.logical_and(
         jnp.logical_and(row >= 128, row < 256),
@@ -1056,35 +1150,61 @@
     squares = jnp.sum(g_in[...] * g_in[...]) + jnp.sum(g_out[...] * g_out[...])
     squares = squares + jnp.sum(g_up[...] * g_up[...]) + jnp.sum(o_shrink[...] * o_shrink[...])
 
-    net.finish(flows[: cap + 1], base)
     blocks = g_table.shape[1] // HASH
-    chunk = ids.shape[2]
-
-    def add_chunk(i, carry):
-        at = pl.ds(pl.multiple_of(i * chunk, LANE), chunk)
-        now = ids[i]
+    acc_s[...] = jnp.zeros_like(acc_s)
+
+    def add_tokens(now, values):
         low = now & (HASH - 1)
         high = now >> (HASH.bit_length() - 1)
-        values = o_tok[:, at].astype(F32)
+        width = now.shape[1]
         for b in range(0, blocks, 2):
             two = jnp.concatenate(
                 [jnp.where(high == b, values, 0.0), jnp.where(high == b + 1, values, 0.0)], axis=0
             )
-            spread_s[b * cols : (b + 2) * cols, :] = two.astype(BF16)
-        hot = as_bf16(iota((HASH, chunk), 0) == low)
-        part = mm(spread_s[...], hot, NT)
-
-        @pl.when(i == 0)
+            spread_s[b * cols : (b + 2) * cols, 0:width] = two.astype(BF16)
+        hot = as_bf16(iota((HASH, width), 0) == low)
+        acc_s[...] += mm(spread_s[:, 0:width], hot, NT)
+
+    def add_slots(slots_now):
+        for slot in slots_now:
+            pltpu.make_async_copy(tok_view(slot), tok_view(slot), tok_recv.at[slot]).wait()
+        values = [tok_view(slot)[...].astype(F32) for slot in slots_now]
+        add_tokens(
+            jnp.concatenate([ids[slot] for slot in slots_now], axis=1),
+            jnp.concatenate(values, axis=1),
+        )
+
+    def add_near(k, carry):
+        add_slots([lax.rem(me - 2 * k - j + nd, nd) for j in range(2)])
+        return carry
+
+    def add_far(k, carry):
+        extra = n_valid - nd
+        first = me // (nd // extra)
+        add_slots([nd + lax.rem(first - 2 * k - j + 2 * extra, extra) for j in range(2)])
+        return carry
+
+    lax.fori_loop(0, nd // 2, add_near, 0)
+    lax.fori_loop(0, (n_valid - nd) // 2, add_far, 0)
+    net.finish(flows[:1], base)
+    add_tokens(ids_q[...], o_tok[:, n_valid * LP : n_valid * LP + nq * LQ].astype(F32))
+    for c in range(cap):
+
+        @pl.when(within(me, span(c)))
         def _():
-            acc_s[...] = part
-
-        @pl.when(i > 0)
+            sent = o_tok.at[:, pl.ds(0, (nd - 1) * LP)]
+            pltpu.make_async_copy(sent, sent, tok_send.at[c]).wait()
+
+    @pl.when(at_home)
+    def _():
+        for j in range(1, 4):
+            rows_sent(j)
+
+    for ok, sem in ((goes_up, 4), (goes_down, 5), (on_core, 6)):
+
+        @pl.when(ok)
         def _():
-            acc_s[...] += part
-
-        return carry
-
-    lax.fori_loop(0, ids.shape[0], add_chunk, 0)
+            rows_sent(sem)
 
     def add_slot(s, total):
         return total + o_tok[:, pl.ds(pl.multiple_of(s * LP, LANE), LP)].astype(F32)
@@ -1123,7 +1243,7 @@
     o_norm[...] = jnp.sqrt(jnp.sum(norm_all[...], axis=0) + small_squares)
 
 
-def middle(n_valid, nq, nd, narrow, cols, query_home, token_total, arrays):
+def middle(n_valid, nq, nd, narrow, cols, query_home, arrays):
     cap = -(-n_valid // nd)
     rows = n_valid + nq
     tq = nq * LQ
@@ -1149,10 +1269,10 @@
 
     flows = 5 * (cap + 1) + 7
     table_total = -(-(V + LP) // HASH) * HASH
-    chunk = arrays[10].shape[2]
+    chunk = 2 * LP
     return pl.pallas_call(
         functools.partial(
-            middle_body, n_valid, nq, nd, narrow, cols, query_home, token_total
+            middle_body, n_valid, nq, nd, narrow, cols, query_home
         ),
         out_shape=[
             like(2, LANE, D),
@@ -1193,11 +1313,10 @@
             pltpu.VMEM((rows, D), F32),
             pltpu.VMEM((rows, D), F32),
             pltpu.VMEM((8, D), F32),
-            pltpu.VMEM((nd, 48, D), BF16),
-            pltpu.VMEM((cols, token_total), BF16),
+            pltpu.VMEM((cols, n_valid * LP + tq), BF16),
             pltpu.VMEM((nd, cols, LANE), BF16),
             pltpu.VMEM((cols, fac_lanes), BF16),
-            pltpu.VMEM((nd, 16, D), BF16),
+            pltpu.VMEM((2, nd // 2, 16, D), BF16),
             pltpu.VMEM((48, D), BF16),
             pltpu.VMEM((rows, nd * LANE), BF16),
             pltpu.VMEM((rows, D), F32),
@@ -1211,6 +1330,12 @@
             pltpu.VMEM((table_total // HASH * cols, HASH), F32),
             pltpu.VMEM((8, LANE), F32),
             pltpu.VMEM((nd, 8, LANE), F32),
+            pltpu.SemaphoreType.DMA((cap,)),
+            pltpu.SemaphoreType.DMA((n_valid,)),
+            pltpu.SemaphoreType.DMA((2,)),
+            pltpu.SemaphoreType.DMA((2,)),
+            pltpu.SemaphoreType.DMA((7,)),
+            pltpu.SemaphoreType.DMA(()),
             pltpu.SemaphoreType.DMA((flows,)),
             pltpu.SemaphoreType.DMA((flows,)),
             pltpu.SemaphoreType.DMA((flows,)),
@@ -1251,11 +1376,12 @@
 
 
 def first_body(
-    n_valid, nq, nd, narrow, cols, home_at, blocks, forward_from,
+    n_valid, nq, nd, narrow, cols, home_at, blocks, plan,
     ids_mine, small_mine, table, win, wout, pos_mine,
     ids_got, small_got, mine, mine_q, wall, w0,
     stacked, tokens, tokens_q, p0,
-    send_sem, recv_sem, own_sem, wide_send, wide_recv, x_send, x_recv, c_send, c_recv,
+    send_sem, recv_sem, own_sem, up_send, down_send, z_recv, y_send, y_recv, x_send, x_recv,
+    c_send, c_recv,
 ):
     cap = -(-n_valid // nd)
     wide = nd // narrow
@@ -1265,8 +1391,14 @@
     me = net.me
     w_at, n_at = lax.axis_index("wide"), lax.axis_index("narrow")
     x_at, c_at = n_at ^ 2, n_at ^ 1
-    everyone = (0, nd)
-    home = (home_at, home_at + 1)
+    everyone = group(nd, nd)
+    home = (home_at, 1, 1)
+
+    def span(c):
+        return group(nd, nd) if c == 0 else group(n_valid - nd, nd, 1)
+
+    def slot_of(c, d):
+        return c * nd + place(d, span(c))
 
     wall[w_at, n_at] = jnp.concatenate([win[1], wout[1], pos_mine[...]], axis=1).astype(BF16)
     p0[...] = jnp.concatenate([win[0], wout[0]], axis=1).astype(BF16)
@@ -1284,42 +1416,69 @@
     ]
     small_base = net.start(small)
 
-    def wide_copy(k, carry):
-        t = lax.rem(w_at + k, wide)
+    tall = wide // 2
+    z_at, y_at = w_at // 2, lax.rem(w_at, 2)
+
+    def pass_on(row, col, w_to, n_to, sent, got):
         pltpu.make_async_remote_copy(
-            src_ref=wall.at[w_at, n_at], dst_ref=wall.at[w_at, n_at],
-            send_sem=wide_send, recv_sem=wide_recv.at[w_at],
-            device_id=(t, n_at), device_id_type=MESH,
+            src_ref=wall.at[row, col], dst_ref=wall.at[row, col], send_sem=sent, recv_sem=got,
+            device_id=(w_to, n_to), device_id_type=MESH,
         ).start()
-        return carry
-
-    lax.fori_loop(1, wide, wide_copy, 0)
-
-    def to_x(row):
-        return pltpu.make_async_remote_copy(
-            src_ref=wall.at[row, n_at], dst_ref=wall.at[row, n_at],
-            send_sem=x_send, recv_sem=x_recv.at[row],
-            device_id=(w_at, x_at), device_id_type=MESH,
-        )
-
-    def to_core(row, col, which):
-        return pltpu.make_async_remote_copy(
-            src_ref=wall.at[row, col], dst_ref=wall.at[row, col],
-            send_sem=c_send, recv_sem=c_recv.at[which, row],
-            device_id=(w_at, c_at), device_id_type=MESH,
-        )
-
-    def forward(k):
-        row = lax.rem(w_at - k + wide, wide)
-
-        @pl.when(k > 0)
+
+    def await_piece(row, col, sem):
+        pltpu.make_async_copy(wall.at[row, col], wall.at[row, col], sem).wait()
+
+    def up(z):
+        @pl.when(z_at < tall - 1)
         def _():
-            pltpu.make_async_copy(
-                wall.at[row, n_at], wall.at[row, n_at], wide_recv.at[row]
-            ).wait()
-
-        to_x(row).start()
-        to_core(row, n_at, 0).start()
+            pass_on(2 * z + y_at, n_at, w_at + 2, n_at, up_send.at[z], z_recv.at[z])
+
+    def down(z):
+        @pl.when(z_at > 0)
+        def _():
+            pass_on(2 * z + y_at, n_at, w_at - 2, n_at, down_send.at[z], z_recv.at[z])
+
+    def across(row):
+        pass_on(row, n_at, w_at, x_at, x_send, x_recv.at[row])
+        pass_on(row, n_at, w_at, c_at, c_send, c_recv.at[0, row])
+
+    def around(z):
+        pass_on(2 * z + y_at, n_at, w_at ^ 1, n_at, y_send, y_recv.at[z])
+        across(2 * z + y_at)
+
+    def z_step(k):
+        for z, onward in ((z_at - k, up), (z_at + k, down)):
+
+            @pl.when(jnp.logical_and(z >= 0, z < tall))
+            def _():
+                await_piece(2 * z + y_at, n_at, z_recv.at[z])
+                onward(z)
+                around(z)
+
+    def y_step(z):
+        row = 2 * z + (y_at ^ 1)
+        await_piece(row, n_at, y_recv.at[z])
+        across(row)
+
+    def x_step(row):
+        await_piece(row, x_at, x_recv.at[row])
+        pass_on(row, x_at, w_at, c_at, c_send, c_recv.at[1, row])
+
+    def forward(step):
+        if step < tall:
+            z_step(step)
+        elif step < 2 * tall:
+            y_step(lax.rem(z_at + step - tall, tall))
+        else:
+            k = step - 2 * tall
+            row = 2 * lax.rem(z_at + k, tall) + y_at if k < tall else (
+                2 * lax.rem(z_at + k, tall) + (y_at ^ 1)
+            )
+            x_step(row)
+
+    up(z_at)
+    down(z_at)
+    around(z_at)
 
     stack_table(cols, blocks, table, stacked)
     net.finish(small, small_base)
@@ -1327,10 +1486,10 @@
     pairs = n_valid // n_own
     moves = [
         Flow(
-            lambda s, t, c=c: tokens.at[(c * nd + t) // n_own, lax.rem(c * nd + t, n_own)],
+            lambda s, t, c=c: tokens.at[slot_of(c, t) // n_own, lax.rem(slot_of(c, t), n_own)],
             lambda s, t, c=c: mine.at[s, :, pl.ds(c * LP, LP)],
             lambda n: mine.at[pl.ds(0, n), :, pl.ds(0, LP)],
-            everyone, (0, min(nd, n_valid - c * nd)),
+            everyone, span(c),
         )
         for c in range(cap)
     ]
@@ -1341,7 +1500,8 @@
         for j in range(n_own):
             slot = at * n_own + j
             c = slot // nd
-            t = lax.rem(slot, nd)
+            far = span(1)
+            t = jnp.where(c == 0, slot, far[0] + far[1] * (slot - nd))
             dst = mine.at[me, :, pl.ds(pl.multiple_of(c * LP, LANE), LP)]
 
             @pl.when(t != me)
@@ -1367,9 +1527,12 @@
         def _():
             send_pair(lax.rem(i - 1 + me, pairs))
 
-        @pl.when(jnp.logical_and(i >= forward_from, i < forward_from + wide))
-        def _():
-            forward(i - forward_from)
+        for step, turn in enumerate(plan):
+            if 0 < step and turn < pairs:
+
+                @pl.when(i == turn)
+                def _():
+                    forward(step)
 
         return carry
 
@@ -1393,17 +1556,9 @@
     home_base = net.start(home_moves)
     lax.fori_loop(0, pairs, gather, 0)
     send_pair(lax.rem(pairs - 1 + me, pairs))
-    for k in range(wide):
-        if forward_from + k >= pairs:
-            forward(k)
-
-    def second(k, carry):
-        row = lax.rem(w_at - k + wide, wide)
-        pltpu.make_async_copy(wall.at[row, x_at], wall.at[row, x_at], x_recv.at[row]).wait()
-        to_core(row, x_at, 1).start()
-        return carry
-
-    lax.fori_loop(0, wide, second, 0)
+    for step, turn in enumerate(plan):
+        if 0 < step and turn >= pairs:
+            forward(step)
     net.finish(moves, base)
     net.finish(q_moves, q_base)
     net.finish(home_moves, home_base)
@@ -1416,15 +1571,25 @@
         return carry
 
     lax.fori_loop(0, wide, last, 0)
-    many = wall.at[pl.ds(0, wide - 1), 0]
-    pltpu.make_async_copy(many, many, wide_send).wait()
+    for z in range(tall):
+        for hop, ok in (
+            (up_send, jnp.logical_and(z_at < tall - 1, z <= z_at)),
+            (down_send, jnp.logical_and(z_at > 0, z >= z_at)),
+        ):
+
+            @pl.when(ok)
+            def _():
+                await_piece(0, 0, hop.at[z])
+
+    many = wall.at[pl.ds(0, tall), 0]
+    pltpu.make_async_copy(many, many, y_send).wait()
     many = wall.at[:, 0]
     pltpu.make_async_copy(many, many, x_send).wait()
     many = wall.at[:, pl.ds(0, 2)]
     pltpu.make_async_copy(many, many, c_send).wait()
 
 
-def first(n_valid, nq, nd, narrow, cols, home_at, arrays, forward_from):
+def first(n_valid, nq, nd, narrow, cols, home_at, arrays, plan):
     cap = -(-n_valid // nd)
     wide = nd // narrow
     tq = nq * LQ
@@ -1440,7 +1605,7 @@
     dma = pltpu.SemaphoreType.DMA
     return pl.pallas_call(
         functools.partial(
-            first_body, n_valid, nq, nd, narrow, cols, home_at, blocks, forward_from
+            first_body, n_valid, nq, nd, narrow, cols, home_at, blocks, plan
         ),
         out_shape=[
             like(nd, *ids_mine.shape, dtype=jnp.int32),
@@ -1458,7 +1623,8 @@
             pltpu.VMEM((cols, tq), BF16),
             pltpu.VMEM((cols, 4 * D), BF16),
             dma((flows,)), dma((flows,)), dma((flows,)),
-            dma(()), dma((wide,)), dma(()), dma((wide,)), dma(()), dma((2, wide)),
+            dma((wide // 2,)), dma((wide // 2,)), dma((wide // 2,)), dma(()), dma((wide // 2,)),
+            dma(()), dma((wide,)), dma(()), dma((2, wide)),
         ],
         compiler_params=pltpu.CompilerParams(
             collective_id=2, has_side_effects=True, vmem_limit_bytes=62 * 1024 * 1024
@@ -1838,7 +2004,7 @@
     attend_out_first, attend_out_second, expand_first, expand_second,
     shrink_first, shrink_second, gains_first, gains_second, bias_first, bias_second,
 ):
-    if embed_table.shape[1] % 8 != 0 or lax.axis_size("narrow") != 4 or passage_ids.shape[0] != 2:
+    if embed_table.shape[1] % 8 != 0 or lax.axis_size("narrow") != 4 or lax.axis_size("wide") != 8 or passage_ids.shape[0] != 2:
         return on_device_rows(
             passage_ids, query_ids, passage_query, kept_mask, neg_count, step_count,
             embed_table, attend_in, attend_out, expand_weight, shrink_weight, norm_gains,
@@ -1878,15 +2044,12 @@
     ids_got, small_got, mine, mine_q, w_one, w_zero = first(
         n_valid, nq, nd, narrow, cols, query_home,
         [ids_mine, small_mine, table_t, attend_in, attend_out, table_t[:, V : V + LP]],
-        12,
+        FORWARD_PLAN,
     )
     w_one = w_one.reshape(D, 4 * D + LP)
     w_zero = w_zero.reshape(D, 4 * D)
     pid = ids_got[:, :n_own, :LP].reshape(n_slots, LP)[:n_valid]
     qid = jnp.sum(ids_got[:, n_own, :tq], axis=0)
-    q_from = n_valid * LP
-    token_total = -(-(q_from + tq) // 1024) * 1024
-    all_ids = jnp.pad(jnp.concatenate([pid.reshape(-1), qid]), (0, token_total - q_from - tq))
     gains = small_got[:, :6, :cols].transpose(1, 0, 2).reshape(2, 3, D).astype(F32)
     bias = small_got[:, 6:, : bias_terms.shape[1]].transpose(1, 0, 2).reshape(2, -1).astype(F32)
 
@@ -1918,14 +2081,16 @@
         ((0, 5), (0, -(-n_valid // LANE) * LANE - n_valid)),
     )
     shrink_g, loss, g_table, g_in, g_out, g_up, g_bin, g_small, norm = middle(
-        n_valid, nq, nd, narrow, cols, query_home, token_total,
+        n_valid, nq, nd, narrow, cols, query_home,
         [mine, mine_q, w_one, w_zero, up_mine, w_down, cv, rv, b_in, slots,
-         all_ids.reshape(-1, 1, 1024)],
+         pid.reshape(n_valid, 1, LP), qid.reshape(1, tq)],
     )
     loss = loss[0, 0]
     grad_norm = norm[0, 0]
     g_small = g_small.reshape(2, 16, D)
-    g_bin = g_bin[:2].reshape(2, nd, LANE)[:, :, :ff_cols].reshape(2, FF)
+    g_bin = g_bin[:2].reshape(2, 2, nd // 2, LANE)[..., :ff_cols]
+    g_bin = g_bin.transpose(0, 2, 1, 3).reshape(2, FF)
+    g_up = g_up.reshape(2, cols, 2, nd // 2, LANE)[..., :ff_cols].transpose(0, 1, 3, 2, 4)
     bias_grad = jnp.concatenate(
         [g_small[:, :4].reshape(2, 4 * D), g_bin, g_small[:, 4:7].reshape(2, 3 * D)], axis=1
     )
@@ -1933,7 +2098,7 @@
         g_table[:, : V + LP].T,
         g_in,
         g_out,
-        g_up.reshape(2, cols, nd, LANE)[..., :ff_cols].reshape(2, cols, FF),
+        g_up.reshape(2, cols, FF),
         shrink_g[:, :ff_cols],
         lax.dynamic_slice_in_dim(g_small[:, 7:10], me * cols, cols, 2),
         lax.dynamic_slice_in_dim(bias_grad, me * bias_terms.shape[1], bias_terms.shape[1], 1),

time: 271 us -> 245 us (0.904)
  Pallas kernels: 232 us -> 205 us
    pallas_call x1, Pallas kernels: 153 us -> 130 us  [middle(): pl.pallas_call(functools.partial(middle_body, n_valid, nq, nd, narrow, co...]
    pallas_call x1, Pallas kernels: 78.7 us -> 74.1 us  [first(): pl.pallas_call(functools.partial(first_body, n_valid, nq, nd, narrow, col...]
where the time goes in v3:
time: 245 us; the launch traced here: 244 us
  Pallas kernels  205 us (84%)
  other arithmetic  20.4 us (8%)
  local copies, waits for them, and re-layouts  17 us (7%)
  between operations  2.45 us (1%)
    pallas_call x1, Pallas kernels, middle(): pl.pallas_call(functools.partial(middle_body, n_valid, nq, nd, narrow, co...  130 us
    pallas_call x1, Pallas kernels, first(): pl.pallas_call(functools.partial(first_body, n_valid, nq, nd, narrow, col...  74.1 us
    sub x7, other arithmetic, adam_update(): weight - rate * (first_hat / (jnp.sqrt(second_hat) + ADAM_EPS) + WEIGHT_D...  13.5 us

profile of v3, /device:TPU:0, one launch (start us, length us, event | category | flops | bytes accessed | tf_op | source)
XLA Modules:
  0.0 244.4 jit_solution(9116189449607218852)
XLA Ops:
  0.7 0.7 tile.11
  1.3 0.1 tile.12
  1.4 1.3 pad_add_fusion.ids_mine
  2.7 1.5 slice.155.pos_mine
  4.2 0.7 convert.16
  4.9 0.7 convert.17
  5.6 0.6 fusion.9.small_mine
  6.2 74.1 %first.1 = (s32[32,3,384]{2,1,0:T(4,128)}, bf16[32,8,384]{2,1,0:T(8,128)(2,1)}, bf16[32,24,768]{2,1,0:T(8,128)(2,1)}, bf16[32,24,256]{2,1,0:T(8,128)(2,1)}, bf16...) custom-call(s32[3,384]{1,0:T(4,128)} %pad_add_fusion.ids_mine, bf16[8,384]{1,0:T(8,128)(2,1)} %fusion.9.small_mine, ...), custom_call_target="tpu_custom_call" | custom-call | tf_op jit(solution)/shard_map/first/pallas_call | solution.py:1606
  80.3 1.0 convert_bitcast_fusion.1
  81.3 0.2 reshape.171
  81.5 0.9 convert_bitcast_fusion
  82.4 0.1 reshape.170
  82.5 1.3 stack.26.rv
  83.9 0.9 copy.74.cv
  84.8 0.1 reshape.161
  84.9 0.6 pad.35.b_in
  85.5 0.9 slice.143
  86.4 0.7 reshape.162.ids
  87.2 1.5 slice_reduce_fusion
  88.7 0.0 copy-start.17
  88.8 0.4 reshape.160
  89.1 0.2 copy.93
  89.3 0.8 pad.33.up_mine
  90.2 0.8 pad.34.w_down
  90.9 0.1 fusion.15
  91.0 0.6 pad.36.slots
  91.6 0.0 copy-start.20
  91.6 0.0 copy-start.21
  91.7 130.4 %middle.1 = (f32[2,128,768]{2,1,0:T(8,128)}, f32[8,128]{1,0:T(8,128)}, f32[24,18432]{1,0:T(8,128)}, f32[2,24,2304]{2,1,0:T(8,128)}, f32[2,24,768]{2,1,0:T(8,128)...) custom-call(bf16[32,24,768]{2,1,0:T(8,128)(2,1)} %get-tuple-element.38.mine, ...), custom_call_target="tpu_custom_call" | custom-call | tf_op jit(solution)/shard_map/middle/pallas_call | solution.py:1273
  222.1 0.9 slice_bitcast_fusion.1
  223.1 0.1 reshape.168
  223.2 1.0 slice_bitcast_fusion.2
  224.2 0.8 slice_bitcast_fusion.3
  225.0 1.2 slice.146
  227.7 0.7 multiply_subtract_fusion.4
  228.4 0.1 constant_dynamic-slice_fusion
  228.5 0.6 add_subtract_fusion.1
  229.1 2.8 %multiply_subtract_fusion = (f32[2,96,768]{2,1,0:T(8,128)}, f32[2,96,768]{2,1,0:T(8,128)}, f32[2,96,768]{2,1,0:T(8,128)}) fusion(f32[2,96,768]{2,1,0:T(8,128)S(1)} %copy-done.1, f32[]{:T(128)} %bitcast.26, f32[]{:T(128)} %bitcast.25, f32[]{:T(128)S(6)} %div.104, f32[2,128,768]{2,1,0:T(8,128)} %get-tuple-element.50, f32[2,96,768]{2,1,0:T(8,128)S(1)} %copy-done.8, ...), kind=kLoop, calls=%fused_computation.13 | loop fusion | flops 2359296 | bytes 4128780 | tf_op jit(solution)/shard_map/sub | solution.py:66
  231.9 0.1 copy.81
  232.0 0.1 fusion.2
  232.1 0.0 copy-start.9
  232.1 0.4 copy.75
  232.5 1.1 mul.365
  233.7 1.5 multiply_subtract_fusion.1
  235.2 2.2 multiply_subtract_fusion.3
  237.4 2.5 %multiply_subtract_fusion.2 = (f32[2,24,2304]{2,1,0:T(8,128)}, f32[2,24,2304]{2,1,0:T(8,128)}, f32[2,24,2304]{2,1,0:T(8,128)}) fusion(f32[2,24,2304]{2,1,0:T(8,128)S(1)} %copy-done.6, f32[]{:T(128)} %bitcast.26, f32[]{:T(128)} %bitcast.25, f32[2,24,2304]{2,1,0:T(8,128)} %get-tuple-element.47, f32[]{:T(128)S(6)} %div.104, f32[2,24,2304]{2,1,0:T(8,128)S(1)} %copy-done.12, ...), kind=kLoop, calls=%fused_computation.19 | loop fusion | flops 1769472 | bytes 3096588 | tf_op jit(solution)/shard_map/sub | solution.py:66
  240.0 3.2 %add_subtract_fusion = (f32[18384,24]{0,1:T(8,128)}, f32[18384,24]{0,1:T(8,128)}, f32[18384,24]{0,1:T(8,128)}) fusion(f32[18384,24]{0,1:T(8,128)S(1)} %copy-done, f32[]{:T(128)} %bitcast.26, f32[]{:T(128)} %bitcast.25, f32[]{:T(128)S(6)} %div.104, f32[24,18432]{1,0:T(8,128)S(1)} %copy-done.5, f32[18384,24]{0,1:T(8,128)S(1)} %copy-done.3, ...), kind=kLoop, calls=%fused_computation.4 | loop fusion | flops 6618240 | bytes 12354060 | tf_op jit(solution)/shard_map/sub | solution.py:66
  243.2 1.2 slice.145
  (62 shorter events, 0.4 us)
Async XLA Ops:
  6.2 82.5 %copy-start.2 = (f32[2,24,3072]{2,1,0:T(8,128)S(1)}, f32[2,24,3072]{2,1,0:T(8,128)}, u32[]{:S(2)}) copy-start(f32[2,24,3072]{2,1,0:T(8,128)} %param.35) | copy-start | bytes 1769476
  84.8 5.3 %copy-start.1 = (f32[2,96,768]{2,1,0:T(8,128)S(1)}, f32[2,96,768]{2,1,0:T(8,128)}, u32[]{:S(2)}) copy-start(f32[2,96,768]{2,1,0:T(8,128)} %param.36) | copy-start | bytes 1769476
  88.7 2.2 copy-start.17
  88.7 2.3 copy-start.22
  91.6 136.0 %copy-start.15 = (f32[2,264]{1,0:T(2,128)S(1)}, f32[2,264]{1,0:T(2,128)}, u32[]{:S(2)}) copy-start(f32[2,264]{1,0:T(2,128)} %param.38) | copy-start | bytes 6340
  91.6 136.0 %copy-start.18 = (f32[2,264]{1,0:T(2,128)S(1)}, f32[2,264]{1,0:T(2,128)}, u32[]{:S(2)}) copy-start(f32[2,264]{1,0:T(2,128)} %param.52) | copy-start | bytes 6340
  91.6 136.0 %copy-start.19 = (f32[2,264]{1,0:T(2,128)S(1)}, f32[2,264]{1,0:T(2,128)}, u32[]{:S(2)}) copy-start(f32[2,264]{1,0:T(2,128)} %param.51) | copy-start | bytes 6340
  91.6 136.8 %copy-start.16 = (f32[2,3,24]{2,0,1:T(2,128)S(1)}, f32[2,3,24]{2,0,1:T(2,128)}, u32[]{:S(2)}) copy-start(f32[2,3,24]{2,0,1:T(2,128)} %param.37) | copy-start | bytes 1732
  91.6 136.8 %copy-start.20 = (f32[2,3,24]{2,0,1:T(2,128)S(1)}, f32[2,3,24]{2,0,1:T(2,128)}, u32[]{:S(2)}) copy-start(f32[2,3,24]{2,0,1:T(2,128)} %param.50) | copy-start | bytes 1732
  91.6 136.8 %copy-start.21 = (f32[2,3,24]{2,0,1:T(2,128)S(1)}, f32[2,3,24]{2,0,1:T(2,128)}, u32[]{:S(2)}) copy-start(f32[2,3,24]{2,0,1:T(2,128)} %param.49) | copy-start | bytes 1732
  91.7 137.4 %copy-start.8 = (f32[2,96,768]{2,1,0:T(8,128)S(1)}, f32[2,96,768]{2,1,0:T(8,128)}, u32[]{:S(2)}) copy-start(f32[2,96,768]{2,1,0:T(8,128)} %param.48) | copy-start | bytes 1769476
  229.1 2.8 %copy-start.7 = (f32[48,4096]{1,0:T(8,128)S(1)}, f32[48,4096]{1,0:T(8,128)}, u32[]{:S(2)}) copy-start(f32[48,4096]{1,0:T(8,128)} %get-tuple-element.49) | copy-start | bytes 2359300
  232.1 1.5 copy-start.9
  232.1 1.5 copy-start.10
  232.5 2.6 %copy-start.13 = (f32[2,24,768]{2,1,0:T(8,128)S(1)}, f32[2,24,768]{2,1,0:T(8,128)}, u32[]{:S(2)}) copy-start(f32[2,24,768]{2,1,0:T(8,128)} %param.44) | copy-start | bytes 442372
  232.5 2.6 %copy-start.14 = (f32[2,24,768]{2,1,0:T(8,128)S(1)}, f32[2,24,768]{2,1,0:T(8,128)}, u32[]{:S(2)}) copy-start(f32[2,24,768]{2,1,0:T(8,128)} %param.43) | copy-start | bytes 442372
  233.6 1.5 copy-start.11
  233.6 3.8 %copy-start.6 = (f32[2,24,2304]{2,1,0:T(8,128)S(1)}, f32[2,24,2304]{2,1,0:T(8,128)}, u32[]{:S(2)}) copy-start(f32[2,24,2304]{2,1,0:T(8,128)} %win.1) | copy-start | bytes 1327108
  233.7 3.8 %copy-start.12 = (f32[2,24,2304]{2,1,0:T(8,128)S(1)}, f32[2,24,2304]{2,1,0:T(8,128)}, u32[]{:S(2)}) copy-start(f32[2,24,2304]{2,1,0:T(8,128)} %param.42) | copy-start | bytes 1327108
  233.7 6.3 %copy-start.4 = (f32[18384,24]{0,1:T(8,128)S(1)}, f32[18384,24]{0,1:T(8,128)}, u32[]{:S(2)}) copy-start(f32[18384,24]{0,1:T(8,128)} %param.39) | copy-start | bytes 5294596
  233.7 6.3 %copy-start.5 = (f32[24,18432]{1,0:T(8,128)S(1)}, f32[24,18432]{1,0:T(8,128)}, u32[]{:S(2)}) copy-start(f32[24,18432]{1,0:T(8,128)} %get-tuple-element.46) | copy-start | bytes 5308420
  235.2 4.8 %copy-start.3 = (f32[18384,24]{0,1:T(8,128)S(1)}, f32[18384,24]{0,1:T(8,128)}, u32[]{:S(2)}) copy-start(f32[18384,24]{0,1:T(8,128)} %param.40) | copy-start | bytes 5294596
  237.4 2.6 %copy-start = (f32[18384,24]{0,1:T(8,128)S(1)}, f32[18384,24]{0,1:T(8,128)}, u32[]{:S(2)}) copy-start(f32[18384,24]{0,1:T(8,128)} %param.32) | copy-start | bytes 5294596

commit v4 on v3

--- a/solution.py
+++ b/solution.py
@@ -393,7 +393,7 @@
 
 
 def place(index, span):
-    return (index - span[0]) // span[1]
+    return (index - span[0]) >> (span[1].bit_length() - 1)
 
 
 class Flow:
@@ -410,13 +410,13 @@
         self.used = 0
 
     def where(self, t):
-        return (t // self.narrow, lax.rem(t, self.narrow))
+        return (t >> (self.narrow.bit_length() - 1), t & (self.narrow - 1))
 
     def barrier(self):
         sem = pltpu.get_barrier_semaphore()
 
         def greet(k, carry):
-            t = lax.rem(self.me + k, self.nd)
+            t = (self.me + k) & (self.nd - 1)
             pl.semaphore_signal(sem, inc=1, device_id=self.where(t), device_id_type=MESH)
             return carry
 
@@ -429,7 +429,7 @@
         self.used += len(flows)
 
         def push(k, carry):
-            t = lax.rem(me + k, nd)
+            t = (me + k) & (nd - 1)
             for i, f in enumerate(flows):
 
                 @pl.when(jnp.logical_and(within(me, f.sources), within(t, f.targets)))
@@ -589,7 +589,7 @@
 
 def middle_body(
     n_valid, nq, nd, narrow, cols, query_home,
-    mine, mine_q, w_one, w_zero, up_mine, w_down, cv, rv, b_in, slots, ids, ids_q,
+    mine, mine_q, w_one, w_zero, up_mine, shrink, small, slots, ids,
     o_shrink, o_loss, g_table, g_in, g_out, g_up, g_bin, g_small, o_norm,
     hat_s, scale_s, xl_s, xf_s, q_s, k_s, v_s, p_s, a_s,
     hat_q, scale_q, xl_q, xf_q, q_q, k_q, v_q, p_q, a_q,
@@ -597,6 +597,7 @@
     du_own, du_f, gtok, gtok_q, fac, fac_q, line, line_q, f_s, slope_s, hlow_s, g_top_s, sums_s,
     o_tok, o_fac, o_facq, o_line, o_lineq, o_du, o_h, up_got, w_up,
     t_all, w_all, q_exp, d_exp, spread_s, acc_s, norm_own, norm_all,
+    w_down, bias_s, gain_s, rows_s, cv, rv, b_in,
     tok_send, tok_recv, twin_send, twin_recv, chain_send, chain_recv,
     send_sem, recv_sem, own_sem,
 ):
@@ -628,6 +629,35 @@
         )
     ]
     up_base = net.start(up_flows)
+
+    ff_cols = shrink.shape[1]
+    bias_cols = (5 * D + FF + 2 * D) // nd
+    bias_s[...] = jnp.zeros_like(bias_s)
+    gain_s[...] = jnp.zeros_like(gain_s)
+    span_b, span_g = small.shape[2] + LANE, 2 * LANE
+    for d in range(nd):
+        block = small[d].astype(F32)
+        wide_block = jnp.concatenate([block, jnp.zeros((8, LANE), F32)], axis=1)
+        at, turn = bias_cols * d // LANE * LANE, bias_cols * d % LANE
+        bias_s[:, at : at + span_b] += pltpu.roll(wide_block, turn, 1) if turn else wide_block
+        at, turn = cols * d // LANE * LANE, cols * d % LANE
+        near = block[:, 0:span_g]
+        gain_s[:, at : at + span_g] += pltpu.roll(near, turn, 1) if turn else near
+    rows_s[...] = jnp.zeros_like(rows_s)
+    w_down[...] = jnp.zeros_like(w_down)
+    inner = pltpu.roll(bias_s[:, O_IN : O_IN + FF], jnp.where(me == 0, 0, FF - ff_cols * me), 1)
+    inner = jnp.where(iota((8, LANE), 1) < ff_cols, inner[:, 0:LANE], 0.0)
+    for e in range(2):
+        for j, at in enumerate((O_Q, O_O, O_1, O_OUT, O_2)):
+            rv[8 * e + j : 8 * e + j + 1, :] = bias_s[6 + e : 7 + e, at : at + D]
+        for j in (1, 2):
+            rv[8 * e + 4 + j : 8 * e + 5 + j, :] = gain_s[3 * e + j : 3 * e + j + 1, 0:D]
+        rows_s[3 * e : 3 * e + 1, :] = gain_s[3 * e : 3 * e + 1, 0:D]
+        rows_s[3 * e + 1 : 3 * e + 2, :] = bias_s[6 + e : 7 + e, O_EMB : O_EMB + D]
+        rows_s[3 * e + 2 : 3 * e + 3, :] = bias_s[6 + e : 7 + e, O_V : O_V + D]
+        b_in[e : e + 1, :] = inner[6 + e : 7 + e, :]
+        w_down[e, 0:ff_cols, :] = shrink[e].astype(BF16)
+    cv[...] = jnp.transpose(rows_s[...])
 
     def front(c, carry):
         at = pl.ds(pl.multiple_of(c * LP, LANE), LP)
@@ -819,7 +849,7 @@
         Flow(
             lambda s, t: du_own,
             lambda s, t: o_du.at[
-                :, pl.ds(pl.multiple_of(((s & 1) * (nd // 2) + s // 2) * LANE, LANE), LANE)
+                :, pl.ds(pl.multiple_of(((s & 1) * (nd // 2) + (s >> 1)) * LANE, LANE), LANE)
             ],
             lambda n: o_du.at[:, pl.ds(0, n * LANE)],
             alike, alike,
@@ -931,13 +961,13 @@
     row_flows = [
         Flow(
             lambda s, t: line_q.at[pl.ds(0, 16), :],
-            lambda s, t: o_line.at[s & 1, s // 2],
+            lambda s, t: o_line.at[s & 1, s >> 1],
             lambda n: o_line.at[0, pl.ds(0, n)],
             alike, alike,
         ),
     ]
     plane, home_core = query_home // 8, query_home % 2
-    z_at = me // 8
+    z_at = me >> 3
     on_core = core == home_core
     query_rows = line_q.at[pl.ds(16, 48), :]
 
@@ -990,7 +1020,7 @@
         return o_tok.at[:, pl.ds(pl.multiple_of(slot * LP, LANE), LP)]
 
     def push_tokens(k, carry):
-        t = lax.rem(me + k, nd)
+        t = (me + k) & (nd - 1)
         for c in range(cap):
 
             @pl.when(within(me, span(c)))
@@ -1062,7 +1092,7 @@
     to_twin(o_line.at[core], 1).wait()
 
     def expand(d, carry):
-        both = o_line[d & 1, d // 2].astype(F32)
+        both = o_line[d & 1, d >> 1].astype(F32)
         for c in range(2):
             at = pl.ds(pl.multiple_of(32 * d + 16 * c, 16), 16)
             q_exp[at, :] = (both[c : c + 1, :] * mask16).astype(BF16)
@@ -1074,7 +1104,7 @@
     row, col = iota((272, nd * 16), 0), iota((272, nd * 16), 1)
     kind = col & 15
     at_block = col >> 4
-    device = (at_block & (half - 1)) * 2 + (at_block // half)
+    device = (at_block & (half - 1)) * 2 + (at_block >> (half.bit_length() - 1))
     pair = device * 2 + (col & 1)
     dq_rows = jnp.logical_and(row < 128, jnp.logical_and((kind >> 1) == 2, pair == row))
     do_rows = jnp.logical_and(
@@ -1170,24 +1200,30 @@
             pltpu.make_async_copy(tok_view(slot), tok_view(slot), tok_recv.at[slot]).wait()
         values = [tok_view(slot)[...].astype(F32) for slot in slots_now]
         add_tokens(
-            jnp.concatenate([ids[slot] for slot in slots_now], axis=1),
+            jnp.concatenate(
+                [ids[slot >> 1, pl.ds(slot & 1, 1), 0:LP] for slot in slots_now], axis=1
+            ),
             jnp.concatenate(values, axis=1),
         )
 
     def add_near(k, carry):
-        add_slots([lax.rem(me - 2 * k - j + nd, nd) for j in range(2)])
+        add_slots([(me - 2 * k - j) & (nd - 1) for j in range(2)])
         return carry
 
     def add_far(k, carry):
         extra = n_valid - nd
-        first = me // (nd // extra)
-        add_slots([nd + lax.rem(first - 2 * k - j + 2 * extra, extra) for j in range(2)])
+        first = me >> 2
+        add_slots([nd + ((first - 2 * k - j) & (extra - 1)) for j in range(2)])
         return carry
 
     lax.fori_loop(0, nd // 2, add_near, 0)
     lax.fori_loop(0, (n_valid - nd) // 2, add_far, 0)
     net.finish(flows[:1], base)
-    add_tokens(ids_q[...], o_tok[:, n_valid * LP : n_valid * LP + nq * LQ].astype(F32))
+    tq = nq * LQ
+    ids_q = jnp.zeros((1, tq), jnp.int32)
+    for d in range(0, nd, narrow):
+        ids_q = ids_q + ids[d, 2:3, 0:tq]
+    add_tokens(ids_q, o_tok[:, n_valid * LP : n_valid * LP + nq * LQ].astype(F32))
     for c in range(cap):
 
         @pl.when(within(me, span(c)))
@@ -1330,6 +1366,13 @@
             pltpu.VMEM((table_total // HASH * cols, HASH), F32),
             pltpu.VMEM((8, LANE), F32),
             pltpu.VMEM((nd, 8, LANE), F32),
+            pltpu.VMEM((2, LANE, D), BF16),
+            pltpu.VMEM((8, 7 * D + FF + 4 * LANE), F32),
+            pltpu.VMEM((8, D + 2 * LANE), F32),
+            pltpu.VMEM((LANE, D), F32),
+            pltpu.VMEM((D, LANE), F32),
+            pltpu.VMEM((16, D), F32),
+            pltpu.VMEM((8, LANE), F32),
             pltpu.SemaphoreType.DMA((cap,)),
             pltpu.SemaphoreType.DMA((n_valid,)),
             pltpu.SemaphoreType.DMA((2,)),
@@ -1417,7 +1460,7 @@
     small_base = net.start(small)
 
     tall = wide // 2
-    z_at, y_at = w_at // 2, lax.rem(w_at, 2)
+    z_at, y_at = w_at >> 1, w_at & 1
 
     def pass_on(row, col, w_to, n_to, sent, got):
         pltpu.make_async_remote_copy(
@@ -1468,17 +1511,24 @@
         if step < tall:
             z_step(step)
         elif step < 2 * tall:
-            y_step(lax.rem(z_at + step - tall, tall))
+            y_step((z_at + step - tall) & (tall - 1))
         else:
             k = step - 2 * tall
-            row = 2 * lax.rem(z_at + k, tall) + y_at if k < tall else (
-                2 * lax.rem(z_at + k, tall) + (y_at ^ 1)
+            row = 2 * ((z_at + k) & (tall - 1)) + y_at if k < tall else (
+                2 * ((z_at + k) & (tall - 1)) + (y_at ^ 1)
             )
             x_step(row)
 
     up(z_at)
     down(z_at)
     around(z_at)
+    home_moves = [
+        Flow(
+            lambda s, t: p0, lambda s, t: w0.at[s],
+            lambda n: w0.at[pl.ds(0, n)], everyone, home,
+        ),
+    ]
+    home_base = net.start(home_moves)
 
     stack_table(cols, blocks, table, stacked)
     net.finish(small, small_base)
@@ -1486,7 +1536,7 @@
     pairs = n_valid // n_own
     moves = [
         Flow(
-            lambda s, t, c=c: tokens.at[slot_of(c, t) // n_own, lax.rem(slot_of(c, t), n_own)],
+            lambda s, t, c=c: tokens.at[slot_of(c, t) >> 1, slot_of(c, t) & 1],
             lambda s, t, c=c: mine.at[s, :, pl.ds(c * LP, LP)],
             lambda n: mine.at[pl.ds(0, n), :, pl.ds(0, LP)],
             everyone, span(c),
@@ -1499,7 +1549,7 @@
     def send_pair(at):
         for j in range(n_own):
             slot = at * n_own + j
-            c = slot // nd
+            c = (slot >= nd).astype(jnp.int32)
             far = span(1)
             t = jnp.where(c == 0, slot, far[0] + far[1] * (slot - nd))
             dst = mine.at[me, :, pl.ds(pl.multiple_of(c * LP, LANE), LP)]
@@ -1516,8 +1566,14 @@
             def _():
                 pltpu.make_async_copy(tokens.at[at, j], dst, own_sem.at[base + c]).start()
 
+    def turn_of(i):
+        at = i + me
+        for _ in range((pairs + nd - 2) // pairs):
+            at = jnp.where(at >= pairs, at - pairs, at)
+        return at
+
     def gather(i, carry):
-        at = lax.rem(i + me, pairs)
+        at = turn_of(i)
         ids = jnp.concatenate([ids_got[at, j : j + 1, 0:LP] for j in range(n_own)], axis=1)
         rows = pick_tokens(cols, blocks, stacked, ids)
         for j in range(n_own):
@@ -1525,7 +1581,7 @@
 
         @pl.when(i > 0)
         def _():
-            send_pair(lax.rem(i - 1 + me, pairs))
+            send_pair(turn_of(i - 1))
 
         for step, turn in enumerate(plan):
             if 0 < step and turn < pairs:
@@ -1546,16 +1602,9 @@
             lambda n: mine_q.at[pl.ds(0, n)], everyone, home,
         ),
     ]
-    home_moves = [
-        Flow(
-            lambda s, t: p0, lambda s, t: w0.at[s],
-            lambda n: w0.at[pl.ds(0, n)], everyone, home,
-        ),
-    ]
     q_base = net.start(q_moves)
-    home_base = net.start(home_moves)
     lax.fori_loop(0, pairs, gather, 0)
-    send_pair(lax.rem(pairs - 1 + me, pairs))
+    send_pair(turn_of(pairs - 1))
     for step, turn in enumerate(plan):
         if 0 < step and turn >= pairs:
             forward(step)
@@ -2048,32 +2097,8 @@
     )
     w_one = w_one.reshape(D, 4 * D + LP)
     w_zero = w_zero.reshape(D, 4 * D)
-    pid = ids_got[:, :n_own, :LP].reshape(n_slots, LP)[:n_valid]
-    qid = jnp.sum(ids_got[:, n_own, :tq], axis=0)
-    gains = small_got[:, :6, :cols].transpose(1, 0, 2).reshape(2, 3, D).astype(F32)
-    bias = small_got[:, 6:, : bias_terms.shape[1]].transpose(1, 0, 2).reshape(2, -1).astype(F32)
-
-    vocab = V + LP
-    total = -(-vocab // HASH) * HASH
     up_mine = expand_weight.astype(BF16).reshape(2, cols, nd, ff_cols).transpose(2, 0, 1, 3)
     up_mine = jnp.pad(up_mine, ((0, 0), (0, 0), (0, 0), (0, LANE - ff_cols)))
-    w_down = jnp.pad(shrink_weight.astype(BF16), ((0, 0), (0, LANE - ff_cols), (0, 0)))
-    cv = jnp.stack(
-        [v for e in range(2) for v in (
-            gains[e, 0], bias[e, O_EMB : O_EMB + D], bias[e, O_V : O_V + D])]
-        + [jnp.zeros((D,), F32)] * 2,
-        axis=1,
-    )
-    rv = jnp.stack(
-        [v for e in range(2) for v in (
-            bias[e, O_Q : O_Q + D], bias[e, O_O : O_O + D], bias[e, O_1 : O_1 + D],
-            bias[e, O_OUT : O_OUT + D], bias[e, O_2 : O_2 + D], gains[e, 1], gains[e, 2],
-            jnp.zeros((D,), F32))]
-    )
-    b_in = lax.dynamic_index_in_dim(
-        bias[:, O_IN : O_IN + FF].reshape(2, nd, ff_cols), me, 1, False
-    )
-    b_in = jnp.pad(b_in, ((0, 6), (0, LANE - ff_cols)))
     earlier = jnp.concatenate([jnp.full((1,), -1, jnp.int32), passage_query[:-1]])
     first_slot = ((passage_query >= 0) & (passage_query != earlier)).astype(jnp.int32)
     slots = jnp.pad(
@@ -2082,8 +2107,7 @@
     )
     shrink_g, loss, g_table, g_in, g_out, g_up, g_bin, g_small, norm = middle(
         n_valid, nq, nd, narrow, cols, query_home,
-        [mine, mine_q, w_one, w_zero, up_mine, w_down, cv, rv, b_in, slots,
-         pid.reshape(n_valid, 1, LP), qid.reshape(1, tq)],
+        [mine, mine_q, w_one, w_zero, up_mine, shrink_weight, small_got, slots, ids_got],
     )
     loss = loss[0, 0]
     grad_norm = norm[0, 0]

time: 245 us -> 231 us (0.943)
  local copies, waits for them, and re-layouts: 17 us -> 11.3 us
  Pallas kernels: 205 us -> 200 us
  other arithmetic: 20.4 us -> 17 us
    pallas_call x1, Pallas kernels: 130 us -> 127 us  [middle(): pl.pallas_call(functools.partial(middle_body, n_valid, nq, nd, narrow, co...]
where the time goes in v4:
time: 231 us
  Pallas kernels  200 us (87%)
  other arithmetic  17 us (7%)
  local copies, waits for them, and re-layouts  11.3 us (5%)
  between operations  2.41 us (1%)
    pallas_call x1, Pallas kernels, middle(): pl.pallas_call(functools.partial(middle_body, n_valid, nq, nd, narrow, co...  127 us
    pallas_call x1, Pallas kernels, first(): pl.pallas_call(functools.partial(first_body, n_valid, nq, nd, narrow, col...  73.2 us
    sub x7, other arithmetic, adam_update(): weight - rate * (first_hat / (jnp.sqrt(second_hat) + ADAM_EPS) + WEIGHT_D...  13.5 us

profile of v4, /device:TPU:0, one launch (start us, length us, event | category | flops | bytes accessed | tf_op | source)
XLA Modules:
  0.0 230.8 jit_solution(17033399022903349832)
XLA Ops:
  0.7 0.7 tile.11
  1.4 0.1 tile.12
  1.5 1.3 pad_add_fusion.ids_mine
  2.8 1.5 slice.52.pos_mine
  4.3 0.7 convert.12
  5.0 0.7 convert.13
  5.7 0.6 fusion.9.small_mine
  6.3 73.2 %first.1 = (s32[32,3,384]{2,1,0:T(4,128)}, bf16[32,8,384]{2,1,0:T(8,128)(2,1)}, bf16[32,24,768]{2,1,0:T(8,128)(2,1)}, bf16[32,24,256]{2,1,0:T(8,128)(2,1)}, bf16...) custom-call(s32[3,384]{1,0:T(4,128)} %pad_add_fusion.ids_mine, bf16[8,384]{1,0:T(8,128)(2,1)} %fusion.9.small_mine, ...), custom_call_target="tpu_custom_call" | custom-call | tf_op jit(solution)/shard_map/first/pallas_call | solution.py:1655
  79.4 0.0 copy-start.17
  79.5 0.0 copy-start.22
  79.5 0.4 reshape.142
  79.9 0.2 copy.72
  80.1 0.8 pad.25.up_mine
  80.9 0.1 fusion.15
  81.0 0.6 pad.26.slots
  81.6 0.0 copy-start.20
  81.6 0.0 copy-start.21
  81.6 0.0 copy-start.1
  81.6 0.0 copy-start.8
  81.6 126.9 %middle.1 = (f32[2,128,768]{2,1,0:T(8,128)}, f32[8,128]{1,0:T(8,128)}, f32[24,18432]{1,0:T(8,128)}, f32[2,24,2304]{2,1,0:T(8,128)}, f32[2,24,768]{2,1,0:T(8,128)...) custom-call(bf16[32,24,768]{2,1,0:T(8,128)(2,1)} %get-tuple-element.38.mine, ...), custom_call_target="tpu_custom_call" | custom-call | tf_op jit(solution)/shard_map/middle/pallas_call | solution.py:1309
  208.5 1.2 slice.43
  210.4 1.0 slice_bitcast_fusion.2
  211.4 0.8 slice_bitcast_fusion.3
  212.2 0.9 slice_bitcast_fusion.1
  213.2 0.1 reshape.147
  214.1 0.7 multiply_subtract_fusion.4
  214.8 0.1 constant_dynamic-slice_fusion
  214.9 0.0 copy-done.20
  214.9 0.6 add_subtract_fusion.1
  215.5 2.8 %multiply_subtract_fusion = (f32[2,96,768]{2,1,0:T(8,128)}, f32[2,96,768]{2,1,0:T(8,128)}, f32[2,96,768]{2,1,0:T(8,128)}) fusion(f32[2,96,768]{2,1,0:T(8,128)S(1)} %copy-done.1, f32[]{:T(128)} %bitcast.12, f32[]{:T(128)} %bitcast.11, f32[]{:T(128)S(6)} %div.104, f32[2,128,768]{2,1,0:T(8,128)} %get-tuple-element.50, f32[2,96,768]{2,1,0:T(8,128)S(1)} %copy-done.8, ...), kind=kLoop, calls=%fused_computation.13 | loop fusion | flops 2359296 | bytes 4128780 | tf_op jit(solution)/shard_map/sub | solution.py:66
  218.3 0.1 copy.60
  218.4 0.1 fusion.2
  218.5 0.0 copy-start.9
  218.5 0.0 copy-start.10
  218.5 0.4 copy.55
  218.9 0.0 copy-start.13
  219.0 0.0 copy-start.14
  219.0 1.1 mul.364
  220.1 0.0 copy-start.11
  220.1 0.0 copy-start.6
  220.1 0.0 copy-start.12
  220.1 0.0 copy-start.4
  220.1 1.5 multiply_subtract_fusion.1
  221.6 0.0 copy-start.3
  221.6 2.2 multiply_subtract_fusion.3
  223.9 2.5 %multiply_subtract_fusion.2 = (f32[2,24,2304]{2,1,0:T(8,128)}, f32[2,24,2304]{2,1,0:T(8,128)}, f32[2,24,2304]{2,1,0:T(8,128)}) fusion(f32[2,24,2304]{2,1,0:T(8,128)S(1)} %copy-done.6, f32[]{:T(128)} %bitcast.12, f32[]{:T(128)} %bitcast.11, f32[2,24,2304]{2,1,0:T(8,128)} %get-tuple-element.47, f32[]{:T(128)S(6)} %div.104, f32[2,24,2304]{2,1,0:T(8,128)S(1)} %copy-done.12, ...), kind=kLoop, calls=%fused_computation.19 | loop fusion | flops 1769472 | bytes 3096588 | tf_op jit(solution)/shard_map/sub | solution.py:66
  226.4 3.2 %add_subtract_fusion = (f32[18384,24]{0,1:T(8,128)}, f32[18384,24]{0,1:T(8,128)}, f32[18384,24]{0,1:T(8,128)}) fusion(f32[18384,24]{0,1:T(8,128)S(1)} %copy-done, f32[]{:T(128)} %bitcast.12, f32[]{:T(128)} %bitcast.11, f32[]{:T(128)S(6)} %div.104, f32[24,18432]{1,0:T(8,128)S(1)} %copy-done.5, f32[18384,24]{0,1:T(8,128)S(1)} %copy-done.3, ...), kind=kLoop, calls=%fused_computation.4 | loop fusion | flops 6618240 | bytes 12354060 | tf_op jit(solution)/shard_map/sub | solution.py:66
  229.6 1.2 slice.42
  (40 shorter events, 0.2 us)
Async XLA Ops:
  0.7 78.8 %copy-start.2 = (f32[2,24,3072]{2,1,0:T(8,128)S(1)}, f32[2,24,3072]{2,1,0:T(8,128)}, u32[]{:S(2)}) copy-start(f32[2,24,3072]{2,1,0:T(8,128)} %param.35) | copy-start | bytes 1769476
  79.4 1.4 copy-start.17
  79.5 1.5 copy-start.22
  81.6 132.5 %copy-start.15 = (f32[2,264]{1,0:T(2,128)S(1)}, f32[2,264]{1,0:T(2,128)}, u32[]{:S(2)}) copy-start(f32[2,264]{1,0:T(2,128)} %param.38) | copy-start | bytes 6340
  81.6 132.5 %copy-start.18 = (f32[2,264]{1,0:T(2,128)S(1)}, f32[2,264]{1,0:T(2,128)}, u32[]{:S(2)}) copy-start(f32[2,264]{1,0:T(2,128)} %param.52) | copy-start | bytes 6340
  81.6 132.5 %copy-start.19 = (f32[2,264]{1,0:T(2,128)S(1)}, f32[2,264]{1,0:T(2,128)}, u32[]{:S(2)}) copy-start(f32[2,264]{1,0:T(2,128)} %param.51) | copy-start | bytes 6340
  81.6 133.3 %copy-start.16 = (f32[2,3,24]{2,0,1:T(2,128)S(1)}, f32[2,3,24]{2,0,1:T(2,128)}, u32[]{:S(2)}) copy-start(f32[2,3,24]{2,0,1:T(2,128)} %param.37) | copy-start | bytes 1732
  81.6 133.3 %copy-start.20 = (f32[2,3,24]{2,0,1:T(2,128)S(1)}, f32[2,3,24]{2,0,1:T(2,128)}, u32[]{:S(2)}) copy-start(f32[2,3,24]{2,0,1:T(2,128)} %param.50) | copy-start | bytes 1732
  81.6 133.3 %copy-start.21 = (f32[2,3,24]{2,0,1:T(2,128)S(1)}, f32[2,3,24]{2,0,1:T(2,128)}, u32[]{:S(2)}) copy-start(f32[2,3,24]{2,0,1:T(2,128)} %param.49) | copy-start | bytes 1732
  81.6 133.9 %copy-start.1 = (f32[2,96,768]{2,1,0:T(8,128)S(1)}, f32[2,96,768]{2,1,0:T(8,128)}, u32[]{:S(2)}) copy-start(f32[2,96,768]{2,1,0:T(8,128)} %shrink.1) | copy-start | bytes 1769476
  81.6 133.9 %copy-start.8 = (f32[2,96,768]{2,1,0:T(8,128)S(1)}, f32[2,96,768]{2,1,0:T(8,128)}, u32[]{:S(2)}) copy-start(f32[2,96,768]{2,1,0:T(8,128)} %param.48) | copy-start | bytes 1769476
  215.5 2.8 %copy-start.7 = (f32[48,4096]{1,0:T(8,128)S(1)}, f32[48,4096]{1,0:T(8,128)}, u32[]{:S(2)}) copy-start(f32[48,4096]{1,0:T(8,128)} %get-tuple-element.49) | copy-start | bytes 2359300
  218.5 1.5 copy-start.9
  218.5 1.5 copy-start.10
  218.9 2.6 %copy-start.13 = (f32[2,24,768]{2,1,0:T(8,128)S(1)}, f32[2,24,768]{2,1,0:T(8,128)}, u32[]{:S(2)}) copy-start(f32[2,24,768]{2,1,0:T(8,128)} %param.44) | copy-start | bytes 442372
  219.0 2.6 %copy-start.14 = (f32[2,24,768]{2,1,0:T(8,128)S(1)}, f32[2,24,768]{2,1,0:T(8,128)}, u32[]{:S(2)}) copy-start(f32[2,24,768]{2,1,0:T(8,128)} %param.43) | copy-start | bytes 442372
  220.1 1.5 copy-start.11
  220.1 3.8 %copy-start.6 = (f32[2,24,2304]{2,1,0:T(8,128)S(1)}, f32[2,24,2304]{2,1,0:T(8,128)}, u32[]{:S(2)}) copy-start(f32[2,24,2304]{2,1,0:T(8,128)} %win.1) | copy-start | bytes 1327108
  220.1 3.8 %copy-start.12 = (f32[2,24,2304]{2,1,0:T(8,128)S(1)}, f32[2,24,2304]{2,1,0:T(8,128)}, u32[]{:S(2)}) copy-start(f32[2,24,2304]{2,1,0:T(8,128)} %param.42) | copy-start | bytes 1327108
  220.1 6.3 %copy-start.4 = (f32[18384,24]{0,1:T(8,128)S(1)}, f32[18384,24]{0,1:T(8,128)}, u32[]{:S(2)}) copy-start(f32[18384,24]{0,1:T(8,128)} %param.39) | copy-start | bytes 5294596
  220.1 6.3 %copy-start.5 = (f32[24,18432]{1,0:T(8,128)S(1)}, f32[24,18432]{1,0:T(8,128)}, u32[]{:S(2)}) copy-start(f32[24,18432]{1,0:T(8,128)} %get-tuple-element.46) | copy-start | bytes 5308420
  221.6 4.8 %copy-start.3 = (f32[18384,24]{0,1:T(8,128)S(1)}, f32[18384,24]{0,1:T(8,128)}, u32[]{:S(2)}) copy-start(f32[18384,24]{0,1:T(8,128)} %param.40) | copy-start | bytes 5294596
  223.9 2.6 %copy-start = (f32[18384,24]{0,1:T(8,128)S(1)}, f32[18384,24]{0,1:T(8,128)}, u32[]{:S(2)}) copy-start(f32[18384,24]{0,1:T(8,128)} %param.32) | copy-start | bytes 5294596
